TPU v7x, 32 devices: a whole 2x2x4 slice. The times are simulated.
32 devices in a mesh: gx: 4 (over y, core), gy: 8 (over z, x).
Axes of the slice: x: 2, y: 2, z: 4, core: 2. Of those that a mesh axis runs over, the one named last changes fastest.
Arguments:
- weighted_jacobian_strips: float32 [4096, 3, 768], P(('gx', 'gy')), may hold values from -0.3125 to 0.3125
- leading_pose_index: int32 [4096, 1], P(('gx', 'gy')), may hold values from 0 to 31; in each aligned block of 128 rows (0 to 127, 128 to 255, ...) at most 6 rows name the same one
- levenberg_shift: float32 [32, 768], P(('gx', 'gy')), may hold values from 0.05 to 0.5
- removal_flags: int32 [32], replicated, may hold values from 0 to 1, as said below
Outputs:
- schur: float32 [32, 3, 768, 768], P(('gx', 'gy'))
- coupling: float32 [32, 4, 768, 768], P(('gx', 'gy'))
Inputs may be any that keep to these rules, and one draw needn't show every extreme that they name: `leading_pose_index`: within the 128 columns of one device no block is the base of more than 6 columns, and some device reaches 6. `removal_flags`: eliminated blocks lie 3 or more blocks apart around the cycle of 32 blocks.
All inputs are finite; a program needn't handle non-finite values.
Results may differ from a plain program's by a relative error of at most 0.0003.
Values sent between devices are 32-bit elements; how exact they have to be, the bound alone decides.
No kernel may reach another device: no remote copies, remote signals or barrier semaphores. Data moves between devices by JAX's collectives and lax.ppermute only.
A program may use at most 192 MiB of HBM per device.

v0:
```python
import functools
import math

import jax
import jax.numpy as jnp
from jax import lax
from jax.experimental import pallas as pl
from jax.experimental.pallas import tpu as pltpu
from jax.sharding import PartitionSpec as P


AXES = ("gx", "gy")
TILE = 128
GROUP = 8
WIDE = 256
PARTS = 3
NT = (((1,), (1,)), ((), ()))
TN = (((0,), (0,)), ((), ()))
NN = (((1,), (0,)), ((), ()))
VMEM_SPEC = pl.BlockSpec(memory_space=pltpu.VMEM)
SMEM_SPEC = pl.BlockSpec(memory_space=pltpu.SMEM)
ANY_SPEC = pl.BlockSpec(memory_space=pl.ANY)
PIECES = ((0, 2), (1, 3), (0, 1), (2, 3))


def passed_along(value, steps):
    count = lax.axis_size(AXES)
    pairs = [(source, (source + steps) % count) for source in range(count)]
    return lax.ppermute(value, AXES, pairs)


def product(left, right, dims, precision=lax.Precision.HIGHEST):
    return lax.dot_general(
        left, right, dims, precision=precision, preferred_element_type=jnp.float32
    )


def bucket_kernel(count, capacity, index_ref, strips_ref, out_ref, rows_ref):
    surfels = strips_ref.shape[1]
    width = strips_ref.shape[2]
    lane_tiles = width // WIDE
    index = index_ref[...]
    base = lax.broadcasted_iota(jnp.int32, (count, surfels), 0)
    hot = (base == index).astype(jnp.float32)
    first = lax.broadcasted_iota(jnp.int32, (surfels, surfels), 0)
    second = lax.broadcasted_iota(jnp.int32, (surfels, surfels), 1)
    ahead = (first < second).astype(jnp.float32)
    earlier = product(hot, ahead, NN)
    within = jnp.sum(earlier * hot, axis=0, keepdims=True).astype(jnp.int32)
    period = GROUP // math.gcd(capacity, GROUP)
    for piece in range(3):
        moved = index + piece
        moved = jnp.where(moved >= count, moved - count, moved)
        slot = moved * capacity + within
        row = lax.broadcasted_iota(jnp.int32, (count * capacity, surfels), 0)
        pick = (row == slot).astype(jnp.bfloat16)
        values = strips_ref[piece]
        high = values.astype(jnp.bfloat16)
        rest = values - high.astype(jnp.float32)
        middle = rest.astype(jnp.bfloat16)
        low = (rest - middle.astype(jnp.float32)).astype(jnp.bfloat16)
        rows_ref[...] = product(
            jnp.concatenate([pick, pick, pick], axis=1),
            jnp.concatenate([high, middle, low], axis=0),
            NN,
            lax.Precision.DEFAULT,
        )

        def spread(turn, carry, piece=piece):
            start = pl.multiple_of(turn * (period * capacity), GROUP)
            for tile in range(lane_tiles):
                block = rows_ref[pl.ds(start, period * capacity), WIDE * tile : WIDE * (tile + 1)]
                for member in range(period):
                    begin = (piece * lane_tiles + tile) * capacity
                    out_ref[turn * period + member, begin : begin + capacity, :] = block[
                        member * capacity : (member + 1) * capacity
                    ]
            return carry

        lax.fori_loop(0, count // period, spread, 0)


def bucketed(index_row, strips, count, capacity):
    width = strips.shape[2]
    return pl.pallas_call(
        functools.partial(bucket_kernel, count, capacity),
        out_shape=jax.ShapeDtypeStruct(
            (count, 3 * (width // WIDE) * capacity, WIDE), jnp.float32
        ),
        in_specs=[VMEM_SPEC, VMEM_SPEC],
        out_specs=VMEM_SPEC,
        scratch_shapes=[pltpu.VMEM((count * capacity, width), jnp.float32)],
        name="bucket",
    )(index_row, strips)


def regroup_kernel(capacity, in_ref, out_ref, two_ref, one_ref):
    count = in_ref.shape[0]
    width = out_ref.shape[1]
    lane_tiles = width // WIDE
    period = GROUP // math.gcd(capacity, GROUP)

    def gather(turn, carry):
        for piece in range(3):
            for tile in range(lane_tiles):
                begin = (piece * lane_tiles + tile) * capacity
                block = jnp.concatenate(
                    [
                        in_ref[turn * period + member, begin : begin + capacity, :]
                        for member in range(period)
                    ],
                    axis=0,
                )
                start = pl.multiple_of(
                    piece * count * capacity + turn * (period * capacity), GROUP
                )
                out_ref[
                    pl.ds(start, period * capacity), WIDE * tile : WIDE * (tile + 1)
                ] = block
        return carry

    lax.fori_loop(0, count // period, gather, 0)
    side = count * capacity
    two_ref[...] = out_ref[: 2 * side, :]
    one_ref[...] = out_ref[2 * side :, :]


def regrouped(chunks, capacity, width):
    side = chunks.shape[0] * capacity
    return pl.pallas_call(
        functools.partial(regroup_kernel, capacity),
        out_shape=tuple(
            jax.ShapeDtypeStruct((parts * side, width), jnp.float32) for parts in (3, 2, 1)
        ),
        in_specs=[VMEM_SPEC],
        out_specs=(VMEM_SPEC,) * 3,
        compiler_params=pltpu.CompilerParams(vmem_limit_bytes=16 << 20),
        name="regroup",
    )(chunks)


def full(value):
    return jnp.broadcast_to(value, (GROUP, TILE))


def half_factor(pair_ref, done_ref, start):
    groups = pair_ref.shape[0] // GROUP
    sub = lax.broadcasted_iota(jnp.int32, (GROUP, TILE), 0)
    rows = [pair_ref[GROUP * g : GROUP * (g + 1), :] for g in range(groups)]
    eight = range(GROUP)
    for p in range(groups):
        strip = rows[p]
        cols = [full(strip[:, GROUP * p + k : GROUP * p + k + 1]) for k in eight]
        m = [[full(cols[k][i : i + 1, :]) if k <= i else None for k in eight] for i in eight]
        r = [None] * GROUP
        u = [full(strip[j : j + 1, :]) for j in eight]
        for j in eight:
            r[j] = lax.rsqrt(m[j][j])
            for i in range(j + 1, GROUP):
                m[i][j] = m[i][j] * r[j]
            for k in range(j + 1, GROUP):
                for i in range(k, GROUP):
                    m[i][k] = m[i][k] - m[i][j] * m[k][j]
            u[j] = u[j] * r[j]
            for i in range(j + 1, GROUP):
                u[i] = u[i] - m[i][j] * u[j]
        joined = u[0]
        for j in range(1, GROUP):
            joined = jnp.where(sub == j, u[j], joined)
        done_ref[pl.ds(start + GROUP * p, GROUP), :] = joined
        for g in range(p + 1, groups):
            side = [full(rows[g][:, GROUP * p + k : GROUP * p + k + 1]) for k in eight]
            x = rows[g]
            for j in eight:
                side[j] = side[j] * r[j]
                for i in range(j + 1, GROUP):
                    side[i] = side[i] - m[i][j] * side[j]
                x = x - side[j] * u[j]
            rows[g] = x


def tile_factor(tile, pair_ref, done_ref, cross_ref, corner_ref):
    half = TILE // 2
    row = lax.broadcasted_iota(jnp.int32, (half, half), 0)
    col = lax.broadcasted_iota(jnp.int32, (half, half), 1)
    unit = jnp.where(row == col, 1.0, 0.0).astype(jnp.float32)
    zero = jnp.zeros((half, half), jnp.float32)
    pair_ref[...] = jnp.concatenate([tile[:half, :half], unit], axis=1)
    cross_ref[...] = tile[:half, half:]
    corner_ref[...] = tile[half:, half:]

    def turn(number, carry):
        half_factor(pair_ref, done_ref, pl.multiple_of(number * half, half))

        @pl.when(number == 0)
        def _():
            cross = near_product(done_ref[:half, half:], cross_ref[...], NN)
            cross_ref[...] = cross
            both = halves(cross)
            rest = corner_ref[...] - product_of_halves(both, both, TN)
            pair_ref[...] = jnp.concatenate([rest, unit], axis=1)

        return carry

    lax.fori_loop(0, 2, turn, 0)
    first, second = done_ref[:half, half:], done_ref[half:, half:]
    middle = near_product(cross_ref[...], first, TN)
    upper = jnp.concatenate(
        [
            jnp.concatenate([done_ref[:half, :half], cross_ref[...]], axis=1),
            jnp.concatenate([zero, done_ref[half:, :half]], axis=1),
        ],
        axis=0,
    )
    inverse = jnp.concatenate(
        [
            jnp.concatenate([first, zero], axis=1),
            jnp.concatenate([-near_product(second, middle, NN), second], axis=1),
        ],
        axis=0,
    )
    return upper, inverse


def halves(value):
    high = value.astype(jnp.bfloat16)
    return high, (value - high.astype(jnp.float32)).astype(jnp.bfloat16)


def product_of_halves(left, right, dims):
    total = product(left[0], right[0], dims, lax.Precision.DEFAULT)
    total = total + product(left[0], right[1], dims, lax.Precision.DEFAULT)
    return total + product(left[1], right[0], dims, lax.Precision.DEFAULT)


def lanes_at(number):
    return pl.ds(pl.multiple_of(number * WIDE, WIDE), WIDE)


def tall_product(left_refs, rows, depth, right_at, put, width):
    left = tuple(ref[:rows, :depth] for ref in left_refs)

    def block(number, carry):
        put(lanes_at(number), product_of_halves(left, halves(right_at(lanes_at(number))), NN))
        return carry

    lax.fori_loop(0, width // WIDE, block, 0)


def keep_halves(left_refs, value):
    rows, depth = value.shape
    high, low = halves(value)
    left_refs[0][:rows, :depth] = high
    left_refs[1][:rows, :depth] = low


def piece_shapes(side, lanes):
    return tuple(
        jax.ShapeDtypeStruct(((stop - start) * side, lanes), jnp.float32) for start, stop in PIECES
    )


def part_kernel(side, bounds, number, *refs):
    first, last = bounds[number], bounds[number + 1]
    final = number == len(bounds) - 2
    x_ref, start_ref = refs[:2]
    before = refs[2 : 2 + 2 * number]
    refs = refs[2 + 2 * number :]
    low_ref, outs = refs[0], refs[1:5]
    gram_refs, refs = (refs[5:7], refs[7:]) if final else ((), refs[5:])
    small_refs, refs = refs[:4], refs[4:]
    low_high_ref, low_less_ref, y_high_ref, y_less_ref = refs[:4]
    depth, width = x_ref.shape
    begin, end = first * TILE, last * TILE
    reach = end - TILE
    row = lax.broadcasted_iota(jnp.int32, (TILE, TILE), 0)
    col = lax.broadcasted_iota(jnp.int32, (TILE, TILE), 1)

    if number == 0:
        turned = refs[4:6]
        keep_halves(turned, x_ref[...].T)

        def gram(lanes, value):
            low_ref[:, lanes] = value

        tall_product(turned, width, depth, lambda lanes: x_ref[:, lanes], gram, width)
        for i in range(width // TILE):
            rows = slice(i * TILE, (i + 1) * TILE)
            low_ref[rows, rows] = low_ref[rows, rows] + jnp.where(
                row == col, jnp.broadcast_to(start_ref[:, rows], (TILE, TILE)), 0.0
            )
    else:
        low_ref[...] = start_ref[...]
        high, less = halves(start_ref[:, :begin])
        low_high_ref[:, :begin] = high
        low_less_ref[:, :begin] = less
        for k in range(number):
            lanes = slice(bounds[k] * TILE, bounds[k + 1] * TILE)
            for ref, rows in ((before[2 * k], slice(0, 2 * side)), (before[2 * k + 1], slice(2 * side, 3 * side))):
                high, less = halves(ref[...])
                y_high_ref[rows, lanes] = high
                y_less_ref[rows, lanes] = less
    for ref in (low_high_ref, low_less_ref):
        ref[:, begin:] = jnp.zeros((width, end - begin), jnp.bfloat16)
    for ref in (y_high_ref, y_less_ref):
        ref[:, begin:] = jnp.zeros((depth, end - begin), jnp.bfloat16)

    def step(j, carry):
        start = pl.multiple_of(j * TILE, TILE)
        cols = pl.ds(start, TILE)
        local = pl.ds(pl.multiple_of((j - first) * TILE, TILE), TILE)

        def reduced(value, high_ref, less_ref, rows):
            if reach == 0:
                return value
            return value - product_of_halves(
                (high_ref[rows, :reach], less_ref[rows, :reach]),
                (low_high_ref[cols, :reach], low_less_ref[cols, :reach]),
                NT,
            )

        tile = reduced(low_ref[cols, cols], low_high_ref, low_less_ref, cols)
        upper, inverse = tile_factor(tile, *small_refs)
        inverse = halves(inverse)
        for i in range(depth // side):
            rows = slice(i * side, (i + 1) * side)
            value = reduced(x_ref[rows, cols], y_high_ref, y_less_ref, rows)
            value = product_of_halves(halves(value), inverse, NT)
            for out_ref, (head, tail) in zip(outs, PIECES):
                if head <= i < tail:
                    out_ref[(i - head) * side : (i - head + 1) * side, local] = value
            high, less = halves(value)
            y_high_ref[rows, cols] = high
            y_less_ref[rows, cols] = less
        for i in range(first * TILE // WIDE, width // WIDE):
            rows = slice(i * WIDE, (i + 1) * WIDE)
            value = reduced(low_ref[rows, cols], low_high_ref, low_less_ref, rows)
            value = product_of_halves(halves(value), inverse, NT)
            place = lax.broadcasted_iota(jnp.int32, (WIDE, TILE), 0) + i * WIDE
            value = jnp.where(place >= start + TILE, value, 0.0)
            low_ref[rows, cols] = value
            high, less = halves(value)
            low_high_ref[rows, cols] = high
            low_less_ref[rows, cols] = less
        low_ref[cols, cols] = jnp.where(col <= row, upper.T, 0.0)
        return carry

    lax.fori_loop(first, last, step, 0)
    if number > 0:
        for i in range(first * TILE // WIDE):
            rows = slice(i * WIDE, (i + 1) * WIDE)
            low_ref[rows, begin:end] = jnp.zeros((WIDE, end - begin), jnp.float32)
    if final:
        for gram_ref, left, right in (
            (gram_refs[0], slice(2 * side, 3 * side), slice(0, 2 * side)),
            (gram_refs[1], slice(side, 2 * side), slice(0, side)),
        ):
            gram_ref[...] = product_of_halves(
                (y_high_ref[left, :], y_less_ref[left, :]),
                (y_high_ref[right, :], y_less_ref[right, :]),
                NT,
            )


def factored_part(x, start, before, side, bounds, number):
    depth, width = x.shape
    first, last = bounds[number], bounds[number + 1]
    final = number == len(bounds) - 2
    end = last * TILE
    shapes = [jax.ShapeDtypeStruct((width, width), jnp.float32)]
    shapes += piece_shapes(side, (last - first) * TILE)
    if final:
        shapes += [
            jax.ShapeDtypeStruct((side, 2 * side), jnp.float32),
            jax.ShapeDtypeStruct((side, side), jnp.float32),
        ]
    half = TILE // 2
    scratch = [pltpu.VMEM((half, TILE), jnp.float32), pltpu.VMEM((TILE, TILE), jnp.float32)]
    scratch += [pltpu.VMEM((half, half), jnp.float32)] * 2
    scratch += [pltpu.VMEM((width, end), jnp.bfloat16)] * 2
    scratch += [pltpu.VMEM((depth, end), jnp.bfloat16)] * 2
    if number == 0:
        scratch += [pltpu.VMEM((width, depth), jnp.bfloat16)] * 2
    return pl.pallas_call(
        functools.partial(part_kernel, side, bounds, number),
        out_shape=tuple(shapes),
        in_specs=[VMEM_SPEC] * (2 + len(before)),
        out_specs=(VMEM_SPEC,) * len(shapes),
        scratch_shapes=scratch,
        compiler_params=pltpu.CompilerParams(vmem_limit_bytes=24 << 20),
        cost_estimate=pl.CostEstimate(
            flops=20_000_000_000, bytes_accessed=3 * depth * width * 4, transcendentals=0
        ),
        name="factor_part",
    )(x, start, *before)


def near_product(left, right, dims):
    return product_of_halves(halves(left), halves(right), dims)


def put_coupling(side, start, y_refs, x_ref, buffer_ref, left_refs, out_ref, sems):
    rows = buffer_ref.shape[1]
    width = x_ref.shape[1]
    copies = []
    for place, (number, begin, end) in enumerate(((3, 0, 1), (1, 0, 2), (0, 1, 3), (2, 2, 3))):
        keep_halves(left_refs, y_refs[number][...].T)

        def put(lanes, value, place=place):
            buffer_ref[place, :, lanes] = value

        tall_product(
            left_refs,
            rows,
            (end - begin) * side,
            lambda lanes, begin=begin, end=end: x_ref[begin * side : end * side, lanes],
            put,
            width,
        )
        copy = pltpu.make_async_copy(
            buffer_ref.at[place], out_ref.at[place, pl.ds(start, rows), :], sems.at[place]
        )
        copy.start()
        copies.append(copy)
    return copies


def early_kernel(side, starts, x_ref, *refs):
    parts = len(starts)
    y_refs, refs = refs[: 4 * parts], refs[4 * parts :]
    out_ref, refs = refs[0], refs[1:]
    buffers, (high_ref, less_ref, sems) = refs[:parts], refs[parts:]
    copies = []
    for number, start in enumerate(starts):
        copies += put_coupling(
            side,
            start,
            y_refs[4 * number : 4 * number + 4],
            x_ref,
            buffers[number],
            (high_ref, less_ref),
            out_ref,
            sems.at[number],
        )
    for copy in copies:
        copy.wait()


def early(x, parts, starts, side):
    width = x.shape[1]
    heights = [part[0].shape[1] for part in parts]
    most = max(heights)
    return pl.pallas_call(
        functools.partial(early_kernel, side, starts),
        out_shape=jax.ShapeDtypeStruct((4, width, width), jnp.float32),
        in_specs=[VMEM_SPEC] * (1 + 4 * len(parts)),
        out_specs=ANY_SPEC,
        scratch_shapes=[pltpu.VMEM((4, height, width), jnp.float32) for height in heights]
        + [
            pltpu.VMEM((most, 2 * side), jnp.bfloat16),
            pltpu.VMEM((most, 2 * side), jnp.bfloat16),
            pltpu.SemaphoreType.DMA((len(parts), 4)),
        ],
        compiler_params=pltpu.CompilerParams(vmem_limit_bytes=24 << 20),
        cost_estimate=pl.CostEstimate(
            flops=8_000_000_000, bytes_accessed=4 * width * width * 4, transcendentals=0
        ),
        name="early",
    )(x, *[piece for part in parts for piece in part])


def late_kernel(side, starts, flags_ref, *refs):
    (
        x_ref,
        shift_ref,
        direct_ref,
        onward_ref,
        second_ref,
        extra_ref,
        low_ref,
        gram_one_ref,
        gram_two_ref,
    ) = refs[:9]
    parts = len(starts)
    refs = refs[9:]
    mine, refs = refs[:parts], refs[parts:]
    pieces, refs = [refs[4 * k : 4 * k + 4] for k in range(parts)], refs[4 * parts :]
    lasts = pieces[-1]
    partial_ref, schur_ref, coupling_ref = refs[:3]
    buffer_ref, tile_ref, rest_ref, near_ref, far_ref, high_ref, less_ref, sems, outs = refs[3:]
    left_refs = (high_ref, less_ref)
    width = x_ref.shape[1]
    cut = starts[-1]
    copies = put_coupling(side, cut, lasts, x_ref, buffer_ref, left_refs, coupling_ref, sems)
    own, above, second_above, under, second_under = [flags_ref[k] > 0 for k in range(5)]
    one, two, three = slice(0, side), slice(side, 2 * side), slice(2 * side, 3 * side)
    pair, tail = slice(0, 2 * side), slice(side, 3 * side)
    rest_ref[...] = x_ref[...]
    near_ref[three, :] = jnp.zeros((side, width), jnp.float32)
    far_ref[two, :] = jnp.zeros((side, width), jnp.float32)

    @pl.when(own)
    def _():
        for start, ref in zip(starts, mine):
            lanes = slice(start, start + ref.shape[1])
            near_ref[pair, lanes] = ref[...]
            far_ref[one, lanes] = ref[side:, :]

    @pl.when(jnp.logical_not(own))
    def _():
        near_ref[pair, :] = x_ref[tail, :]
        far_ref[one, :] = x_ref[three, :]

    def weighed(number, rows):
        gram = 0.0
        for part in pieces:
            both = halves(part[number][...])
            gram = gram + product_of_halves(both, both, NT)
        return near_product(gram, x_ref[rows, :], NN)

    @pl.when(second_above)
    def _():
        rest_ref[one, :] = rest_ref[one, :] - weighed(3, one)

    @pl.when(above)
    def _():
        term = weighed(1, pair)
        rest_ref[pair, :] = rest_ref[pair, :] - term
        near_ref[one, :] = near_ref[one, :] - term[side:]

    @pl.when(under)
    def _():
        term = weighed(0, tail)
        rest_ref[tail, :] = rest_ref[tail, :] - term
        far_ref[one, :] = far_ref[one, :] - term[side:]
        far_ref[two, :] = -near_product(gram_one_ref[...], x_ref[tail, :], NN)

    @pl.when(second_under)
    def _():
        term = weighed(2, three)
        rest_ref[three, :] = rest_ref[three, :] - term
        near_ref[two, :] = near_ref[two, :] - term
        near_ref[three, :] = -near_product(gram_two_ref[...], x_ref[three, :], NN)

    def put(place):
        copy = pltpu.make_async_copy(tile_ref.at[place], schur_ref.at[place], outs.at[place])
        copy.start()
        return copy

    def fill(place, left, right_ref):
        keep_halves(left_refs, left.T)

        def put(lanes, value):
            tile_ref[place, :, lanes] = value

        tall_product(
            left_refs, width, left.shape[0], lambda lanes: right_ref[:, lanes], put, width
        )

    def from_coupling(place, member):
        copy = pltpu.make_async_copy(
            partial_ref.at[member, pl.ds(0, cut), :],
            tile_ref.at[place, pl.ds(0, cut), :],
            outs.at[place],
        )
        copy.start()
        tile_ref[place, cut:, :] = buffer_ref[member]
        copy.wait()

    @pl.when(own)
    def _():
        tile_ref[2] = low_ref[...]

    @pl.when(jnp.logical_not(own))
    def _():
        fill(2, x_ref[...], rest_ref)
        for i in range(width // TILE):
            rows = slice(i * TILE, (i + 1) * TILE)
            row = lax.broadcasted_iota(jnp.int32, (TILE, TILE), 0)
            col = lax.broadcasted_iota(jnp.int32, (TILE, TILE), 1)
            tile_ref[2, rows, rows] = tile_ref[2, rows, rows] + jnp.where(
                row == col, jnp.broadcast_to(shift_ref[:, rows], (TILE, TILE)), 0.0
            )

    copies.append(put(2))

    @pl.when(under)
    def _():
        from_coupling(1, 2)

    @pl.when(jnp.logical_not(under))
    def _():
        below = direct_ref[...] + onward_ref[...]
        fill(1, jnp.concatenate([below, extra_ref[...]], axis=0), near_ref)

    copies.append(put(1))

    @pl.when(second_under)
    def _():
        from_coupling(0, 3)

    @pl.when(jnp.logical_not(second_under))
    def _():
        fill(0, second_ref[...], far_ref)

    copies.append(put(0))
    for copy in copies:
        copy.wait()


def late(flags, x, shift, received, low, grams, mine, parts, partial, starts, side):
    depth, width = x.shape
    rest = parts[-1][0].shape[1]
    inputs = [x, shift, *received, low, *grams, *mine] + [piece for part in parts for piece in part]
    return pl.pallas_call(
        functools.partial(late_kernel, side, starts),
        out_shape=(
            jax.ShapeDtypeStruct((3, width, width), jnp.float32),
            jax.ShapeDtypeStruct((4, width, width), jnp.float32),
        ),
        in_specs=[SMEM_SPEC] + [VMEM_SPEC] * len(inputs) + [ANY_SPEC],
        out_specs=(ANY_SPEC, ANY_SPEC),
        input_output_aliases={1 + len(inputs): 1},
        scratch_shapes=[
            pltpu.VMEM((4, rest, width), jnp.float32),
            pltpu.VMEM((3, width, width), jnp.float32),
            pltpu.VMEM((depth, width), jnp.float32),
            pltpu.VMEM((depth, width), jnp.float32),
            pltpu.VMEM((2 * side, width), jnp.float32),
            pltpu.VMEM((width, depth), jnp.bfloat16),
            pltpu.VMEM((width, depth), jnp.bfloat16),
            pltpu.SemaphoreType.DMA((4,)),
            pltpu.SemaphoreType.DMA((3,)),
        ],
        compiler_params=pltpu.CompilerParams(vmem_limit_bytes=40 << 20),
        cost_estimate=pl.CostEstimate(
            flops=12_000_000_000, bytes_accessed=7 * width * width * 4, transcendentals=0
        ),
        name="late",
    )(flags, *inputs, partial)


def local(weighted_jacobian_strips, leading_pose_index, levenberg_shift, removal_flags):
    count = lax.axis_size(AXES)
    own = lax.axis_index(AXES)
    surfels, _, width = weighted_jacobian_strips.shape
    capacity = max(2, (3 * surfels + 2 * count - 1) // (2 * count))
    side = count * capacity
    tiles = width // TILE
    bounds = tuple(tiles * k // PARTS for k in range(PARTS + 1))
    starts = tuple(bound * TILE for bound in bounds[:-1])
    flags = removal_flags[(own + jnp.array((0, 1, 2, -1, -2), jnp.int32)) % count]

    chunks = bucketed(
        leading_pose_index.reshape(1, surfels),
        weighted_jacobian_strips.transpose(1, 0, 2),
        count,
        capacity,
    )
    chunks = lax.all_to_all(chunks, AXES, split_axis=0, concat_axis=0, tiled=True)
    x, two, last = regrouped(chunks, capacity, width)

    def sent_parts(parts):
        return [passed_along(part, steps) for part, steps in zip(parts, (1, -1, 2, -2))]

    direct = lax.ppermute(two, AXES, [(k, k + 1) for k in range(0, count, 2)])
    second = passed_along(two, 2)

    def solved(number, start, known):
        before = [part[k] for part in known for k in (0, 3)]
        return factored_part(x, start, before, side, bounds, number)

    low, *part = solved(0, levenberg_shift, ())
    known = [part]
    parts = [sent_parts(part)]
    for number in range(1, PARTS - 1):
        low, *part = solved(number, low, known)
        known.append(part)
        parts.append(sent_parts(part))
    onward = lax.ppermute(second, AXES, [(k + 1, k) for k in range(0, count, 2)])
    extra = passed_along(last, 1)
    low, *part, gram_one, gram_two = solved(PARTS - 1, low, known)
    known.append(part)
    parts.append(sent_parts(part))
    grams = (passed_along(gram_one, 1), passed_along(gram_two, 2))
    partial = early(x, parts[:-1], starts[:-1], side)
    schur, coupling = late(
        flags,
        x,
        levenberg_shift,
        (direct, onward, second, extra),
        low,
        grams,
        [part[1] for part in known],
        parts,
        partial,
        starts,
        side,
    )
    return schur[None], coupling[None]


def solution(mesh):
    in_specs = (P(AXES, None, None), P(AXES, None), P(AXES, None), P())
    out_specs = (P(AXES, None, None, None), P(AXES, None, None, None))

    return jax.shard_map(local, mesh=mesh, in_specs=in_specs, out_specs=out_specs, check_vma=False)
```

profile of v0, /device:TPU:0, one launch (start us, length us, event | category | flops | bytes accessed | tf_op | source)
XLA Modules:
  0.0 265.7 jit_solution(13409712314257847417)
XLA Ops:
  0.6 4.1 %bucket.1 = f32[32,54,256]{2,1,0:T(8,128)} custom-call(s32[1,128]{1,0:T(1,128)} %bitcast.5, f32[3,128,768]{2,1,0:T(8,128)} %bitcast.4), custom_call_target="tpu_custom_call" | custom-call | tf_op jit(solution)/shard_map/bucket/pallas_call | solution.py:85
  4.8 51.7 %all_to_all.5.in_ref = f32[32,54,256]{2,1,0:T(8,128)S(1)} all-to-all(f32[32,54,256]{2,1,0:T(8,128)} %bucket.1), channel_id=1, replica_groups=mesh['gx'=4,'gy'=8] {'gx','gy'}, dimensions={0} | all-to-all | bytes 3538944 | tf_op jit(solution)/shard_map/all_to_all | solution.py:660
  56.4 1.5 regroup.1
  58.5 18.2 %factor_part.3 = (f32[768,768]{1,0:T(8,128)S(1)}, f32[384,256]{1,0:T(8,128)}, f32[384,256]{1,0:T(8,128)S(1)}, f32[192,256]{1,0:T(8,128)S(1)}, f32[192,256]{1,0:T(8,128)S(1)}) custom-call(f32[576,768]{1,0:T(8,128)S(1)} %get-tuple-element.24.refs_0_.x_ref, f32[1,768]{1,0:T(1,128)S(1)} %copy-done.29), custom_call_target="tpu_custom_call" | custom-call | flops 20000000000 | bytes 5308416 | tf_op jit(solution)/shard_map/factor_part/pallas_call | solution.py:384
  76.7 16.3 %factor_part.4 = (f32[768,768]{1,0:T(8,128)S(1)}, f32[384,256]{1,0:T(8,128)}, f32[384,256]{1,0:T(8,128)}, f32[192,256]{1,0:T(8,128)S(1)}, f32[192,256]{1,0:T(8,128)S(1)}) custom-call(f32[576,768]{1,0:T(8,128)S(1)} %get-tuple-element.24.refs_0_.x_ref, f32[768,768]{1,0:T(8,128)S(1)} %get-tuple-element.27.refs_1_, f32[384,256]{1,0:T(8,128)} %get-tuple-element.28.refs_2_, ...), custom_call_target="tpu_custom_call" | custom-call | flops 20000000000 | bytes 5308416 | tf_op jit(solution)/shard_map/factor_part/pallas_call | solution.py:384
  93.0 16.3 %factor_part.5 = (f32[768,768]{1,0:T(8,128)S(1)}, f32[384,256]{1,0:T(8,128)S(1)}, f32[384,256]{1,0:T(8,128)S(1)}, f32[192,256]{1,0:T(8,128)S(1)}, f32[192,256]{1...) custom-call(f32[576,768]{1,0:T(8,128)S(1)} %get-tuple-element.24.refs_0_.x_ref, ...), custom_call_target="tpu_custom_call" | custom-call | flops 20000000000 | bytes 5308416 | tf_op jit(solution)/shard_map/factor_part/pallas_call | solution.py:384
  110.0 0.7 copy-done.5
  110.7 1.4 copy-done.30
  112.1 1.5 collective-permute-start.5
  113.6 3.0 %collective-permute-start.9 = (f32[192,256]{1,0:T(8,128)S(1)}, f32[192,256]{1,0:T(8,128)S(1)}, u32[]{:S(2)}, u32[]{:S(2)}) collective-permute-start(f32[192,256]{1,0:T(8,128)S(1)} %get-tuple-element.29.refs_3_), channel_id=1, source_target_pairs={{0,30},{1,31},{2,0},{3,1},{4,2},{5,3},{6,4},{7,5},{8,6},{9,7},{10,... | collective-permute-start | bytes 589832 | tf_op jit(solution)/shard_map/ppermute | solution.py:29
  116.6 5.4 %collective-permute-done.5.refs_8_ = f32[192,192]{1,0:T(8,128)S(1)} collective-permute-done((f32[192,192]{1,0:T(8,128)S(1)}, f32[192,192]{1,0:T(8,128)S(1)}, u32[]{:S(2)}, u32[]{:S(2)}) %collective-permute-start.5) | collective-permute-done | bytes 147488 | tf_op jit(solution)/shard_map/ppermute | solution.py:29
  122.7 5.0 %collective-permute-start.13 = (f32[192,256]{1,0:T(8,128)S(1)}, f32[192,256]{1,0:T(8,128)S(1)}, u32[]{:S(2)}, u32[]{:S(2)}) collective-permute-start(f32[192,256]{1,0:T(8,128)S(1)} %get-tuple-element.32.refs_5_), channel_id=1, source_target_pairs={{0,30},{1,31},{2,0},{3,1},{4,2},{5,3},{6,4},{7,5},{8,6},{9,7},{10,... | collective-permute-start | bytes 589832 | tf_op jit(solution)/shard_map/ppermute | solution.py:29
  128.5 1.7 collective-permute-start.7
  132.2 1.7 collective-permute-done.13.refs_7_.refs_19_
  134.6 10.7 %collective-permute-start.17 = (f32[192,256]{1,0:T(8,128)S(1)}, f32[192,256]{1,0:T(8,128)S(1)}, u32[]{:S(2)}, u32[]{:S(2)}) collective-permute-start(f32[192,256]{1,0:T(8,128)S(1)} %get-tuple-element.43), channel_id=1, source_target_pairs={{0,30},{1,31},{2,0},{3,1},{4,2},{5,3},{6,4},{7,5},{8,6},{9,7},{10,... | collective-permute-start | bytes 589832 | tf_op jit(solution)/shard_map/ppermute | solution.py:29
  145.3 2.8 %collective-permute-done.16.refs_22_ = f32[192,256]{1,0:T(8,128)S(1)} collective-permute-done((f32[192,256]{1,0:T(8,128)S(1)}, f32[192,256]{1,0:T(8,128)S(1)}, u32[]{:S(2)}, u32[]{:S(2)}) %collective-permute-start.16) | collective-permute-done | bytes 196640 | tf_op jit(solution)/shard_map/ppermute | solution.py:29
  148.7 3.5 %collective-permute-start = (f32[384,768]{1,0:T(8,128)}, f32[384,768]{1,0:T(8,128)}, u32[]{:S(2)}, u32[]{:S(2)}) collective-permute-start(f32[384,768]{1,0:T(8,128)} %get-tuple-element.25), channel_id=1, source_target_pairs={{0,1},{2,3},{4,5},{6,7},{8,9},{10,11},{12,13},{14,15},{16,17},{18,... | collective-permute-start | bytes 3538952 | tf_op jit(solution)/shard_map/ppermute | solution.py:666
  152.2 1.3 collective-permute-start.2
  154.2 3.7 %collective-permute-start.6 = (f32[384,256]{1,0:T(8,128)}, f32[384,256]{1,0:T(8,128)}, u32[]{:S(2)}, u32[]{:S(2)}) collective-permute-start(f32[384,256]{1,0:T(8,128)} %get-tuple-element.28.refs_2_), channel_id=1, source_target_pairs={{0,1},{1,2},{2,3},{3,4},{4,5},{5,6},{6,7},{7,8},{8,9},{9,10},{10,1... | collective-permute-start | bytes 1179656 | tf_op jit(solution)/shard_map/ppermute | solution.py:29
  159.4 5.3 %collective-permute-start.11 = (f32[384,256]{1,0:T(8,128)}, f32[384,256]{1,0:T(8,128)}, u32[]{:S(2)}, u32[]{:S(2)}) collective-permute-start(f32[384,256]{1,0:T(8,128)} %get-tuple-element.37.refs_10_), channel_id=1, source_target_pairs={{0,31},{1,0},{2,1},{3,2},{4,3},{5,4},{6,5},{7,6},{8,7},{9,8},{10,9... | collective-permute-start | bytes 1179656 | tf_op jit(solution)/shard_map/ppermute | solution.py:29
  165.4 29.3 %collective-permute-done.6.refs_0_.refs_12_ = f32[384,256]{1,0:T(8,128)} collective-permute-done((f32[384,256]{1,0:T(8,128)}, f32[384,256]{1,0:T(8,128)}, u32[]{:S(2)}, u32[]{:S(2)}) %collective-permute-start.6) | collective-permute-done | bytes 393248 | tf_op jit(solution)/shard_map/ppermute | solution.py:29
  194.7 2.5 collective-permute-start.3
  197.2 5.9 %collective-permute-done.10.refs_4_.refs_16_ = f32[384,256]{1,0:T(8,128)} collective-permute-done((f32[384,256]{1,0:T(8,128)}, f32[384,256]{1,0:T(8,128)}, u32[]{:S(2)}, u32[]{:S(2)}) %collective-permute-start.10) | collective-permute-done | bytes 393248 | tf_op jit(solution)/shard_map/ppermute | solution.py:29
  203.1 2.5 collective-permute-start.14
  205.6 22.1 %collective-permute-done.11.refs_5_.refs_17_ = f32[384,256]{1,0:T(8,128)} collective-permute-done((f32[384,256]{1,0:T(8,128)}, f32[384,256]{1,0:T(8,128)}, u32[]{:S(2)}, u32[]{:S(2)}) %collective-permute-start.11) | collective-permute-done | bytes 393248 | tf_op jit(solution)/shard_map/ppermute | solution.py:29
  227.8 1.1 copy-done.7
  228.8 0.9 copy-done.12
  229.7 0.9 copy-done.17
  230.7 0.9 copy-done.20
  231.6 0.9 copy-done.23
  232.6 11.3 %early.1.refs_24_ = f32[4,768,768]{2,1,0:T(8,128)} custom-call(f32[576,768]{1,0:T(8,128)S(1)} %get-tuple-element.24.refs_0_.x_ref, f32[384,256]{1,0:T(8,128)} %collective-permute-done.6.refs_0_.refs_12_, f32[384,256]{1,0:T(8,128)S(1)} %copy-done.7, f32[192,256]{1,0:T(8,128)S(1)} %copy-done.12, f32[192,256]{1,0:T(8,128)S(1)} %copy-done.17, ...), custom_call_target="tpu_custom_call" | custom-call | flops 8000000000 | bytes 9437184 | tf_op jit(solution)/shard_map/early/pallas_call | solution.py:453
  244.1 21.4 %late.1 = (f32[3,768,768]{2,1,0:T(8,128)}, f32[4,768,768]{2,1,0:T(8,128)}) custom-call(s32[5]{0:T(128)S(1)} %gather_fusion, f32[576,768]{1,0:T(8,128)S(1)} %get-tuple-element.24.refs_0_.x_ref, f32[1,768]{1,0:T(1,128)S(1)} %copy-done.29, f32[384,768]{1,0:T(8,128)} %collective-permute-done.refs_2_, ...), custom_call_target="tpu_custom_call", output_to_operand_aliasing={{1}: (25, {})} | custom-call | flops 12000000000 | bytes 16515072 | tf_op jit(solution)/shard_map/late/pallas_call | solution.py:615
  (81 shorter events, 9.1 us)
Async XLA Ops:
  0.6 164.1 %copy-start = (s32[32]{0:T(128)S(1)}, s32[32]{0:T(128)}, u32[]{:S(2)}) copy-start(s32[32]{0:T(128)} %param.8) | copy-start | bytes 388
  57.9 94.4 %collective-permute-start.1 = (f32[384,768]{1,0:T(8,128)}, f32[384,768]{1,0:T(8,128)S(1)}, u32[]{:S(2)}, u32[]{:S(2)}) collective-permute-start(f32[384,768]{1,0:T(8,128)} %get-tuple-element.25), channel_id=1, source_target_pairs={{0,2},{1,3},{2,4},{3,5},{4,6},{5,7},{6,8},{7,9},{8,10},{9,11},{10,... | collective-permute-start | bytes 3538952 | tf_op jit(solution)/shard_map/ppermute | solution.py:29
  76.7 51.8 %copy-start.1 = (f32[384,256]{1,0:T(8,128)}, f32[384,256]{1,0:T(8,128)S(1)}, u32[]{:S(2)}) copy-start(f32[384,256]{1,0:T(8,128)S(1)} %get-tuple-element.36.refs_9_) | copy-start | bytes 1179652
  76.7 51.1 %collective-permute-start.8 = (f32[192,256]{1,0:T(8,128)S(1)}, f32[192,256]{1,0:T(8,128)S(1)}, u32[]{:S(2)}, u32[]{:S(2)}) collective-permute-start(f32[192,256]{1,0:T(8,128)S(1)} %get-tuple-element.39), channel_id=1, source_target_pairs={{0,2},{1,3},{2,4},{3,5},{4,6},{5,7},{6,8},{7,9},{8,10},{9,11},{10,... | collective-permute-start | bytes 589832 | tf_op jit(solution)/shard_map/ppermute | solution.py:29
  93.0 71.7 %copy-start.32 = (s32[5]{0:T(128)S(1)}, s32[5]{0:T(128)}, u32[]{:S(2)}) copy-start(s32[5]{0:T(128)} %constant.29.clone) | copy-start | bytes 64
  112.1 9.9 %collective-permute-start.5 = (f32[192,192]{1,0:T(8,128)S(1)}, f32[192,192]{1,0:T(8,128)S(1)}, u32[]{:S(2)}, u32[]{:S(2)}) collective-permute-start(f32[192,192]{1,0:T(8,128)S(1)} %get-tuple-element.35), channel_id=1, source_target_pairs={{0,2},{1,3},{2,4},{3,5},{4,6},{5,7},{6,8},{7,9},{8,10},{9,11},{10,... | collective-permute-start | bytes 442376 | tf_op jit(solution)/shard_map/ppermute | solution.py:29
  113.6 16.5 %collective-permute-start.9 = (f32[192,256]{1,0:T(8,128)S(1)}, f32[192,256]{1,0:T(8,128)S(1)}, u32[]{:S(2)}, u32[]{:S(2)}) collective-permute-start(f32[192,256]{1,0:T(8,128)S(1)} %get-tuple-element.29.refs_3_), channel_id=1, source_target_pairs={{0,30},{1,31},{2,0},{3,1},{4,2},{5,3},{6,4},{7,5},{8,6},{9,7},{10,... | collective-permute-start | bytes 589832 | tf_op jit(solution)/shard_map/ppermute | solution.py:29
  116.6 14.6 %collective-permute-start.12 = (f32[192,256]{1,0:T(8,128)S(1)}, f32[192,256]{1,0:T(8,128)S(1)}, u32[]{:S(2)}, u32[]{:S(2)}) collective-permute-start(f32[192,256]{1,0:T(8,128)S(1)} %get-tuple-element.40), channel_id=1, source_target_pairs={{0,2},{1,3},{2,4},{3,5},{4,6},{5,7},{6,8},{7,9},{8,10},{9,11},{10,... | collective-permute-start | bytes 589832 | tf_op jit(solution)/shard_map/ppermute | solution.py:29
  122.7 11.2 %collective-permute-start.13 = (f32[192,256]{1,0:T(8,128)S(1)}, f32[192,256]{1,0:T(8,128)S(1)}, u32[]{:S(2)}, u32[]{:S(2)}) collective-permute-start(f32[192,256]{1,0:T(8,128)S(1)} %get-tuple-element.32.refs_5_), channel_id=1, source_target_pairs={{0,30},{1,31},{2,0},{3,1},{4,2},{5,3},{6,4},{7,5},{8,6},{9,7},{10,... | collective-permute-start | bytes 589832 | tf_op jit(solution)/shard_map/ppermute | solution.py:29
  128.5 30.1 %collective-permute-start.7 = (f32[384,256]{1,0:T(8,128)S(1)}, f32[384,256]{1,0:T(8,128)S(1)}, u32[]{:S(2)}, u32[]{:S(2)}) collective-permute-start(f32[384,256]{1,0:T(8,128)S(1)} %get-tuple-element.36.refs_9_), channel_id=1, source_target_pairs={{0,31},{1,0},{2,1},{3,2},{4,3},{5,4},{6,5},{7,6},{8,7},{9,8},{10,9... | collective-permute-start | bytes 1179656 | tf_op jit(solution)/shard_map/ppermute | solution.py:29
  130.8 27.1 %collective-permute-start.4 = (f32[192,384]{1,0:T(8,128)S(1)}, f32[192,384]{1,0:T(8,128)S(1)}, u32[]{:S(2)}, u32[]{:S(2)}) collective-permute-start(f32[192,384]{1,0:T(8,128)S(1)} %get-tuple-element.34), channel_id=1, source_target_pairs={{0,1},{1,2},{2,3},{3,4},{4,5},{5,6},{6,7},{7,8},{8,9},{9,10},{10,1... | collective-permute-start | bytes 884744 | tf_op jit(solution)/shard_map/ppermute | solution.py:29
  131.9 16.2 %collective-permute-start.16 = (f32[192,256]{1,0:T(8,128)S(1)}, f32[192,256]{1,0:T(8,128)S(1)}, u32[]{:S(2)}, u32[]{:S(2)}) collective-permute-start(f32[192,256]{1,0:T(8,128)S(1)} %get-tuple-element.42), channel_id=1, source_target_pairs={{0,2},{1,3},{2,4},{3,5},{4,6},{5,7},{6,8},{7,9},{8,10},{9,11},{10,... | collective-permute-start | bytes 589832 | tf_op jit(solution)/shard_map/ppermute | solution.py:29
  134.6 18.9 %collective-permute-start.17 = (f32[192,256]{1,0:T(8,128)S(1)}, f32[192,256]{1,0:T(8,128)S(1)}, u32[]{:S(2)}, u32[]{:S(2)}) collective-permute-start(f32[192,256]{1,0:T(8,128)S(1)} %get-tuple-element.43), channel_id=1, source_target_pairs={{0,30},{1,31},{2,0},{3,1},{4,2},{5,3},{6,4},{7,5},{8,6},{9,7},{10,... | collective-permute-start | bytes 589832 | tf_op jit(solution)/shard_map/ppermute | solution.py:29
  148.7 95.2 %collective-permute-start = (f32[384,768]{1,0:T(8,128)}, f32[384,768]{1,0:T(8,128)}, u32[]{:S(2)}, u32[]{:S(2)}) collective-permute-start(f32[384,768]{1,0:T(8,128)} %get-tuple-element.25), channel_id=1, source_target_pairs={{0,1},{2,3},{4,5},{6,7},{8,9},{10,11},{12,13},{14,15},{16,17},{18,... | collective-permute-start | bytes 3538952 | tf_op jit(solution)/shard_map/ppermute | solution.py:666
  152.2 91.7 %collective-permute-start.2 = (f32[384,768]{1,0:T(8,128)S(1)}, f32[384,768]{1,0:T(8,128)}, u32[]{:S(2)}, u32[]{:S(2)}) collective-permute-start(f32[384,768]{1,0:T(8,128)S(1)} %collective-permute-done.1.refs_4_), channel_id=1, source_target_pairs={{1,0},{3,2},{5,4},{7,6},{9,8},{11,10},{13,12},{15,14},{17,16},{19,... | collective-permute-start | bytes 3538952 | tf_op jit(solution)/shard_map/ppermute | solution.py:680
  154.2 40.4 %collective-permute-start.6 = (f32[384,256]{1,0:T(8,128)}, f32[384,256]{1,0:T(8,128)}, u32[]{:S(2)}, u32[]{:S(2)}) collective-permute-start(f32[384,256]{1,0:T(8,128)} %get-tuple-element.28.refs_2_), channel_id=1, source_target_pairs={{0,1},{1,2},{2,3},{3,4},{4,5},{5,6},{6,7},{7,8},{8,9},{9,10},{10,1... | collective-permute-start | bytes 1179656 | tf_op jit(solution)/shard_map/ppermute | solution.py:29
  158.6 44.5 %collective-permute-start.10 = (f32[384,256]{1,0:T(8,128)}, f32[384,256]{1,0:T(8,128)}, u32[]{:S(2)}, u32[]{:S(2)}) collective-permute-start(f32[384,256]{1,0:T(8,128)} %get-tuple-element.31.refs_4_), channel_id=1, source_target_pairs={{0,1},{1,2},{2,3},{3,4},{4,5},{5,6},{6,7},{7,8},{8,9},{9,10},{10,1... | collective-permute-start | bytes 1179656 | tf_op jit(solution)/shard_map/ppermute | solution.py:29
  159.4 68.4 %collective-permute-start.11 = (f32[384,256]{1,0:T(8,128)}, f32[384,256]{1,0:T(8,128)}, u32[]{:S(2)}, u32[]{:S(2)}) collective-permute-start(f32[384,256]{1,0:T(8,128)} %get-tuple-element.37.refs_10_), channel_id=1, source_target_pairs={{0,31},{1,0},{2,1},{3,2},{4,3},{5,4},{6,5},{7,6},{8,7},{9,8},{10,9... | collective-permute-start | bytes 1179656 | tf_op jit(solution)/shard_map/ppermute | solution.py:29
  194.7 49.3 %collective-permute-start.3 = (f32[192,768]{1,0:T(8,128)S(1)}, f32[192,768]{1,0:T(8,128)S(1)}, u32[]{:S(2)}, u32[]{:S(2)}) collective-permute-start(f32[192,768]{1,0:T(8,128)S(1)} %get-tuple-element.26), channel_id=1, source_target_pairs={{0,1},{1,2},{2,3},{3,4},{4,5},{5,6},{6,7},{7,8},{8,9},{9,10},{10,1... | collective-permute-start | bytes 1769480 | tf_op jit(solution)/shard_map/ppermute | solution.py:29
  203.1 40.8 %collective-permute-start.14 = (f32[384,256]{1,0:T(8,128)}, f32[384,256]{1,0:T(8,128)S(1)}, u32[]{:S(2)}, u32[]{:S(2)}) collective-permute-start(f32[384,256]{1,0:T(8,128)} %copy-done.5), channel_id=1, source_target_pairs={{0,1},{1,2},{2,3},{3,4},{4,5},{5,6},{6,7},{7,8},{8,9},{9,10},{10,1... | collective-permute-start | bytes 1179656 | tf_op jit(solution)/shard_map/ppermute | solution.py:29
  227.7 16.2 %copy-start.2 = (f32[384,256]{1,0:T(8,128)S(1)}, f32[384,256]{1,0:T(8,128)}, u32[]{:S(2)}) copy-start(f32[384,256]{1,0:T(8,128)} %copy-done.1) | copy-start | bytes 1179652
  227.7 16.2 %copy-start.4 = (f32[384,256]{1,0:T(8,128)S(1)}, f32[384,256]{1,0:T(8,128)}, u32[]{:S(2)}) copy-start(f32[384,256]{1,0:T(8,128)} %copy-done.3) | copy-start | bytes 1179652
  227.7 16.2 %collective-permute-start.15 = (f32[384,256]{1,0:T(8,128)}, f32[384,256]{1,0:T(8,128)S(1)}, u32[]{:S(2)}, u32[]{:S(2)}) collective-permute-start(f32[384,256]{1,0:T(8,128)} %copy-done.3), channel_id=1, source_target_pairs={{0,31},{1,0},{2,1},{3,2},{4,3},{5,4},{6,5},{7,6},{8,7},{9,8},{10,9... | collective-permute-start | bytes 1179656 | tf_op jit(solution)/shard_map/ppermute | solution.py:29
  232.5 11.5 %copy-start.10 = (f32[192,384]{1,0:T(8,128)S(1)}, f32[192,384]{1,0:T(8,128)}, u32[]{:S(2)}) copy-start(f32[192,384]{1,0:T(8,128)} %copy-done.9) | copy-start | bytes 884740
  232.5 11.5 %copy-start.13 = (f32[192,256]{1,0:T(8,128)S(1)}, f32[192,256]{1,0:T(8,128)}, u32[]{:S(2)}) copy-start(f32[192,256]{1,0:T(8,128)} %copy-done.11) | copy-start | bytes 589828
  232.5 11.5 %copy-start.15 = (f32[192,192]{1,0:T(8,128)S(1)}, f32[192,192]{1,0:T(8,128)}, u32[]{:S(2)}) copy-start(f32[192,192]{1,0:T(8,128)} %copy-done.14) | copy-start | bytes 442372
  232.5 11.5 %copy-start.18 = (f32[192,256]{1,0:T(8,128)S(1)}, f32[192,256]{1,0:T(8,128)}, u32[]{:S(2)}) copy-start(f32[192,256]{1,0:T(8,128)} %copy-done.16) | copy-start | bytes 589828
  232.5 11.5 %copy-start.21 = (f32[192,256]{1,0:T(8,128)S(1)}, f32[192,256]{1,0:T(8,128)}, u32[]{:S(2)}) copy-start(f32[192,256]{1,0:T(8,128)} %copy-done.19) | copy-start | bytes 589828
  232.6 11.5 %copy-start.24 = (f32[192,256]{1,0:T(8,128)S(1)}, f32[192,256]{1,0:T(8,128)}, u32[]{:S(2)}) copy-start(f32[192,256]{1,0:T(8,128)} %copy-done.22) | copy-start | bytes 589828
  232.6 11.5 %copy-start.26 = (f32[192,256]{1,0:T(8,128)S(1)}, f32[192,256]{1,0:T(8,128)}, u32[]{:S(2)}) copy-start(f32[192,256]{1,0:T(8,128)} %copy-done.25) | copy-start | bytes 589828
  232.6 11.5 %copy-start.28 = (f32[192,256]{1,0:T(8,128)S(1)}, f32[192,256]{1,0:T(8,128)}, u32[]{:S(2)}) copy-start(f32[192,256]{1,0:T(8,128)} %copy-done.27) | copy-start | bytes 589828
  232.6 11.5 %copy-start.31 = (f32[768,768]{1,0:T(8,128)S(1)}, f32[768,768]{1,0:T(8,128)}, u32[]{:S(2)}) copy-start(f32[768,768]{1,0:T(8,128)} %copy-done.30) | copy-start | bytes 7077892
  (19 other events, 27.5 us)
where the time goes:
time: 268 us; the launch traced here: 266 us
  Pallas kernels  89 us (33%)
  waiting for transfers between devices  67.3 us (25%)
  blocking collectives  51.7 us (19%)
  starting transfers between devices  41.9 us (16%)
  local copies, waits for them, and re-layouts  14.6 us (5%)
    ppermute x16, waiting for transfers between devices, passed_along(): return lax.ppermute(value, AXES, pairs)  67.3 us
    all_to_all x1, blocking collectives, local(): lax.all_to_all(chunks, AXES, split_axis=0, concat_axis=0, tiled=True)  51.7 us
    pallas_call x3, Pallas kernels, factored_part(): pl.pallas_call(functools.partial(part_kernel, side, bounds, number), out_...  50.7 us
    ppermute x16, starting transfers between devices, passed_along(): return lax.ppermute(value, AXES, pairs)  37.1 us
    pallas_call x1, Pallas kernels, late(): pl.pallas_call(functools.partial(late_kernel, side, starts), out_shape=(j...  21.4 us
    unnamed x66, local copies, waits for them, and re-layouts  14 us
    pallas_call x1, Pallas kernels, early(): pl.pallas_call(functools.partial(early_kernel, side, starts), out_shape=j...  11.3 us
  transfers between devices with their start and end apart: 18, of which 6 were waited for; matrix products, arithmetic and copies ran while one was open for 0% of the time, Pallas kernels for 23%

commit v1 on v0

--- a/solution.py
+++ b/solution.py
@@ -13,7 +13,7 @@
 TILE = 128
 GROUP = 8
 WIDE = 256
-PARTS = 3
+PARTS = 4
 NT = (((1,), (1,)), ((), ()))
 TN = (((0,), (0,)), ((), ()))
 NN = (((1,), (0,)), ((), ()))
@@ -647,7 +647,7 @@
     capacity = max(2, (3 * surfels + 2 * count - 1) // (2 * count))
     side = count * capacity
     tiles = width // TILE
-    bounds = tuple(tiles * k // PARTS for k in range(PARTS + 1))
+    bounds = (0, 1, tiles // 2, tiles - 1, tiles)
     starts = tuple(bound * TILE for bound in bounds[:-1])
     flags = removal_flags[(own + jnp.array((0, 1, 2, -1, -2), jnp.int32)) % count]
 
@@ -674,10 +674,11 @@
     known = [part]
     parts = [sent_parts(part)]
     for number in range(1, PARTS - 1):
+        if number == 2:
+            onward = lax.ppermute(second, AXES, [(k + 1, k) for k in range(0, count, 2)])
         low, *part = solved(number, low, known)
         known.append(part)
         parts.append(sent_parts(part))
-    onward = lax.ppermute(second, AXES, [(k + 1, k) for k in range(0, count, 2)])
     extra = passed_along(last, 1)
     low, *part, gram_one, gram_two = solved(PARTS - 1, low, known)
     known.append(part)

time: 268 us -> 272 us (1.015)
  local copies, waits for them, and re-layouts: 14.6 us -> 20.6 us
  Pallas kernels: 89 us -> 92.2 us
  starting transfers between devices: 41.9 us -> 38.9 us
    unnamed x66 -> x92, local copies, waits for them, and re-layouts: 14 us -> 20 us
    ppermute x16 -> x20, starting transfers between devices: 37.1 us -> 33 us  [passed_along(): return lax.ppermute(value, AXES, pairs)]
    pallas_call x1, Pallas kernels: 11.3 us -> 14.8 us  [early(): pl.pallas_call(functools.partial(early_kernel, side, starts), out_shape=j...]
    ppermute x16 -> x20, waiting for transfers between devices: 67.3 us -> 64.8 us  [passed_along(): return lax.ppermute(value, AXES, pairs)]
    pallas_call x3 -> x4, Pallas kernels: 50.7 us -> 51 us  [factored_part(): pl.pallas_call(functools.partial(part_kernel, side, bounds, number), out_...]
  transfers between devices with their start and end apart: 18 -> 22, of which waited for: 6 -> 7; matrix products, arithmetic and copies ran while one was open for 0% -> 0% of each run, Pallas kernels for 23% -> 24%
where the time goes in v1:
time: 272 us; the launch traced here: 269 us
  Pallas kernels  92.2 us (34%)
  waiting for transfers between devices  64.8 us (24%)
  blocking collectives  51.7 us (19%)
  starting transfers between devices  38.9 us (14%)
  local copies, waits for them, and re-layouts  20.6 us (8%)
    ppermute x20, waiting for transfers between devices, passed_along(): return lax.ppermute(value, AXES, pairs)  64.8 us
    all_to_all x1, blocking collectives, local(): lax.all_to_all(chunks, AXES, split_axis=0, concat_axis=0, tiled=True)  51.7 us
    pallas_call x4, Pallas kernels, factored_part(): pl.pallas_call(functools.partial(part_kernel, side, bounds, number), out_...  51 us
    ppermute x20, starting transfers between devices, passed_along(): return lax.ppermute(value, AXES, pairs)  33 us
    pallas_call x1, Pallas kernels, late(): pl.pallas_call(functools.partial(late_kernel, side, starts), out_shape=(j...  20.8 us
    unnamed x92, local copies, waits for them, and re-layouts  20 us
    pallas_call x1, Pallas kernels, early(): pl.pallas_call(functools.partial(early_kernel, side, starts), out_shape=j...  14.8 us
  transfers between devices with their start and end apart: 22, of which 7 were waited for; matrix products, arithmetic and copies ran while one was open for 0% of the time, Pallas kernels for 24%

profile of v1, /device:TPU:0, one launch (start us, length us, event | category | flops | bytes accessed | tf_op | source)
XLA Modules:
  0.0 269.4 jit_solution(8640007570428110657)
XLA Ops:
  0.6 4.1 %bucket.1 = f32[32,54,256]{2,1,0:T(8,128)} custom-call(s32[1,128]{1,0:T(1,128)} %bitcast.5, f32[3,128,768]{2,1,0:T(8,128)} %bitcast.4), custom_call_target="tpu_custom_call" | custom-call | tf_op jit(solution)/shard_map/bucket/pallas_call | solution.py:85
  4.8 51.7 %all_to_all.5.in_ref = f32[32,54,256]{2,1,0:T(8,128)S(1)} all-to-all(f32[32,54,256]{2,1,0:T(8,128)} %bucket.1), channel_id=1, replica_groups=mesh['gx'=4,'gy'=8] {'gx','gy'}, dimensions={0} | all-to-all | bytes 3538944 | tf_op jit(solution)/shard_map/all_to_all | solution.py:660
  56.4 1.5 regroup.1
  58.5 8.8 %factor_part.4 = (f32[768,768]{1,0:T(8,128)S(1)}, f32[384,128]{1,0:T(8,128)S(1)}, f32[384,128]{1,0:T(8,128)S(1)}, f32[192,128]{1,0:T(8,128)S(1)}, f32[192,128]{1,0:T(8,128)S(1)}) custom-call(f32[576,768]{1,0:T(8,128)S(1)} %get-tuple-element.29.refs_0_.x_ref, f32[1,768]{1,0:T(1,128)S(1)} %copy-done.42), custom_call_target="tpu_custom_call" | custom-call | flops 20000000000 | bytes 5308416 | tf_op jit(solution)/shard_map/factor_part/pallas_call | solution.py:384
  67.4 4.4 %collective-permute-start.9 = (f32[192,128]{1,0:T(8,128)S(1)}, f32[192,128]{1,0:T(8,128)S(1)}, u32[]{:S(2)}, u32[]{:S(2)}) collective-permute-start(f32[192,128]{1,0:T(8,128)S(1)} %get-tuple-element.34.refs_3_), channel_id=1, source_target_pairs={{0,30},{1,31},{2,0},{3,1},{4,2},{5,3},{6,4},{7,5},{8,6},{9,7},{10,... | collective-permute-start | bytes 294920 | tf_op jit(solution)/shard_map/ppermute | solution.py:29
  71.9 1.1 collective-permute-start.7
  73.0 15.6 %factor_part.5 = (f32[768,768]{1,0:T(8,128)S(1)}, f32[384,256]{1,0:T(8,128)}, f32[384,256]{1,0:T(8,128)S(1)}, f32[192,256]{1,0:T(8,128)S(1)}, f32[192,256]{1,0:T(8,128)S(1)}) custom-call(f32[576,768]{1,0:T(8,128)S(1)} %get-tuple-element.29.refs_0_.x_ref, f32[768,768]{1,0:T(8,128)S(1)} %get-tuple-element.32.refs_1_, ...), custom_call_target="tpu_custom_call" | custom-call | flops 20000000000 | bytes 5308416 | tf_op jit(solution)/shard_map/factor_part/pallas_call | solution.py:384
  88.6 17.6 %factor_part.6 = (f32[768,768]{1,0:T(8,128)S(1)}, f32[384,256]{1,0:T(8,128)}, f32[384,256]{1,0:T(8,128)}, f32[192,256]{1,0:T(8,128)S(1)}, f32[192,256]{1,0:T(8,128)S(1)}) custom-call(f32[576,768]{1,0:T(8,128)S(1)} %get-tuple-element.29.refs_0_.x_ref, f32[768,768]{1,0:T(8,128)S(1)} %get-tuple-element.35.refs_1_, f32[384,128]{1,0:T(8,128)S(1)} %get-tuple-element.33.refs_2_, ...), custom_call_target="tpu_custom_call" | custom-call | flops 20000000000 | bytes 5308416 | tf_op jit(solution)/shard_map/factor_part/pallas_call | solution.py:384
  106.2 9.0 %factor_part.7 = (f32[768,768]{1,0:T(8,128)S(1)}, f32[384,128]{1,0:T(8,128)S(1)}, f32[384,128]{1,0:T(8,128)S(1)}, f32[192,128]{1,0:T(8,128)S(1)}, f32[192,128]{1...) custom-call(f32[576,768]{1,0:T(8,128)S(1)} %get-tuple-element.29.refs_0_.x_ref, ...), custom_call_target="tpu_custom_call" | custom-call | flops 20000000000 | bytes 5308416 | tf_op jit(solution)/shard_map/factor_part/pallas_call | solution.py:384
  116.6 1.4 copy-done.43
  119.9 4.4 %collective-permute-start.21 = (f32[192,128]{1,0:T(8,128)S(1)}, f32[192,128]{1,0:T(8,128)S(1)}, u32[]{:S(2)}, u32[]{:S(2)}) collective-permute-start(f32[192,128]{1,0:T(8,128)S(1)} %get-tuple-element.53), channel_id=1, source_target_pairs={{0,30},{1,31},{2,0},{3,1},{4,2},{5,3},{6,4},{7,5},{8,6},{9,7},{10,... | collective-permute-start | bytes 294920 | tf_op jit(solution)/shard_map/ppermute | solution.py:29
  124.3 5.7 %collective-permute-done.20.refs_27_ = f32[192,128]{1,0:T(8,128)S(1)} collective-permute-done((f32[192,128]{1,0:T(8,128)S(1)}, f32[192,128]{1,0:T(8,128)S(1)}, u32[]{:S(2)}, u32[]{:S(2)}) %collective-permute-start.20) | collective-permute-done | bytes 98336 | tf_op jit(solution)/shard_map/ppermute | solution.py:29
  131.3 1.1 collective-permute-start.12
  133.1 3.4 %collective-permute-start.13 = (f32[192,256]{1,0:T(8,128)S(1)}, f32[192,256]{1,0:T(8,128)S(1)}, u32[]{:S(2)}, u32[]{:S(2)}) collective-permute-start(f32[192,256]{1,0:T(8,128)S(1)} %get-tuple-element.37.refs_5_), channel_id=1, source_target_pairs={{0,30},{1,31},{2,0},{3,1},{4,2},{5,3},{6,4},{7,5},{8,6},{9,7},{10,... | collective-permute-start | bytes 589832 | tf_op jit(solution)/shard_map/ppermute | solution.py:29
  137.1 2.4 collective-permute-start.11
  139.5 2.1 collective-permute-done.6.refs_0_.refs_13_
  142.9 1.0 collective-permute-done.13.refs_7_.refs_20_
  144.6 3.4 %collective-permute-start.17 = (f32[192,256]{1,0:T(8,128)S(1)}, f32[192,256]{1,0:T(8,128)S(1)}, u32[]{:S(2)}, u32[]{:S(2)}) collective-permute-start(f32[192,256]{1,0:T(8,128)S(1)} %get-tuple-element.40.refs_7_), channel_id=1, source_target_pairs={{0,30},{1,31},{2,0},{3,1},{4,2},{5,3},{6,4},{7,5},{8,6},{9,7},{10,... | collective-permute-start | bytes 589832 | tf_op jit(solution)/shard_map/ppermute | solution.py:29
  148.1 6.1 %collective-permute-done.18.refs_25_ = f32[384,128]{1,0:T(8,128)S(1)} collective-permute-done((f32[384,128]{1,0:T(8,128)S(1)}, f32[384,128]{1,0:T(8,128)S(1)}, u32[]{:S(2)}, u32[]{:S(2)}) %collective-permute-start.18) | collective-permute-done | bytes 196640 | tf_op jit(solution)/shard_map/ppermute | solution.py:29
  154.9 4.6 %collective-permute-start = (f32[384,768]{1,0:T(8,128)}, f32[384,768]{1,0:T(8,128)}, u32[]{:S(2)}, u32[]{:S(2)}) collective-permute-start(f32[384,768]{1,0:T(8,128)} %get-tuple-element.30), channel_id=1, source_target_pairs={{0,1},{2,3},{4,5},{6,7},{8,9},{10,11},{12,13},{14,15},{16,17},{18,... | collective-permute-start | bytes 3538952 | tf_op jit(solution)/shard_map/ppermute | solution.py:666
  159.5 1.3 collective-permute-start.2
  161.4 3.6 %collective-permute-start.10 = (f32[384,256]{1,0:T(8,128)}, f32[384,256]{1,0:T(8,128)}, u32[]{:S(2)}, u32[]{:S(2)}) collective-permute-start(f32[384,256]{1,0:T(8,128)} %get-tuple-element.36.refs_4_), channel_id=1, source_target_pairs={{0,1},{1,2},{2,3},{3,4},{4,5},{5,6},{6,7},{7,8},{8,9},{9,10},{10,1... | collective-permute-start | bytes 1179656 | tf_op jit(solution)/shard_map/ppermute | solution.py:29
  166.5 5.3 %collective-permute-start.15 = (f32[384,256]{1,0:T(8,128)}, f32[384,256]{1,0:T(8,128)}, u32[]{:S(2)}, u32[]{:S(2)}) collective-permute-start(f32[384,256]{1,0:T(8,128)} %get-tuple-element.46.refs_11_), channel_id=1, source_target_pairs={{0,31},{1,0},{2,1},{3,2},{4,3},{5,4},{6,5},{7,6},{8,7},{9,8},{10,9... | collective-permute-start | bytes 1179656 | tf_op jit(solution)/shard_map/ppermute | solution.py:29
  172.5 29.4 %collective-permute-done.10.refs_4_.refs_17_ = f32[384,256]{1,0:T(8,128)} collective-permute-done((f32[384,256]{1,0:T(8,128)}, f32[384,256]{1,0:T(8,128)}, u32[]{:S(2)}, u32[]{:S(2)}) %collective-permute-start.10) | collective-permute-done | bytes 393248 | tf_op jit(solution)/shard_map/ppermute | solution.py:29
  201.9 2.5 collective-permute-start.3
  204.4 8.1 %collective-permute-done.14.refs_8_.refs_21_ = f32[384,256]{1,0:T(8,128)} collective-permute-done((f32[384,256]{1,0:T(8,128)}, f32[384,256]{1,0:T(8,128)}, u32[]{:S(2)}, u32[]{:S(2)}) %collective-permute-start.14) | collective-permute-done | bytes 393248 | tf_op jit(solution)/shard_map/ppermute | solution.py:29
  212.5 12.4 %collective-permute-done.15.refs_9_.refs_22_ = f32[384,256]{1,0:T(8,128)} collective-permute-done((f32[384,256]{1,0:T(8,128)}, f32[384,256]{1,0:T(8,128)}, u32[]{:S(2)}, u32[]{:S(2)}) %collective-permute-start.15) | collective-permute-done | bytes 393248 | tf_op jit(solution)/shard_map/ppermute | solution.py:29
  224.9 1.0 copy-done.4
  226.0 0.9 copy-done.10
  226.9 0.9 copy-done.17
  233.5 14.8 %early.1.refs_29_ = f32[4,768,768]{2,1,0:T(8,128)} custom-call(f32[576,768]{1,0:T(8,128)S(1)} %get-tuple-element.29.refs_0_.x_ref, f32[384,128]{1,0:T(8,128)S(1)} %copy-done.17, f32[384,128]{1,0:T(8,128)S(1)} %copy-done.10, f32[192,128]{1,0:T(8,128)S(1)} %copy-done.34, f32[192,128]{1,0:T(8,128)S(1)} %copy-done.37, ...), custom_call_target="tpu_custom_call" | custom-call | flops 8000000000 | bytes 9437184 | tf_op jit(solution)/shard_map/early/pallas_call | solution.py:453
  248.4 20.8 %late.1 = (f32[3,768,768]{2,1,0:T(8,128)}, f32[4,768,768]{2,1,0:T(8,128)}) custom-call(s32[5]{0:T(128)S(1)} %gather_fusion, f32[576,768]{1,0:T(8,128)S(1)} %get-tuple-element.29.refs_0_.x_ref, f32[1,768]{1,0:T(1,128)S(1)} %copy-done.42, f32[384,768]{1,0:T(8,128)} %collective-permute-done.refs_2_, ...), custom_call_target="tpu_custom_call", output_to_operand_aliasing={{1}: (30, {})} | custom-call | flops 12000000000 | bytes 16515072 | tf_op jit(solution)/shard_map/late/pallas_call | solution.py:615
  (116 shorter events, 17.7 us)
Async XLA Ops:
  0.6 171.2 %copy-start = (s32[32]{0:T(128)S(1)}, s32[32]{0:T(128)}, u32[]{:S(2)}) copy-start(s32[32]{0:T(128)} %param.8) | copy-start | bytes 388
  57.9 101.6 %collective-permute-start.1 = (f32[384,768]{1,0:T(8,128)}, f32[384,768]{1,0:T(8,128)S(1)}, u32[]{:S(2)}, u32[]{:S(2)}) collective-permute-start(f32[384,768]{1,0:T(8,128)} %get-tuple-element.30), channel_id=1, source_target_pairs={{0,2},{1,3},{2,4},{3,5},{4,6},{5,7},{6,8},{7,9},{8,10},{9,11},{10,... | collective-permute-start | bytes 3538952 | tf_op jit(solution)/shard_map/ppermute | solution.py:29
  67.4 21.3 %copy-start.7 = (f32[384,128]{1,0:T(8,128)}, f32[384,128]{1,0:T(8,128)S(1)}, u32[]{:S(2)}) copy-start(f32[384,128]{1,0:T(8,128)S(1)} %get-tuple-element.44.refs_9_) | copy-start | bytes 589828
  67.4 51.2 %collective-permute-start.8 = (f32[192,128]{1,0:T(8,128)S(1)}, f32[192,128]{1,0:T(8,128)S(1)}, u32[]{:S(2)}, u32[]{:S(2)}) collective-permute-start(f32[192,128]{1,0:T(8,128)S(1)} %get-tuple-element.48), channel_id=1, source_target_pairs={{0,2},{1,3},{2,4},{3,5},{4,6},{5,7},{6,8},{7,9},{8,10},{9,11},{10,... | collective-permute-start | bytes 294920 | tf_op jit(solution)/shard_map/ppermute | solution.py:29
  67.4 51.8 %collective-permute-start.9 = (f32[192,128]{1,0:T(8,128)S(1)}, f32[192,128]{1,0:T(8,128)S(1)}, u32[]{:S(2)}, u32[]{:S(2)}) collective-permute-start(f32[192,128]{1,0:T(8,128)S(1)} %get-tuple-element.34.refs_3_), channel_id=1, source_target_pairs={{0,30},{1,31},{2,0},{3,1},{4,2},{5,3},{6,4},{7,5},{8,6},{9,7},{10,... | collective-permute-start | bytes 294920 | tf_op jit(solution)/shard_map/ppermute | solution.py:29
  71.9 64.6 %collective-permute-start.7 = (f32[384,128]{1,0:T(8,128)S(1)}, f32[384,128]{1,0:T(8,128)S(1)}, u32[]{:S(2)}, u32[]{:S(2)}) collective-permute-start(f32[384,128]{1,0:T(8,128)S(1)} %get-tuple-element.44.refs_9_), channel_id=1, source_target_pairs={{0,31},{1,0},{2,1},{3,2},{4,3},{5,4},{6,5},{7,6},{8,7},{9,8},{10,9... | collective-permute-start | bytes 589832 | tf_op jit(solution)/shard_map/ppermute | solution.py:29
  88.6 48.5 %copy-start.1 = (f32[384,256]{1,0:T(8,128)}, f32[384,256]{1,0:T(8,128)S(1)}, u32[]{:S(2)}) copy-start(f32[384,256]{1,0:T(8,128)S(1)} %get-tuple-element.45.refs_10_) | copy-start | bytes 1179652
  106.2 65.6 %copy-start.45 = (s32[5]{0:T(128)S(1)}, s32[5]{0:T(128)}, u32[]{:S(2)}) copy-start(s32[5]{0:T(128)} %constant.29.clone) | copy-start | bytes 64
  118.0 14.4 %collective-permute-start.5 = (f32[192,192]{1,0:T(8,128)S(1)}, f32[192,192]{1,0:T(8,128)S(1)}, u32[]{:S(2)}, u32[]{:S(2)}) collective-permute-start(f32[192,192]{1,0:T(8,128)S(1)} %get-tuple-element.43), channel_id=1, source_target_pairs={{0,2},{1,3},{2,4},{3,5},{4,6},{5,7},{6,8},{7,9},{8,10},{9,11},{10,... | collective-permute-start | bytes 442376 | tf_op jit(solution)/shard_map/ppermute | solution.py:29
  119.2 10.8 %collective-permute-start.20 = (f32[192,128]{1,0:T(8,128)S(1)}, f32[192,128]{1,0:T(8,128)S(1)}, u32[]{:S(2)}, u32[]{:S(2)}) collective-permute-start(f32[192,128]{1,0:T(8,128)S(1)} %get-tuple-element.52), channel_id=1, source_target_pairs={{0,2},{1,3},{2,4},{3,5},{4,6},{5,7},{6,8},{7,9},{8,10},{9,11},{10,... | collective-permute-start | bytes 294920 | tf_op jit(solution)/shard_map/ppermute | solution.py:29
  119.9 10.8 %collective-permute-start.21 = (f32[192,128]{1,0:T(8,128)S(1)}, f32[192,128]{1,0:T(8,128)S(1)}, u32[]{:S(2)}, u32[]{:S(2)}) collective-permute-start(f32[192,128]{1,0:T(8,128)S(1)} %get-tuple-element.53), channel_id=1, source_target_pairs={{0,30},{1,31},{2,0},{3,1},{4,2},{5,3},{6,4},{7,5},{8,6},{9,7},{10,... | collective-permute-start | bytes 294920 | tf_op jit(solution)/shard_map/ppermute | solution.py:29
  130.7 10.9 %collective-permute-start.6 = (f32[384,128]{1,0:T(8,128)S(1)}, f32[384,128]{1,0:T(8,128)S(1)}, u32[]{:S(2)}, u32[]{:S(2)}) collective-permute-start(f32[384,128]{1,0:T(8,128)S(1)} %get-tuple-element.33.refs_2_), channel_id=1, source_target_pairs={{0,1},{1,2},{2,3},{3,4},{4,5},{5,6},{6,7},{7,8},{8,9},{9,10},{10,1... | collective-permute-start | bytes 589832 | tf_op jit(solution)/shard_map/ppermute | solution.py:29
  131.3 10.9 %collective-permute-start.12 = (f32[192,256]{1,0:T(8,128)S(1)}, f32[192,256]{1,0:T(8,128)S(1)}, u32[]{:S(2)}, u32[]{:S(2)}) collective-permute-start(f32[192,256]{1,0:T(8,128)S(1)} %get-tuple-element.49), channel_id=1, source_target_pairs={{0,2},{1,3},{2,4},{3,5},{4,6},{5,7},{6,8},{7,9},{8,10},{9,11},{10,... | collective-permute-start | bytes 589832 | tf_op jit(solution)/shard_map/ppermute | solution.py:29
  133.1 10.9 %collective-permute-start.13 = (f32[192,256]{1,0:T(8,128)S(1)}, f32[192,256]{1,0:T(8,128)S(1)}, u32[]{:S(2)}, u32[]{:S(2)}) collective-permute-start(f32[192,256]{1,0:T(8,128)S(1)} %get-tuple-element.37.refs_5_), channel_id=1, source_target_pairs={{0,30},{1,31},{2,0},{3,1},{4,2},{5,3},{6,4},{7,5},{8,6},{9,7},{10,... | collective-permute-start | bytes 589832 | tf_op jit(solution)/shard_map/ppermute | solution.py:29
  137.1 28.6 %collective-permute-start.11 = (f32[384,256]{1,0:T(8,128)S(1)}, f32[384,256]{1,0:T(8,128)S(1)}, u32[]{:S(2)}, u32[]{:S(2)}) collective-permute-start(f32[384,256]{1,0:T(8,128)S(1)} %get-tuple-element.45.refs_10_), channel_id=1, source_target_pairs={{0,31},{1,0},{2,1},{3,2},{4,3},{5,4},{6,5},{7,6},{8,7},{9,8},{10,9... | collective-permute-start | bytes 1179656 | tf_op jit(solution)/shard_map/ppermute | solution.py:29
  142.2 12.0 %collective-permute-start.18 = (f32[384,128]{1,0:T(8,128)S(1)}, f32[384,128]{1,0:T(8,128)S(1)}, u32[]{:S(2)}, u32[]{:S(2)}) collective-permute-start(f32[384,128]{1,0:T(8,128)S(1)} %get-tuple-element.51), channel_id=1, source_target_pairs={{0,1},{1,2},{2,3},{3,4},{4,5},{5,6},{6,7},{7,8},{8,9},{9,10},{10,1... | collective-permute-start | bytes 589832 | tf_op jit(solution)/shard_map/ppermute | solution.py:29
  142.9 17.8 %collective-permute-start.16 = (f32[192,256]{1,0:T(8,128)S(1)}, f32[192,256]{1,0:T(8,128)S(1)}, u32[]{:S(2)}, u32[]{:S(2)}) collective-permute-start(f32[192,256]{1,0:T(8,128)S(1)} %get-tuple-element.50), channel_id=1, source_target_pairs={{0,2},{1,3},{2,4},{3,5},{4,6},{5,7},{6,8},{7,9},{8,10},{9,11},{10,... | collective-permute-start | bytes 589832 | tf_op jit(solution)/shard_map/ppermute | solution.py:29
  144.6 20.5 %collective-permute-start.17 = (f32[192,256]{1,0:T(8,128)S(1)}, f32[192,256]{1,0:T(8,128)S(1)}, u32[]{:S(2)}, u32[]{:S(2)}) collective-permute-start(f32[192,256]{1,0:T(8,128)S(1)} %get-tuple-element.40.refs_7_), channel_id=1, source_target_pairs={{0,30},{1,31},{2,0},{3,1},{4,2},{5,3},{6,4},{7,5},{8,6},{9,7},{10,... | collective-permute-start | bytes 589832 | tf_op jit(solution)/shard_map/ppermute | solution.py:29
  154.9 93.4 %collective-permute-start = (f32[384,768]{1,0:T(8,128)}, f32[384,768]{1,0:T(8,128)}, u32[]{:S(2)}, u32[]{:S(2)}) collective-permute-start(f32[384,768]{1,0:T(8,128)} %get-tuple-element.30), channel_id=1, source_target_pairs={{0,1},{2,3},{4,5},{6,7},{8,9},{10,11},{12,13},{14,15},{16,17},{18,... | collective-permute-start | bytes 3538952 | tf_op jit(solution)/shard_map/ppermute | solution.py:666
  159.5 88.8 %collective-permute-start.2 = (f32[384,768]{1,0:T(8,128)S(1)}, f32[384,768]{1,0:T(8,128)}, u32[]{:S(2)}, u32[]{:S(2)}) collective-permute-start(f32[384,768]{1,0:T(8,128)S(1)} %collective-permute-done.1.refs_4_), channel_id=1, source_target_pairs={{1,0},{3,2},{5,4},{7,6},{9,8},{11,10},{13,12},{15,14},{17,16},{19,... | collective-permute-start | bytes 3538952 | tf_op jit(solution)/shard_map/ppermute | solution.py:678
  161.4 40.5 %collective-permute-start.10 = (f32[384,256]{1,0:T(8,128)}, f32[384,256]{1,0:T(8,128)}, u32[]{:S(2)}, u32[]{:S(2)}) collective-permute-start(f32[384,256]{1,0:T(8,128)} %get-tuple-element.36.refs_4_), channel_id=1, source_target_pairs={{0,1},{1,2},{2,3},{3,4},{4,5},{5,6},{6,7},{7,8},{8,9},{9,10},{10,1... | collective-permute-start | bytes 1179656 | tf_op jit(solution)/shard_map/ppermute | solution.py:29
  165.7 46.7 %collective-permute-start.14 = (f32[384,256]{1,0:T(8,128)}, f32[384,256]{1,0:T(8,128)}, u32[]{:S(2)}, u32[]{:S(2)}) collective-permute-start(f32[384,256]{1,0:T(8,128)} %get-tuple-element.39.refs_6_), channel_id=1, source_target_pairs={{0,1},{1,2},{2,3},{3,4},{4,5},{5,6},{6,7},{7,8},{8,9},{9,10},{10,1... | collective-permute-start | bytes 1179656 | tf_op jit(solution)/shard_map/ppermute | solution.py:29
  166.5 58.4 %collective-permute-start.15 = (f32[384,256]{1,0:T(8,128)}, f32[384,256]{1,0:T(8,128)}, u32[]{:S(2)}, u32[]{:S(2)}) collective-permute-start(f32[384,256]{1,0:T(8,128)} %get-tuple-element.46.refs_11_), channel_id=1, source_target_pairs={{0,31},{1,0},{2,1},{3,2},{4,3},{5,4},{6,5},{7,6},{8,7},{9,8},{10,9... | collective-permute-start | bytes 1179656 | tf_op jit(solution)/shard_map/ppermute | solution.py:29
  201.9 46.3 %collective-permute-start.3 = (f32[192,768]{1,0:T(8,128)S(1)}, f32[192,768]{1,0:T(8,128)S(1)}, u32[]{:S(2)}, u32[]{:S(2)}) collective-permute-start(f32[192,768]{1,0:T(8,128)S(1)} %get-tuple-element.31), channel_id=1, source_target_pairs={{0,1},{1,2},{2,3},{3,4},{4,5},{5,6},{6,7},{7,8},{8,9},{9,10},{10,1... | collective-permute-start | bytes 1769480 | tf_op jit(solution)/shard_map/ppermute | solution.py:29
  212.5 35.7 %collective-permute-start.19 = (f32[384,128]{1,0:T(8,128)}, f32[384,128]{1,0:T(8,128)S(1)}, u32[]{:S(2)}, u32[]{:S(2)}) collective-permute-start(f32[384,128]{1,0:T(8,128)} %copy-done.12), channel_id=1, source_target_pairs={{0,31},{1,0},{2,1},{3,2},{4,3},{5,4},{6,5},{7,6},{8,7},{9,8},{10,9... | collective-permute-start | bytes 589832 | tf_op jit(solution)/shard_map/ppermute | solution.py:29
  224.9 23.3 %copy-start.2 = (f32[384,256]{1,0:T(8,128)S(1)}, f32[384,256]{1,0:T(8,128)}, u32[]{:S(2)}) copy-start(f32[384,256]{1,0:T(8,128)} %copy-done.1) | copy-start | bytes 1179652
  224.9 23.3 %collective-permute-start.4 = (f32[192,384]{1,0:T(8,128)}, f32[192,384]{1,0:T(8,128)S(1)}, u32[]{:S(2)}, u32[]{:S(2)}) collective-permute-start(f32[192,384]{1,0:T(8,128)} %copy-done.6), channel_id=1, source_target_pairs={{0,1},{1,2},{2,3},{3,4},{4,5},{5,6},{6,7},{7,8},{8,9},{9,10},{10,1... | collective-permute-start | bytes 884744 | tf_op jit(solution)/shard_map/ppermute | solution.py:29
  233.3 15.0 %copy-start.15 = (f32[192,192]{1,0:T(8,128)S(1)}, f32[192,192]{1,0:T(8,128)}, u32[]{:S(2)}) copy-start(f32[192,192]{1,0:T(8,128)} %copy-done.14) | copy-start | bytes 442372
  233.3 15.0 %copy-start.18 = (f32[384,128]{1,0:T(8,128)S(1)}, f32[384,128]{1,0:T(8,128)}, u32[]{:S(2)}) copy-start(f32[384,128]{1,0:T(8,128)} %copy-done.16) | copy-start | bytes 589828
  233.4 15.0 %copy-start.21 = (f32[192,256]{1,0:T(8,128)S(1)}, f32[192,256]{1,0:T(8,128)}, u32[]{:S(2)}) copy-start(f32[192,256]{1,0:T(8,128)} %copy-done.19) | copy-start | bytes 589828
  233.4 15.0 %copy-start.24 = (f32[192,256]{1,0:T(8,128)S(1)}, f32[192,256]{1,0:T(8,128)}, u32[]{:S(2)}) copy-start(f32[192,256]{1,0:T(8,128)} %copy-done.22) | copy-start | bytes 589828
  233.4 15.0 %copy-start.26 = (f32[384,128]{1,0:T(8,128)S(1)}, f32[384,128]{1,0:T(8,128)}, u32[]{:S(2)}) copy-start(f32[384,128]{1,0:T(8,128)} %copy-done.25) | copy-start | bytes 589828
  (36 other events, 171.7 us)

commit v2 on v0

--- a/solution.py
+++ b/solution.py
@@ -399,11 +399,15 @@
     return product_of_halves(halves(left), halves(right), dims)
 
 
-def put_coupling(side, start, y_refs, x_ref, buffer_ref, left_refs, out_ref, sems):
+COUPLINGS = ((3, 0, 1), (1, 0, 2), (0, 1, 3), (2, 2, 3))
+
+
+def put_coupling(side, start, y_refs, x_ref, buffer_ref, left_refs, out_ref, sems, places=range(4)):
     rows = buffer_ref.shape[1]
     width = x_ref.shape[1]
     copies = []
-    for place, (number, begin, end) in enumerate(((3, 0, 1), (1, 0, 2), (0, 1, 3), (2, 2, 3))):
+    for place in places:
+        number, begin, end = COUPLINGS[place]
         keep_halves(left_refs, y_refs[number][...].T)
 
         def put(lanes, value, place=place):
@@ -469,7 +473,7 @@
     )(x, *[piece for part in parts for piece in part])
 
 
-def late_kernel(side, starts, flags_ref, *refs):
+def middle_kernel(side, starts, flags_ref, *refs):
     (
         x_ref,
         shift_ref,
@@ -484,14 +488,17 @@
     parts = len(starts)
     refs = refs[9:]
     mine, refs = refs[:parts], refs[parts:]
-    pieces, refs = [refs[4 * k : 4 * k + 4] for k in range(parts)], refs[4 * parts :]
-    lasts = pieces[-1]
+    pieces, refs = [refs[4 * k : 4 * k + 4] for k in range(parts - 1)], refs[4 * parts - 4 :]
+    lasts, refs = (refs[0], None, *refs[1:3]), refs[3:]
+    pieces.append(lasts)
     partial_ref, schur_ref, coupling_ref = refs[:3]
     buffer_ref, tile_ref, rest_ref, near_ref, far_ref, high_ref, less_ref, sems, outs = refs[3:]
     left_refs = (high_ref, less_ref)
     width = x_ref.shape[1]
     cut = starts[-1]
-    copies = put_coupling(side, cut, lasts, x_ref, buffer_ref, left_refs, coupling_ref, sems)
+    copies = put_coupling(
+        side, cut, lasts, x_ref, buffer_ref, left_refs, coupling_ref, sems, (0, 3, 2)
+    )
     own, above, second_above, under, second_under = [flags_ref[k] > 0 for k in range(5)]
     one, two, three = slice(0, side), slice(side, 2 * side), slice(2 * side, 3 * side)
     pair, tail = slice(0, 2 * side), slice(side, 3 * side)
@@ -514,6 +521,8 @@
     def weighed(number, rows):
         gram = 0.0
         for part in pieces:
+            if part[number] is None:
+                continue
             both = halves(part[number][...])
             gram = gram + product_of_halves(both, both, NT)
         return near_product(gram, x_ref[rows, :], NN)
@@ -608,12 +617,13 @@
         copy.wait()
 
 
-def late(flags, x, shift, received, low, grams, mine, parts, partial, starts, side):
+def middle(flags, x, shift, received, low, grams, mine, parts, partial, starts, side):
     depth, width = x.shape
     rest = parts[-1][0].shape[1]
-    inputs = [x, shift, *received, low, *grams, *mine] + [piece for part in parts for piece in part]
+    inputs = [x, shift, *received, low, *grams, *mine] + [piece for part in parts[:-1] for piece in part]
+    inputs += [parts[-1][0], *parts[-1][2:]]
     return pl.pallas_call(
-        functools.partial(late_kernel, side, starts),
+        functools.partial(middle_kernel, side, starts),
         out_shape=(
             jax.ShapeDtypeStruct((3, width, width), jnp.float32),
             jax.ShapeDtypeStruct((4, width, width), jnp.float32),
@@ -636,8 +646,97 @@
         cost_estimate=pl.CostEstimate(
             flops=12_000_000_000, bytes_accessed=7 * width * width * 4, transcendentals=0
         ),
+        name="middle",
+    )(flags, *inputs, partial)
+
+
+def late_kernel(side, flags_ref, x_ref, direct_ref, onward_ref, y_ref, *refs):
+    tiles_ref, _, schur_ref, coupling_ref = refs[:4]
+    buffer_ref, tile_ref, high_ref, less_ref, small_ref, sem, ins, outs = refs[4:]
+    left_refs = (high_ref, less_ref)
+    rows, width = buffer_ref.shape[1:]
+    above = flags_ref[1] > 0
+
+    def moved(place, back):
+        held = tile_ref.at[place - 1]
+        if back:
+            return pltpu.make_async_copy(held, schur_ref.at[place], outs.at[place - 1])
+        return pltpu.make_async_copy(tiles_ref.at[place], held, ins.at[place - 1])
+
+    @pl.when(above)
+    def _():
+        moved(2, False).start()
+        moved(1, False).start()
+
+    keep_halves(left_refs, y_ref[...].T)
+
+    def put(lanes, value):
+        buffer_ref[0, :, lanes] = value
+
+    tall_product(left_refs, rows, 2 * side, lambda lanes: x_ref[: 2 * side, lanes], put, width)
+    copy = pltpu.make_async_copy(
+        buffer_ref.at[0], coupling_ref.at[1, pl.ds(width - rows, rows), :], sem
+    )
+    copy.start()
+
+    @pl.when(above)
+    def _():
+        keep_halves(left_refs, buffer_ref[0].T)
+        moved(2, False).wait()
+
+        def less_diag(lanes, value):
+            tile_ref[1, :, lanes] = tile_ref[1, :, lanes] - value
+
+        tall_product(left_refs, width, rows, lambda lanes: buffer_ref[0, :, lanes], less_diag, width)
+        moved(2, True).start()
+        keep_halves(left_refs, y_ref[side:, :])
+
+        def put_small(lanes, value):
+            small_ref[:, lanes] = value
+
+        tall_product(left_refs, side, rows, lambda lanes: buffer_ref[0, :, lanes], put_small, width)
+        keep_halves(left_refs, (direct_ref[:side, :] + onward_ref[:side, :]).T)
+        moved(1, False).wait()
+
+        def less_near(lanes, value):
+            tile_ref[0, :, lanes] = tile_ref[0, :, lanes] - value
+
+        tall_product(left_refs, width, side, lambda lanes: small_ref[:, lanes], less_near, width)
+        moved(1, True).start()
+        moved(2, True).wait()
+        moved(1, True).wait()
+
+    copy.wait()
+
+
+def late(flags, x, direct, onward, y, tiles, coupling, side):
+    _, width = x.shape
+    rows = y.shape[1]
+    return pl.pallas_call(
+        functools.partial(late_kernel, side),
+        out_shape=(
+            jax.ShapeDtypeStruct((3, width, width), jnp.float32),
+            jax.ShapeDtypeStruct((4, width, width), jnp.float32),
+        ),
+        in_specs=[SMEM_SPEC] + [VMEM_SPEC] * 4 + [ANY_SPEC] * 2,
+        out_specs=(ANY_SPEC, ANY_SPEC),
+        input_output_aliases={5: 0, 6: 1},
+        scratch_shapes=[
+            pltpu.VMEM((1, rows, width), jnp.float32),
+            pltpu.VMEM((2, width, width), jnp.float32),
+            pltpu.VMEM((width, max(2 * side, rows)), jnp.bfloat16),
+            pltpu.VMEM((width, max(2 * side, rows)), jnp.bfloat16),
+            pltpu.VMEM((side, width), jnp.float32),
+            pltpu.SemaphoreType.DMA,
+            pltpu.SemaphoreType.DMA((2,)),
+            pltpu.SemaphoreType.DMA((2,)),
+        ],
+        compiler_params=pltpu.CompilerParams(vmem_limit_bytes=24 << 20),
+        cost_estimate=pl.CostEstimate(
+            flops=4_000_000_000, bytes_accessed=4 * width * width * 4, transcendentals=0
+        ),
         name="late",
-    )(flags, *inputs, partial)
+    )(flags, x, direct, onward, y, tiles, coupling)
 
 
 def local(weighted_jacobian_strips, leading_pose_index, levenberg_shift, removal_flags):
@@ -684,7 +783,7 @@
     parts.append(sent_parts(part))
     grams = (passed_along(gram_one, 1), passed_along(gram_two, 2))
     partial = early(x, parts[:-1], starts[:-1], side)
-    schur, coupling = late(
+    schur, coupling = middle(
         flags,
         x,
         levenberg_shift,
@@ -697,6 +796,9 @@
         starts,
         side,
     )
+    schur, coupling = late(
+        flags, x, direct, onward, parts[-1][1], schur, coupling, side
+    )
     return schur[None], coupling[None]
 
 

time: 268 us -> 272 us (1.015)
  the two profiles are of different devices: /device:TPU:0 before, /device:TPU:1 now
where the time goes in v2:
time: 272 us; the launch traced here: 271 us
  Pallas kernels  96.3 us (35%)
  starting transfers between devices  63.1 us (23%)
  blocking collectives  50.9 us (19%)
  waiting for transfers between devices  45.2 us (17%)
  local copies, waits for them, and re-layouts  14.6 us (5%)
    ppermute x16, starting transfers between devices, passed_along(): return lax.ppermute(value, AXES, pairs)  51.1 us
    all_to_all x1, blocking collectives, local(): lax.all_to_all(chunks, AXES, split_axis=0, concat_axis=0, tiled=True)  50.9 us
    pallas_call x3, Pallas kernels, factored_part(): pl.pallas_call(functools.partial(part_kernel, side, bounds, number), out_...  49.8 us
    ppermute x16, waiting for transfers between devices, passed_along(): return lax.ppermute(value, AXES, pairs)  45.2 us
    pallas_call x1, Pallas kernels, middle(): pl.pallas_call(functools.partial(middle_kernel, side, starts), out_shape=...  21.2 us
    unnamed x58, local copies, waits for them, and re-layouts  14 us
    pallas_call x1, Pallas kernels, early(): pl.pallas_call(functools.partial(early_kernel, side, starts), out_shape=j...  11.3 us
    ppermute x1, starting transfers between devices, local(): direct = lax.ppermute(two, AXES, [(k, k + 1) for k in range(0, count, 2)])  10.7 us
  transfers between devices with their start and end apart: 18, of which 6 were waited for; matrix products, arithmetic and copies ran while one was open for 0% of the time, Pallas kernels for 30%

profile of v2, /device:TPU:1, one launch (start us, length us, event | category | flops | bytes accessed | tf_op | source)
XLA Modules:
  0.0 271.3 jit_solution(8249705455109765970)
XLA Ops:
  0.6 4.1 %bucket.1 = f32[32,54,256]{2,1,0:T(8,128)} custom-call(s32[1,128]{1,0:T(1,128)} %bitcast.7, f32[3,128,768]{2,1,0:T(8,128)} %bitcast.6), custom_call_target="tpu_custom_call" | custom-call | tf_op jit(solution)/shard_map/bucket/pallas_call | solution.py:85
  4.8 50.9 %all_to_all.5.in_ref = f32[32,54,256]{2,1,0:T(8,128)S(1)} all-to-all(f32[32,54,256]{2,1,0:T(8,128)} %bucket.1), channel_id=1, replica_groups=mesh['gx'=4,'gy'=8] {'gx','gy'}, dimensions={0} | all-to-all | bytes 3538944 | tf_op jit(solution)/shard_map/all_to_all | solution.py:759
  55.7 1.4 regroup.1
  57.8 18.3 %factor_part.3 = (f32[768,768]{1,0:T(8,128)S(1)}, f32[384,256]{1,0:T(8,128)}, f32[384,256]{1,0:T(8,128)}, f32[192,256]{1,0:T(8,128)S(1)}, f32[192,256]{1,0:T(8,128)S(1)}) custom-call(f32[576,768]{1,0:T(8,128)S(1)} %get-tuple-element.26.refs_0_.x_ref, f32[1,768]{1,0:T(1,128)S(1)} %copy-done.25), custom_call_target="tpu_custom_call" | custom-call | flops 20000000000 | bytes 5308416 | tf_op jit(solution)/shard_map/factor_part/pallas_call | solution.py:384
  76.2 15.4 %factor_part.4 = (f32[768,768]{1,0:T(8,128)S(1)}, f32[384,256]{1,0:T(8,128)S(1)}, f32[384,256]{1,0:T(8,128)}, f32[192,256]{1,0:T(8,128)S(1)}, f32[192,256]{1,0:T(8,128)S(1)}) custom-call(f32[576,768]{1,0:T(8,128)S(1)} %get-tuple-element.26.refs_0_.x_ref, f32[768,768]{1,0:T(8,128)S(1)} %get-tuple-element.28.refs_1_, f32[384,256]{1,0:T(8,128)} %get-tuple-element.29.refs_2_, ...), custom_call_target="tpu_custom_call" | custom-call | flops 20000000000 | bytes 5308416 | tf_op jit(solution)/shard_map/factor_part/pallas_call | solution.py:384
  91.6 16.1 %factor_part.5 = (f32[768,768]{1,0:T(8,128)S(1)}, f32[384,256]{1,0:T(8,128)S(1)}, f32[384,256]{1,0:T(8,128)S(1)}, f32[192,256]{1,0:T(8,128)S(1)}, f32[192,256]{1...) custom-call(f32[576,768]{1,0:T(8,128)S(1)} %get-tuple-element.26.refs_0_.x_ref, ...), custom_call_target="tpu_custom_call" | custom-call | flops 20000000000 | bytes 5308416 | tf_op jit(solution)/shard_map/factor_part/pallas_call | solution.py:384
  107.7 0.7 copy-done.1
  109.9 1.4 copy-done.26
  111.3 3.5 %collective-permute-start.14 = (f32[192,256]{1,0:T(8,128)S(1)}, f32[192,256]{1,0:T(8,128)S(1)}, u32[]{:S(2)}, u32[]{:S(2)}) collective-permute-start(f32[192,256]{1,0:T(8,128)S(1)} %get-tuple-element.33.refs_5_), channel_id=1, source_target_pairs={{0,30},{1,31},{2,0},{3,1},{4,2},{5,3},{6,4},{7,5},{8,6},{9,7},{10,... | collective-permute-start | bytes 589832 | tf_op jit(solution)/shard_map/ppermute | solution.py:29
  114.9 3.5 %collective-permute-start.10 = (f32[192,256]{1,0:T(8,128)S(1)}, f32[192,256]{1,0:T(8,128)S(1)}, u32[]{:S(2)}, u32[]{:S(2)}) collective-permute-start(f32[192,256]{1,0:T(8,128)S(1)} %get-tuple-element.30.refs_3_), channel_id=1, source_target_pairs={{0,30},{1,31},{2,0},{3,1},{4,2},{5,3},{6,4},{7,5},{8,6},{9,7},{10,... | collective-permute-start | bytes 589832 | tf_op jit(solution)/shard_map/ppermute | solution.py:29
  118.4 2.2 collective-permute-done.6.refs_8_
  122.3 2.9 %collective-permute-start.9 = (f32[192,256]{1,0:T(8,128)S(1)}, f32[192,256]{1,0:T(8,128)S(1)}, u32[]{:S(2)}, u32[]{:S(2)}) collective-permute-start(f32[192,256]{1,0:T(8,128)S(1)} %get-tuple-element.41), channel_id=1, source_target_pairs={{0,2},{1,3},{2,4},{3,5},{4,6},{5,7},{6,8},{7,9},{8,10},{9,11},{10,... | collective-permute-start | bytes 589832 | tf_op jit(solution)/shard_map/ppermute | solution.py:29
  125.2 3.9 %collective-permute-done.13.refs_6_.refs_18_ = f32[192,256]{1,0:T(8,128)S(1)} collective-permute-done((f32[192,256]{1,0:T(8,128)S(1)}, f32[192,256]{1,0:T(8,128)S(1)}, u32[]{:S(2)}, u32[]{:S(2)}) %collective-permute-start.13) | collective-permute-done | bytes 196640 | tf_op jit(solution)/shard_map/ppermute | solution.py:29
  130.5 5.5 %collective-permute-start.17 = (f32[192,256]{1,0:T(8,128)S(1)}, f32[192,256]{1,0:T(8,128)S(1)}, u32[]{:S(2)}, u32[]{:S(2)}) collective-permute-start(f32[192,256]{1,0:T(8,128)S(1)} %get-tuple-element.45), channel_id=1, source_target_pairs={{0,30},{1,31},{2,0},{3,1},{4,2},{5,3},{6,4},{7,5},{8,6},{9,7},{10,... | collective-permute-start | bytes 589832 | tf_op jit(solution)/shard_map/ppermute | solution.py:29
  136.0 1.6 collective-permute-done.9.refs_2_.refs_14_
  138.3 10.7 %collective-permute-start = (f32[384,768]{1,0:T(8,128)}, f32[384,768]{1,0:T(8,128)S(1)}, u32[]{:S(2)}, u32[]{:S(2)}) collective-permute-start(f32[384,768]{1,0:T(8,128)} %get-tuple-element.27), channel_id=1, source_target_pairs={{0,1},{2,3},{4,5},{6,7},{8,9},{10,11},{12,13},{14,15},{16,17},{18,... | collective-permute-start | bytes 3538952 | tf_op jit(solution)/shard_map/ppermute | solution.py:765
  149.0 1.3 collective-permute-start.2
  151.0 5.4 %collective-permute-start.12 = (f32[384,256]{1,0:T(8,128)}, f32[384,256]{1,0:T(8,128)}, u32[]{:S(2)}, u32[]{:S(2)}) collective-permute-start(f32[384,256]{1,0:T(8,128)} %get-tuple-element.40.refs_10_), channel_id=1, source_target_pairs={{0,31},{1,0},{2,1},{3,2},{4,3},{5,4},{6,5},{7,6},{8,7},{9,8},{10,9... | collective-permute-start | bytes 1179656 | tf_op jit(solution)/shard_map/ppermute | solution.py:29
  157.9 4.4 %collective-permute-start.8 = (f32[384,256]{1,0:T(8,128)}, f32[384,256]{1,0:T(8,128)}, u32[]{:S(2)}, u32[]{:S(2)}) collective-permute-start(f32[384,256]{1,0:T(8,128)} %get-tuple-element.39.refs_9_), channel_id=1, source_target_pairs={{0,31},{1,0},{2,1},{3,2},{4,3},{5,4},{6,5},{7,6},{8,7},{9,8},{10,9... | collective-permute-start | bytes 1179656 | tf_op jit(solution)/shard_map/ppermute | solution.py:29
  163.0 31.2 %collective-permute-done.12.refs_5_.refs_17_ = f32[384,256]{1,0:T(8,128)} collective-permute-done((f32[384,256]{1,0:T(8,128)}, f32[384,256]{1,0:T(8,128)}, u32[]{:S(2)}, u32[]{:S(2)}) %collective-permute-start.12) | collective-permute-done | bytes 393248 | tf_op jit(solution)/shard_map/ppermute | solution.py:29
  194.2 4.5 %collective-permute-done.7.refs_0_.refs_12_ = f32[384,256]{1,0:T(8,128)} collective-permute-done((f32[384,256]{1,0:T(8,128)}, f32[384,256]{1,0:T(8,128)}, u32[]{:S(2)}, u32[]{:S(2)}) %collective-permute-start.7) | collective-permute-done | bytes 393248 | tf_op jit(solution)/shard_map/ppermute | solution.py:29
  198.7 2.2 collective-permute-start.5
  200.9 1.7 collective-permute-done.8.refs_1_.refs_13_
  202.6 1.0 copy-done.5
  203.7 0.9 copy-done.11
  204.6 0.9 copy-done.14
  205.5 0.9 copy-done.17
  206.4 0.9 copy-done.20
  207.4 11.3 %early.1.refs_23_ = f32[4,768,768]{2,1,0:T(8,128)} custom-call(f32[576,768]{1,0:T(8,128)S(1)} %get-tuple-element.26.refs_0_.x_ref, f32[384,256]{1,0:T(8,128)} %collective-permute-done.7.refs_0_.refs_12_, f32[384,256]{1,0:T(8,128)} %collective-permute-done.8.refs_1_.refs_13_, f32[192,256]{1,0:T(8,128)S(1)} %copy-done.20, f32[192,256]{1,0:T(8,128)S(1)} %copy-done.17, ...), custom_call_target="tpu_custom_call" | custom-call | flops 8000000000 | bytes 9437184 | tf_op jit(solution)/shard_map/early/pallas_call | solution.py:457
  218.8 22.6 %collective-permute-start.3 = (f32[384,256]{1,0:T(8,128)S(1)}, f32[384,256]{1,0:T(8,128)S(1)}, u32[]{:S(2)}, u32[]{:S(2)}) collective-permute-start(f32[384,256]{1,0:T(8,128)S(1)} %copy-done.2), channel_id=1, source_target_pairs={{0,31},{1,0},{2,1},{3,2},{4,3},{5,4},{6,5},{7,6},{8,7},{9,8},{10,9... | collective-permute-start | bytes 1179656 | tf_op jit(solution)/shard_map/ppermute | solution.py:29
  241.5 21.2 %middle.1 = (f32[3,768,768]{2,1,0:T(8,128)}, f32[4,768,768]{2,1,0:T(8,128)}) custom-call(s32[5]{0:T(128)S(1)} %gather_fusion, f32[576,768]{1,0:T(8,128)S(1)} %get-tuple-element.26.refs_0_.x_ref, f32[1,768]{1,0:T(1,128)S(1)} %copy-done.25, f32[384,768]{1,0:T(8,128)S(1)} %collective-permute-done.refs_2_.direct_ref, ...), custom_call_target="tpu_custom_call", output_to_operand_aliasing={{1}: (24, {})} | custom-call | flops 12000000000 | bytes 16515072 | tf_op jit(solution)/shard_map/middle/pallas_call | solution.py:625
  262.7 8.4 %late.1 = (f32[3,768,768]{2,1,0:T(8,128)}, f32[4,768,768]{2,1,0:T(8,128)}) custom-call(s32[5]{0:T(128)S(1)} %gather_fusion, f32[576,768]{1,0:T(8,128)S(1)} %get-tuple-element.26.refs_0_.x_ref, f32[384,768]{1,0:T(8,128)S(1)} %collective-permute-done.refs_2_.direct_ref, ...), custom_call_target="tpu_custom_call", output_to_operand_aliasing={{0}: (5, {}), {1}: (6, {})} | custom-call | flops 4000000000 | bytes 9437184 | tf_op jit(solution)/shard_map/late/pallas_call | solution.py:715
  (74 shorter events, 8.8 us)
Async XLA Ops:
  0.6 161.7 %copy-start = (s32[32]{0:T(128)S(1)}, s32[32]{0:T(128)}, u32[]{:S(2)}) copy-start(s32[32]{0:T(128)} %param.8) | copy-start | bytes 388
  4.8 53.1 %copy-start.25 = (f32[1,768]{1,0:T(1,128)S(1)}, f32[1,768]{1,0:T(1,128)}, u32[]{:S(2)}) copy-start(f32[1,768]{1,0:T(1,128)} %refs_1_.3) | copy-start | bytes 9220
  57.1 91.8 %collective-permute-start.1 = (f32[384,768]{1,0:T(8,128)}, f32[384,768]{1,0:T(8,128)}, u32[]{:S(2)}, u32[]{:S(2)}) collective-permute-start(f32[384,768]{1,0:T(8,128)} %get-tuple-element.27), channel_id=1, source_target_pairs={{0,2},{1,3},{2,4},{3,5},{4,6},{5,7},{6,8},{7,9},{8,10},{9,11},{10,... | collective-permute-start | bytes 3538952 | tf_op jit(solution)/shard_map/ppermute | solution.py:29
  91.6 70.8 %copy-start.28 = (s32[5]{0:T(128)S(1)}, s32[5]{0:T(128)}, u32[]{:S(2)}) copy-start(s32[5]{0:T(128)} %constant.29.clone) | copy-start | bytes 64
  109.9 1.4 copy-start.26
  111.3 9.3 %collective-permute-start.6 = (f32[192,192]{1,0:T(8,128)S(1)}, f32[192,192]{1,0:T(8,128)S(1)}, u32[]{:S(2)}, u32[]{:S(2)}) collective-permute-start(f32[192,192]{1,0:T(8,128)S(1)} %get-tuple-element.38), channel_id=1, source_target_pairs={{0,2},{1,3},{2,4},{3,5},{4,6},{5,7},{6,8},{7,9},{8,10},{9,11},{10,... | collective-permute-start | bytes 442376 | tf_op jit(solution)/shard_map/ppermute | solution.py:29
  111.3 10.3 %collective-permute-start.14 = (f32[192,256]{1,0:T(8,128)S(1)}, f32[192,256]{1,0:T(8,128)S(1)}, u32[]{:S(2)}, u32[]{:S(2)}) collective-permute-start(f32[192,256]{1,0:T(8,128)S(1)} %get-tuple-element.33.refs_5_), channel_id=1, source_target_pairs={{0,30},{1,31},{2,0},{3,1},{4,2},{5,3},{6,4},{7,5},{8,6},{9,7},{10,... | collective-permute-start | bytes 589832 | tf_op jit(solution)/shard_map/ppermute | solution.py:29
  114.9 14.3 %collective-permute-start.13 = (f32[192,256]{1,0:T(8,128)S(1)}, f32[192,256]{1,0:T(8,128)S(1)}, u32[]{:S(2)}, u32[]{:S(2)}) collective-permute-start(f32[192,256]{1,0:T(8,128)S(1)} %get-tuple-element.42), channel_id=1, source_target_pairs={{0,2},{1,3},{2,4},{3,5},{4,6},{5,7},{6,8},{7,9},{8,10},{9,11},{10,... | collective-permute-start | bytes 589832 | tf_op jit(solution)/shard_map/ppermute | solution.py:29
  114.9 15.0 %collective-permute-start.10 = (f32[192,256]{1,0:T(8,128)S(1)}, f32[192,256]{1,0:T(8,128)S(1)}, u32[]{:S(2)}, u32[]{:S(2)}) collective-permute-start(f32[192,256]{1,0:T(8,128)S(1)} %get-tuple-element.30.refs_3_), channel_id=1, source_target_pairs={{0,30},{1,31},{2,0},{3,1},{4,2},{5,3},{6,4},{7,5},{8,6},{9,7},{10,... | collective-permute-start | bytes 589832 | tf_op jit(solution)/shard_map/ppermute | solution.py:29
  121.3 35.8 %collective-permute-start.11 = (f32[384,256]{1,0:T(8,128)S(1)}, f32[384,256]{1,0:T(8,128)S(1)}, u32[]{:S(2)}, u32[]{:S(2)}) collective-permute-start(f32[384,256]{1,0:T(8,128)S(1)} %get-tuple-element.32.refs_4_), channel_id=1, source_target_pairs={{0,1},{1,2},{2,3},{3,4},{4,5},{5,6},{6,7},{7,8},{8,9},{9,10},{10,1... | collective-permute-start | bytes 1179656 | tf_op jit(solution)/shard_map/ppermute | solution.py:29
  122.3 15.3 %collective-permute-start.9 = (f32[192,256]{1,0:T(8,128)S(1)}, f32[192,256]{1,0:T(8,128)S(1)}, u32[]{:S(2)}, u32[]{:S(2)}) collective-permute-start(f32[192,256]{1,0:T(8,128)S(1)} %get-tuple-element.41), channel_id=1, source_target_pairs={{0,2},{1,3},{2,4},{3,5},{4,6},{5,7},{6,8},{7,9},{8,10},{9,11},{10,... | collective-permute-start | bytes 589832 | tf_op jit(solution)/shard_map/ppermute | solution.py:29
  129.8 20.4 %collective-permute-start.16 = (f32[192,256]{1,0:T(8,128)S(1)}, f32[192,256]{1,0:T(8,128)S(1)}, u32[]{:S(2)}, u32[]{:S(2)}) collective-permute-start(f32[192,256]{1,0:T(8,128)S(1)} %get-tuple-element.44), channel_id=1, source_target_pairs={{0,2},{1,3},{2,4},{3,5},{4,6},{5,7},{6,8},{7,9},{8,10},{9,11},{10,... | collective-permute-start | bytes 589832 | tf_op jit(solution)/shard_map/ppermute | solution.py:29
  130.5 25.9 %collective-permute-start.17 = (f32[192,256]{1,0:T(8,128)S(1)}, f32[192,256]{1,0:T(8,128)S(1)}, u32[]{:S(2)}, u32[]{:S(2)}) collective-permute-start(f32[192,256]{1,0:T(8,128)S(1)} %get-tuple-element.45), channel_id=1, source_target_pairs={{0,30},{1,31},{2,0},{3,1},{4,2},{5,3},{6,4},{7,5},{8,6},{9,7},{10,... | collective-permute-start | bytes 589832 | tf_op jit(solution)/shard_map/ppermute | solution.py:29
  138.3 103.1 %collective-permute-start = (f32[384,768]{1,0:T(8,128)}, f32[384,768]{1,0:T(8,128)S(1)}, u32[]{:S(2)}, u32[]{:S(2)}) collective-permute-start(f32[384,768]{1,0:T(8,128)} %get-tuple-element.27), channel_id=1, source_target_pairs={{0,1},{2,3},{4,5},{6,7},{8,9},{10,11},{12,13},{14,15},{16,17},{18,... | collective-permute-start | bytes 3538952 | tf_op jit(solution)/shard_map/ppermute | solution.py:765
  149.0 92.4 %collective-permute-start.2 = (f32[384,768]{1,0:T(8,128)}, f32[384,768]{1,0:T(8,128)}, u32[]{:S(2)}, u32[]{:S(2)}) collective-permute-start(f32[384,768]{1,0:T(8,128)} %collective-permute-done.1.refs_4_), channel_id=1, source_target_pairs={{1,0},{3,2},{5,4},{7,6},{9,8},{11,10},{13,12},{15,14},{17,16},{19,... | collective-permute-start | bytes 3538952 | tf_op jit(solution)/shard_map/ppermute | solution.py:779
  151.0 43.2 %collective-permute-start.12 = (f32[384,256]{1,0:T(8,128)}, f32[384,256]{1,0:T(8,128)}, u32[]{:S(2)}, u32[]{:S(2)}) collective-permute-start(f32[384,256]{1,0:T(8,128)} %get-tuple-element.40.refs_10_), channel_id=1, source_target_pairs={{0,31},{1,0},{2,1},{3,2},{4,3},{5,4},{6,5},{7,6},{8,7},{9,8},{10,9... | collective-permute-start | bytes 1179656 | tf_op jit(solution)/shard_map/ppermute | solution.py:29
  157.1 41.6 %collective-permute-start.7 = (f32[384,256]{1,0:T(8,128)}, f32[384,256]{1,0:T(8,128)}, u32[]{:S(2)}, u32[]{:S(2)}) collective-permute-start(f32[384,256]{1,0:T(8,128)} %get-tuple-element.29.refs_2_), channel_id=1, source_target_pairs={{0,1},{1,2},{2,3},{3,4},{4,5},{5,6},{6,7},{7,8},{8,9},{9,10},{10,1... | collective-permute-start | bytes 1179656 | tf_op jit(solution)/shard_map/ppermute | solution.py:29
  157.9 44.7 %collective-permute-start.8 = (f32[384,256]{1,0:T(8,128)}, f32[384,256]{1,0:T(8,128)}, u32[]{:S(2)}, u32[]{:S(2)}) collective-permute-start(f32[384,256]{1,0:T(8,128)} %get-tuple-element.39.refs_9_), channel_id=1, source_target_pairs={{0,31},{1,0},{2,1},{3,2},{4,3},{5,4},{6,5},{7,6},{8,7},{9,8},{10,9... | collective-permute-start | bytes 1179656 | tf_op jit(solution)/shard_map/ppermute | solution.py:29
  194.2 47.2 %collective-permute-start.15 = (f32[384,256]{1,0:T(8,128)}, f32[384,256]{1,0:T(8,128)S(1)}, u32[]{:S(2)}, u32[]{:S(2)}) collective-permute-start(f32[384,256]{1,0:T(8,128)} %copy-done.3), channel_id=1, source_target_pairs={{0,1},{1,2},{2,3},{3,4},{4,5},{5,6},{6,7},{7,8},{8,9},{9,10},{10,1... | collective-permute-start | bytes 1179656 | tf_op jit(solution)/shard_map/ppermute | solution.py:29
  198.7 20.0 %collective-permute-start.5 = (f32[192,384]{1,0:T(8,128)}, f32[192,384]{1,0:T(8,128)S(1)}, u32[]{:S(2)}, u32[]{:S(2)}) collective-permute-start(f32[192,384]{1,0:T(8,128)} %copy-done.7), channel_id=1, source_target_pairs={{0,1},{1,2},{2,3},{3,4},{4,5},{5,6},{6,7},{7,8},{8,9},{9,10},{10,1... | collective-permute-start | bytes 884744 | tf_op jit(solution)/shard_map/ppermute | solution.py:29
  202.6 16.1 %copy-start.2 = (f32[384,256]{1,0:T(8,128)S(1)}, f32[384,256]{1,0:T(8,128)}, u32[]{:S(2)}) copy-start(f32[384,256]{1,0:T(8,128)} %copy-done.1) | copy-start | bytes 1179652
  202.6 38.8 %collective-permute-start.4 = (f32[192,768]{1,0:T(8,128)S(1)}, f32[192,768]{1,0:T(8,128)S(1)}, u32[]{:S(2)}, u32[]{:S(2)}) collective-permute-start(f32[192,768]{1,0:T(8,128)S(1)} %get-tuple-element.35), channel_id=1, source_target_pairs={{0,1},{1,2},{2,3},{3,4},{4,5},{5,6},{6,7},{7,8},{8,9},{9,10},{10,1... | collective-permute-start | bytes 1769480 | tf_op jit(solution)/shard_map/ppermute | solution.py:29
  202.6 1.0 copy-start.5
  207.4 34.0 %copy-start.6 = (f32[384,256]{1,0:T(8,128)S(1)}, f32[384,256]{1,0:T(8,128)}, u32[]{:S(2)}) copy-start(f32[384,256]{1,0:T(8,128)} %copy-done.4) | copy-start | bytes 1179652
  207.4 34.0 %copy-start.9 = (f32[192,192]{1,0:T(8,128)S(1)}, f32[192,192]{1,0:T(8,128)}, u32[]{:S(2)}) copy-start(f32[192,192]{1,0:T(8,128)} %copy-done.8) | copy-start | bytes 442372
  207.4 34.1 %copy-start.12 = (f32[192,256]{1,0:T(8,128)S(1)}, f32[192,256]{1,0:T(8,128)}, u32[]{:S(2)}) copy-start(f32[192,256]{1,0:T(8,128)} %copy-done.10) | copy-start | bytes 589828
  207.4 34.1 %copy-start.15 = (f32[192,256]{1,0:T(8,128)S(1)}, f32[192,256]{1,0:T(8,128)}, u32[]{:S(2)}) copy-start(f32[192,256]{1,0:T(8,128)} %copy-done.13) | copy-start | bytes 589828
  207.4 34.1 %copy-start.18 = (f32[192,256]{1,0:T(8,128)S(1)}, f32[192,256]{1,0:T(8,128)}, u32[]{:S(2)}) copy-start(f32[192,256]{1,0:T(8,128)} %copy-done.16) | copy-start | bytes 589828
  207.4 34.1 %copy-start.22 = (f32[192,256]{1,0:T(8,128)S(1)}, f32[192,256]{1,0:T(8,128)}, u32[]{:S(2)}) copy-start(f32[192,256]{1,0:T(8,128)} %copy-done.21) | copy-start | bytes 589828
  207.4 34.1 %copy-start.24 = (f32[192,256]{1,0:T(8,128)S(1)}, f32[192,256]{1,0:T(8,128)}, u32[]{:S(2)}) copy-start(f32[192,256]{1,0:T(8,128)} %copy-done.23) | copy-start | bytes 589828
  207.4 34.1 %copy-start.27 = (f32[768,768]{1,0:T(8,128)S(1)}, f32[768,768]{1,0:T(8,128)}, u32[]{:S(2)}) copy-start(f32[768,768]{1,0:T(8,128)} %copy-done.26) | copy-start | bytes 7077892
  218.8 43.9 %collective-permute-start.3 = (f32[384,256]{1,0:T(8,128)S(1)}, f32[384,256]{1,0:T(8,128)S(1)}, u32[]{:S(2)}, u32[]{:S(2)}) collective-permute-start(f32[384,256]{1,0:T(8,128)S(1)} %copy-done.2), channel_id=1, source_target_pairs={{0,31},{1,0},{2,1},{3,2},{4,3},{5,4},{6,5},{7,6},{8,7},{9,8},{10,9... | collective-permute-start | bytes 1179656 | tf_op jit(solution)/shard_map/ppermute | solution.py:29
  (15 other events, 11.5 us)

commit v3 on v0

--- a/solution.py
+++ b/solution.py
@@ -399,11 +399,15 @@
     return product_of_halves(halves(left), halves(right), dims)
 
 
-def put_coupling(side, start, y_refs, x_ref, buffer_ref, left_refs, out_ref, sems):
+COUPLINGS = ((3, 0, 1), (1, 0, 2), (0, 1, 3), (2, 2, 3))
+
+
+def put_coupling(side, start, y_refs, x_ref, buffer_ref, left_refs, out_ref, sems, places=range(4)):
     rows = buffer_ref.shape[1]
     width = x_ref.shape[1]
     copies = []
-    for place, (number, begin, end) in enumerate(((3, 0, 1), (1, 0, 2), (0, 1, 3), (2, 2, 3))):
+    for place in places:
+        number, begin, end = COUPLINGS[place]
         keep_halves(left_refs, y_refs[number][...].T)
 
         def put(lanes, value, place=place):
@@ -469,7 +473,7 @@
     )(x, *[piece for part in parts for piece in part])
 
 
-def late_kernel(side, starts, flags_ref, *refs):
+def base_kernel(side, cut, flags_ref, *refs):
     (
         x_ref,
         shift_ref,
@@ -481,17 +485,14 @@
         gram_one_ref,
         gram_two_ref,
     ) = refs[:9]
-    parts = len(starts)
     refs = refs[9:]
-    mine, refs = refs[:parts], refs[parts:]
-    pieces, refs = [refs[4 * k : 4 * k + 4] for k in range(parts)], refs[4 * parts :]
-    lasts = pieces[-1]
-    partial_ref, schur_ref, coupling_ref = refs[:3]
-    buffer_ref, tile_ref, rest_ref, near_ref, far_ref, high_ref, less_ref, sems, outs = refs[3:]
+    mine, refs = refs[:PARTS], refs[PARTS:]
+    pieces, refs = [refs[4 * k : 4 * k + 4] for k in range(PARTS - 1)], refs[4 * PARTS - 4 :]
+    partial_ref, schur_ref = refs[:2]
+    tile_ref, rest_ref, near_ref, far_ref, high_ref, less_ref, outs = refs[2:]
     left_refs = (high_ref, less_ref)
     width = x_ref.shape[1]
-    cut = starts[-1]
-    copies = put_coupling(side, cut, lasts, x_ref, buffer_ref, left_refs, coupling_ref, sems)
+    copies = []
     own, above, second_above, under, second_under = [flags_ref[k] > 0 for k in range(5)]
     one, two, three = slice(0, side), slice(side, 2 * side), slice(2 * side, 3 * side)
     pair, tail = slice(0, 2 * side), slice(side, 3 * side)
@@ -501,10 +502,12 @@
 
     @pl.when(own)
     def _():
-        for start, ref in zip(starts, mine):
+        start = 0
+        for ref in mine:
             lanes = slice(start, start + ref.shape[1])
             near_ref[pair, lanes] = ref[...]
             far_ref[one, lanes] = ref[side:, :]
+            start += ref.shape[1]
 
     @pl.when(jnp.logical_not(own))
     def _():
@@ -564,7 +567,7 @@
             outs.at[place],
         )
         copy.start()
-        tile_ref[place, cut:, :] = buffer_ref[member]
+        tile_ref[place, cut:, :] = jnp.zeros((width - cut, width), jnp.float32)
         copy.wait()
 
     @pl.when(own)
@@ -608,36 +611,161 @@
         copy.wait()
 
 
-def late(flags, x, shift, received, low, grams, mine, parts, partial, starts, side):
+def base(flags, x, shift, received, low, grams, mine, parts, partial, cut, side):
     depth, width = x.shape
-    rest = parts[-1][0].shape[1]
     inputs = [x, shift, *received, low, *grams, *mine] + [piece for part in parts for piece in part]
     return pl.pallas_call(
-        functools.partial(late_kernel, side, starts),
-        out_shape=(
-            jax.ShapeDtypeStruct((3, width, width), jnp.float32),
-            jax.ShapeDtypeStruct((4, width, width), jnp.float32),
-        ),
+        functools.partial(base_kernel, side, cut),
+        out_shape=jax.ShapeDtypeStruct((3, width, width), jnp.float32),
         in_specs=[SMEM_SPEC] + [VMEM_SPEC] * len(inputs) + [ANY_SPEC],
-        out_specs=(ANY_SPEC, ANY_SPEC),
-        input_output_aliases={1 + len(inputs): 1},
+        out_specs=ANY_SPEC,
         scratch_shapes=[
-            pltpu.VMEM((4, rest, width), jnp.float32),
             pltpu.VMEM((3, width, width), jnp.float32),
             pltpu.VMEM((depth, width), jnp.float32),
             pltpu.VMEM((depth, width), jnp.float32),
             pltpu.VMEM((2 * side, width), jnp.float32),
             pltpu.VMEM((width, depth), jnp.bfloat16),
             pltpu.VMEM((width, depth), jnp.bfloat16),
-            pltpu.SemaphoreType.DMA((4,)),
             pltpu.SemaphoreType.DMA((3,)),
         ],
-        compiler_params=pltpu.CompilerParams(vmem_limit_bytes=40 << 20),
+        compiler_params=pltpu.CompilerParams(vmem_limit_bytes=36 << 20),
         cost_estimate=pl.CostEstimate(
             flops=12_000_000_000, bytes_accessed=7 * width * width * 4, transcendentals=0
         ),
+        name="base",
+    )(flags, *inputs, partial)
+
+
+def late_kernel(side, flags_ref, x_ref, direct_ref, onward_ref, second_ref, *refs):
+    y_refs, refs = refs[:4], refs[4:]
+    tiles_ref, _, schur_ref, coupling_ref = refs[:4]
+    buffer_ref, tile_ref, high_ref, less_ref, small_ref, sems, ins, outs, edges = refs[4:]
+    left_refs = (high_ref, less_ref)
+    rows, width = buffer_ref.shape[1:]
+    above, second_above, under, second_under = [flags_ref[k] > 0 for k in range(1, 5)]
+    beside = jnp.logical_or(above, second_under)
+    touched = jnp.logical_or(jnp.logical_or(beside, under), second_above)
+
+    def taken(place, slot):
+        return pltpu.make_async_copy(tiles_ref.at[place], tile_ref.at[slot], ins.at[slot])
+
+    def given(place, slot):
+        return pltpu.make_async_copy(tile_ref.at[slot], schur_ref.at[place], outs.at[slot])
+
+    moves = ((touched, 2, 0), (beside, 1, 1), (under, 0, 1))
+    for wanted, place, slot in moves:
+
+        @pl.when(wanted)
+        def _(place=place, slot=slot):
+            taken(place, slot).start()
+
+    copies = put_coupling(
+        side, width - rows, y_refs, x_ref, buffer_ref, left_refs, coupling_ref, sems, (0, 3, 2, 1)
+    )
+
+    def edge(place, member):
+        return pltpu.make_async_copy(
+            buffer_ref.at[member], schur_ref.at[place, pl.ds(width - rows, rows), :], edges.at[place]
+        )
+
+    replaced = ((under, 1, 2), (second_under, 0, 3))
+    for wanted, place, member in replaced:
+
+        @pl.when(wanted)
+        def _(place=place, member=member):
+            edge(place, member).start()
+
+    for wanted, place, slot in moves:
+
+        @pl.when(wanted)
+        def _(place=place, slot=slot):
+            taken(place, slot).wait()
+
+    def take_off(slot, depth, right_at):
+        def put(lanes, value):
+            tile_ref[slot, :, lanes] = tile_ref[slot, :, lanes] - value
+
+        tall_product(left_refs, width, depth, right_at, put, width)
+
+    for wanted, place in ((second_above, 0), (above, 1), (under, 2), (second_under, 3)):
+
+        @pl.when(wanted)
+        def _(place=place):
+            keep_halves(left_refs, buffer_ref[place].T)
+            take_off(0, rows, lambda lanes: buffer_ref[place, :, lanes])
+
+    def put_small(lanes, value):
+        small_ref[:, lanes] = value
+
+    pair_sum = ((above, 1, y_refs[1], 1, 0), (second_under, 3, y_refs[2], 0, 1))
+    for wanted, place, y_ref, row, piece in pair_sum + ((under, 2, y_refs[0], 1, None),):
+
+        @pl.when(wanted)
+        def _(place=place, y_ref=y_ref, row=row, piece=piece):
+            keep_halves(left_refs, y_ref[row * side : (row + 1) * side, :])
+            tall_product(
+                left_refs, side, rows, lambda lanes: buffer_ref[place, :, lanes], put_small, width
+            )
+            if piece is None:
+                left = second_ref[:side, :]
+            else:
+                picked = slice(piece * side, (piece + 1) * side)
+                left = direct_ref[picked, :] + onward_ref[picked, :]
+            keep_halves(left_refs, left.T)
+            take_off(1, side, lambda lanes: small_ref[:, lanes])
+
+    for wanted, place, slot in moves:
+
+        @pl.when(wanted)
+        def _(place=place, slot=slot):
+            given(place, slot).start()
+
+    for wanted, place, slot in moves:
+
+        @pl.when(wanted)
+        def _(place=place, slot=slot):
+            given(place, slot).wait()
+
+    for wanted, place, member in replaced:
+
+        @pl.when(wanted)
+        def _(place=place, member=member):
+            edge(place, member).wait()
+
+    for copy in copies:
+        copy.wait()
+
+
+def late(flags, x, direct, onward, second, pieces, tiles, coupling, side):
+    _, width = x.shape
+    rows = pieces[0].shape[1]
+    most = max(2 * side, rows)
+    return pl.pallas_call(
+        functools.partial(late_kernel, side),
+        out_shape=(
+            jax.ShapeDtypeStruct((3, width, width), jnp.float32),
+            jax.ShapeDtypeStruct((4, width, width), jnp.float32),
+        ),
+        in_specs=[SMEM_SPEC] + [VMEM_SPEC] * 8 + [ANY_SPEC] * 2,
+        out_specs=(ANY_SPEC, ANY_SPEC),
+        input_output_aliases={9: 0, 10: 1},
+        scratch_shapes=[
+            pltpu.VMEM((4, rows, width), jnp.float32),
+            pltpu.VMEM((2, width, width), jnp.float32),
+            pltpu.VMEM((width, most), jnp.bfloat16),
+            pltpu.VMEM((width, most), jnp.bfloat16),
+            pltpu.VMEM((side, width), jnp.float32),
+            pltpu.SemaphoreType.DMA((4,)),
+            pltpu.SemaphoreType.DMA((2,)),
+            pltpu.SemaphoreType.DMA((2,)),
+            pltpu.SemaphoreType.DMA((2,)),
+        ],
+        compiler_params=pltpu.CompilerParams(vmem_limit_bytes=24 << 20),
+        cost_estimate=pl.CostEstimate(
+            flops=4_000_000_000, bytes_accessed=4 * width * width * 4, transcendentals=0
+        ),
         name="late",
-    )(flags, *inputs, partial)
+    )(flags, x, direct, onward, second, *pieces, tiles, coupling)
 
 
 def local(weighted_jacobian_strips, leading_pose_index, levenberg_shift, removal_flags):
@@ -646,8 +774,8 @@
     surfels, _, width = weighted_jacobian_strips.shape
     capacity = max(2, (3 * surfels + 2 * count - 1) // (2 * count))
     side = count * capacity
-    tiles = width // TILE
-    bounds = tuple(tiles * k // PARTS for k in range(PARTS + 1))
+    count_tiles = width // TILE
+    bounds = tuple(count_tiles * k // PARTS for k in range(PARTS + 1))
     starts = tuple(bound * TILE for bound in bounds[:-1])
     flags = removal_flags[(own + jnp.array((0, 1, 2, -1, -2), jnp.int32)) % count]
 
@@ -673,18 +801,18 @@
     low, *part = solved(0, levenberg_shift, ())
     known = [part]
     parts = [sent_parts(part)]
+    onward = lax.ppermute(second, AXES, [(k + 1, k) for k in range(0, count, 2)])
+    extra = passed_along(last, 1)
     for number in range(1, PARTS - 1):
         low, *part = solved(number, low, known)
         known.append(part)
         parts.append(sent_parts(part))
-    onward = lax.ppermute(second, AXES, [(k + 1, k) for k in range(0, count, 2)])
-    extra = passed_along(last, 1)
     low, *part, gram_one, gram_two = solved(PARTS - 1, low, known)
     known.append(part)
     parts.append(sent_parts(part))
     grams = (passed_along(gram_one, 1), passed_along(gram_two, 2))
     partial = early(x, parts[:-1], starts[:-1], side)
-    schur, coupling = late(
+    tiles = base(
         flags,
         x,
         levenberg_shift,
@@ -692,11 +820,12 @@
         low,
         grams,
         [part[1] for part in known],
-        parts,
+        parts[:-1],
         partial,
-        starts,
+        starts[-1],
         side,
     )
+    schur, coupling = late(flags, x, direct, onward, second, parts[-1], tiles, partial, side)
     return schur[None], coupling[None]
 
 

time: 268 us -> 226 us (0.84)
  blocking collectives: 51.7 us -> 0 us
  waiting for transfers between devices: 67.3 us -> 80.4 us
  local copies, waits for them, and re-layouts: 14.6 us -> 8.77 us
  Pallas kernels: 89 us -> 94.6 us
  starting transfers between devices: 41.9 us -> 37.3 us
    all_to_all x1 -> x0, blocking collectives: 51.7 us -> none  [local(): lax.all_to_all(chunks, AXES, split_axis=0, concat_axis=0, tiled=True)]
    all_to_all x0 -> x1, waiting for transfers between devices: none -> 44.3 us  [local(): lax.all_to_all(chunks, AXES, split_axis=0, concat_axis=0, tiled=True)]
    ppermute x16, waiting for transfers between devices: 67.3 us -> 25.6 us  [passed_along(): return lax.ppermute(value, AXES, pairs)]
    ppermute x16, starting transfers between devices: 37.1 us -> 25.8 us  [passed_along(): return lax.ppermute(value, AXES, pairs)]
    ppermute x1, waiting for transfers between devices: 0.01 us -> 10.5 us  [local(): lax.ppermute(second, AXES, [(k + 1, k) for k in range(0, count, 2)])]
    all_to_all x0 -> x1, starting transfers between devices: none -> 7.32 us  [local(): lax.all_to_all(chunks, AXES, split_axis=0, concat_axis=0, tiled=True)]
    pallas_call x1 -> x2, Pallas kernels: 21.4 us -> 28.8 us  [the longest x1 15.4 us: base(): pl.pallas_call(functools.partial(base_kernel, side, cut), out_shape=jax.S...]
    unnamed x66 -> x40, local copies, waits for them, and re-layouts: 14 us -> 8.13 us
  transfers between devices with their start and end apart: 18 -> 19, of which waited for: 6 -> 7; matrix products, arithmetic and copies ran while one was open for 0% -> 0% of each run, Pallas kernels for 23% -> 35%
where the time goes in v3:
time: 226 us; the launch traced here: 222 us
  Pallas kernels  94.6 us (42%)
  waiting for transfers between devices  80.4 us (36%)
  starting transfers between devices  37.3 us (17%)
  local copies, waits for them, and re-layouts  8.77 us (4%)
    pallas_call x3, Pallas kernels, factored_part(): pl.pallas_call(functools.partial(part_kernel, side, bounds, number), out_...  50.3 us
    all_to_all x1, waiting for transfers between devices, local(): lax.all_to_all(chunks, AXES, split_axis=0, concat_axis=0, tiled=True)  44.3 us
    ppermute x16, starting transfers between devices, passed_along(): return lax.ppermute(value, AXES, pairs)  25.8 us
    ppermute x16, waiting for transfers between devices, passed_along(): return lax.ppermute(value, AXES, pairs)  25.6 us
    pallas_call x1, Pallas kernels, base(): pl.pallas_call(functools.partial(base_kernel, side, cut), out_shape=jax.S...  15.4 us
    pallas_call x1, Pallas kernels, late(): pl.pallas_call(functools.partial(late_kernel, side), out_shape=(jax.Shape...  13.4 us
    pallas_call x1, Pallas kernels, early(): pl.pallas_call(functools.partial(early_kernel, side, starts), out_shape=j...  11 us
    ppermute x1, waiting for transfers between devices, local(): lax.ppermute(second, AXES, [(k + 1, k) for k in range(0, count, 2)])  10.5 us
  transfers between devices with their start and end apart: 19, of which 7 were waited for; matrix products, arithmetic and copies ran while one was open for 0% of the time, Pallas kernels for 35%

profile of v3, /device:TPU:0, one launch (start us, length us, event | category | flops | bytes accessed | tf_op | source)
XLA Modules:
  0.0 222.2 jit_solution(5090090000032504126)
XLA Ops:
  0.6 4.1 %bucket.1 = f32[32,54,256]{2,1,0:T(8,128)} custom-call(s32[1,128]{1,0:T(1,128)} %bitcast.7, f32[3,128,768]{2,1,0:T(8,128)} %bitcast.6), custom_call_target="tpu_custom_call" | custom-call | tf_op jit(solution)/shard_map/bucket/pallas_call | solution.py:85
  4.8 7.3 %all-to-all-start = ((f32[32,54,256]{2,1,0:T(8,128)}), f32[32,54,256]{2,1,0:T(8,128)S(1)}, u32[]{:S(2)}, u32[]{:S(2)}) async-start(f32[32,54,256]{2,1,0:T(8,128)} %bucket.1), calls=%async_computation | async-start | bytes 3670016 | tf_op jit(solution)/shard_map/all_to_all | solution.py:788
  12.1 44.3 %all-to-all-done.in_ref = f32[32,54,256]{2,1,0:T(8,128)S(1)} async-done(((f32[32,54,256]{2,1,0:T(8,128)}), f32[32,54,256]{2,1,0:T(8,128)S(1)}, u32[]{:S(2)}, u32[]{:S(2)}) %all-to-all-start) | async-done | bytes 1769504 | tf_op jit(solution)/shard_map/all_to_all | solution.py:788
  56.9 0.8 copy-done.4
  57.7 18.1 %factor_part.3 = (f32[768,768]{1,0:T(8,128)S(1)}, f32[384,256]{1,0:T(8,128)S(1)}, f32[384,256]{1,0:T(8,128)S(1)}, f32[192,256]{1,0:T(8,128)S(1)}, f32[192,256]{1,0:T(8,128)}) custom-call(f32[576,768]{1,0:T(8,128)S(1)} %get-tuple-element.24.refs_0_.x_ref, f32[1,768]{1,0:T(1,128)S(1)} %copy-done.16), custom_call_target="tpu_custom_call" | custom-call | flops 20000000000 | bytes 5308416 | tf_op jit(solution)/shard_map/factor_part/pallas_call | solution.py:384
  75.8 4.4 %collective-permute-start.13 = (f32[192,256]{1,0:T(8,128)}, f32[192,256]{1,0:T(8,128)}, u32[]{:S(2)}, u32[]{:S(2)}) collective-permute-start(f32[192,256]{1,0:T(8,128)} %get-tuple-element.28.refs_3_), channel_id=1, source_target_pairs={{0,30},{1,31},{2,0},{3,1},{4,2},{5,3},{6,4},{7,5},{8,6},{9,7},{10,... | collective-permute-start | bytes 589832 | tf_op jit(solution)/shard_map/ppermute | solution.py:29
  80.2 1.3 collective-permute-start.11
  81.6 16.0 %factor_part.4 = (f32[768,768]{1,0:T(8,128)S(1)}, f32[384,256]{1,0:T(8,128)S(1)}, f32[384,256]{1,0:T(8,128)S(1)}, f32[192,256]{1,0:T(8,128)}, f32[192,256]{1,0:T(8,128)}) custom-call(f32[576,768]{1,0:T(8,128)S(1)} %get-tuple-element.24.refs_0_.x_ref, f32[768,768]{1,0:T(8,128)S(1)} %get-tuple-element.26.refs_1_, f32[384,256]{1,0:T(8,128)S(1)} %get-tuple-element.27.refs_2_, ...), custom_call_target="tpu_custom_call" | custom-call | flops 20000000000 | bytes 5308416 | tf_op jit(solution)/shard_map/factor_part/pallas_call | solution.py:384
  97.6 1.4 copy-done.17
  99.6 3.9 %collective-permute-start.17 = (f32[192,256]{1,0:T(8,128)}, f32[192,256]{1,0:T(8,128)}, u32[]{:S(2)}, u32[]{:S(2)}) collective-permute-start(f32[192,256]{1,0:T(8,128)} %get-tuple-element.31.refs_5_), channel_id=1, source_target_pairs={{0,30},{1,31},{2,0},{3,1},{4,2},{5,3},{6,4},{7,5},{8,6},{9,7},{10,... | collective-permute-start | bytes 589832 | tf_op jit(solution)/shard_map/ppermute | solution.py:29
  104.2 2.7 %collective-permute-start = (f32[384,768]{1,0:T(8,128)S(1)}, f32[384,768]{1,0:T(8,128)S(1)}, u32[]{:S(2)}, u32[]{:S(2)}) collective-permute-start(f32[384,768]{1,0:T(8,128)S(1)} %get-tuple-element.25), channel_id=1, source_target_pairs={{0,1},{2,3},{4,5},{6,7},{8,9},{10,11},{12,13},{14,15},{16,17},{18,... | collective-permute-start | bytes 3538952 | tf_op jit(solution)/shard_map/ppermute | solution.py:794
  106.8 3.1 %collective-permute-done.16.refs_6_.refs_18_ = f32[192,256]{1,0:T(8,128)} collective-permute-done((f32[192,256]{1,0:T(8,128)}, f32[192,256]{1,0:T(8,128)}, u32[]{:S(2)}, u32[]{:S(2)}) %collective-permute-start.16) | collective-permute-done | bytes 196640 | tf_op jit(solution)/shard_map/ppermute | solution.py:29
  109.9 3.1 %collective-permute-done.17.refs_7_.refs_19_ = f32[192,256]{1,0:T(8,128)} collective-permute-done((f32[192,256]{1,0:T(8,128)}, f32[192,256]{1,0:T(8,128)}, u32[]{:S(2)}, u32[]{:S(2)}) %collective-permute-start.17) | collective-permute-done | bytes 196640 | tf_op jit(solution)/shard_map/ppermute | solution.py:29
  113.1 0.7 copy-done.6
  113.8 5.3 %collective-permute-start.15 = (f32[384,256]{1,0:T(8,128)}, f32[384,256]{1,0:T(8,128)S(1)}, u32[]{:S(2)}, u32[]{:S(2)}) collective-permute-start(f32[384,256]{1,0:T(8,128)} %copy-done.8), channel_id=1, source_target_pairs={{0,31},{1,0},{2,1},{3,2},{4,3},{5,4},{6,5},{7,6},{8,7},{9,8},{10,9... | collective-permute-start | bytes 1179656 | tf_op jit(solution)/shard_map/ppermute | solution.py:29
  119.1 1.5 collective-permute-start.2
  120.6 1.5 copy-done.2
  122.1 1.0 copy-done.11
  123.1 1.0 copy-done.13
  124.1 1.7 copy-done.18
  125.8 16.2 %factor_part.5 = (f32[768,768]{1,0:T(8,128)S(1)}, f32[384,256]{1,0:T(8,128)S(1)}, f32[384,256]{1,0:T(8,128)S(1)}, f32[192,256]{1,0:T(8,128)S(1)}, f32[192,256]{1...) custom-call(f32[576,768]{1,0:T(8,128)S(1)} %copy-done.2, f32[768,768]{1,0:T(8,128)S(1)} %copy-done.18, ...), custom_call_target="tpu_custom_call" | custom-call | flops 20000000000 | bytes 5308416 | tf_op jit(solution)/shard_map/factor_part/pallas_call | solution.py:384
  142.0 8.1 %collective-permute-done.10.refs_0_.refs_12_ = f32[384,256]{1,0:T(8,128)S(1)} collective-permute-done((f32[384,256]{1,0:T(8,128)}, f32[384,256]{1,0:T(8,128)S(1)}, u32[]{:S(2)}, u32[]{:S(2)}) %collective-permute-start.10) | collective-permute-done | bytes 393248 | tf_op jit(solution)/shard_map/ppermute | solution.py:29
  150.0 2.4 %collective-permute-start.7 = (f32[192,768]{1,0:T(8,128)S(1)}, f32[192,768]{1,0:T(8,128)S(1)}, u32[]{:S(2)}, u32[]{:S(2)}) collective-permute-start(f32[192,768]{1,0:T(8,128)S(1)} %copy-done.5), channel_id=1, source_target_pairs={{0,1},{1,2},{2,3},{3,4},{4,5},{5,6},{6,7},{7,8},{8,9},{9,10},{10,1... | collective-permute-start | bytes 1769480 | tf_op jit(solution)/shard_map/ppermute | solution.py:29
  152.4 6.0 %collective-permute-done.14.refs_4_.refs_16_ = f32[384,256]{1,0:T(8,128)S(1)} collective-permute-done((f32[384,256]{1,0:T(8,128)}, f32[384,256]{1,0:T(8,128)S(1)}, u32[]{:S(2)}, u32[]{:S(2)}) %collective-permute-start.14) | collective-permute-done | bytes 393248 | tf_op jit(solution)/shard_map/ppermute | solution.py:29
  158.5 2.4 %collective-permute-start.8 = (f32[192,384]{1,0:T(8,128)S(1)}, f32[192,384]{1,0:T(8,128)S(1)}, u32[]{:S(2)}, u32[]{:S(2)}) collective-permute-start(f32[192,384]{1,0:T(8,128)S(1)} %get-tuple-element.38), channel_id=1, source_target_pairs={{0,1},{1,2},{2,3},{3,4},{4,5},{5,6},{6,7},{7,8},{8,9},{9,10},{10,1... | collective-permute-start | bytes 884744 | tf_op jit(solution)/shard_map/ppermute | solution.py:29
  160.9 11.0 %early.1.refs_20_.refs_5_ = f32[4,768,768]{2,1,0:T(8,128)} custom-call(f32[576,768]{1,0:T(8,128)S(1)} %copy-done.2, f32[384,256]{1,0:T(8,128)S(1)} %collective-permute-done.10.refs_0_.refs_12_, f32[384,256]{1,0:T(8,128)S(1)} %copy-done.7, f32[192,256]{1,0:T(8,128)S(1)} %copy-done.15, f32[192,256]{1,0:T(8,128)} %collective-permute-done.13.refs_3_.refs_15_, ...), custom_call_target="tpu_custom_call" | custom-call | flops 8000000000 | bytes 9437184 | tf_op jit(solution)/shard_map/early/pallas_call | solution.py:457
  172.0 5.2 %collective-permute-done.8.refs_7_ = f32[192,384]{1,0:T(8,128)S(1)} collective-permute-done((f32[192,384]{1,0:T(8,128)S(1)}, f32[192,384]{1,0:T(8,128)S(1)}, u32[]{:S(2)}, u32[]{:S(2)}) %collective-permute-start.8) | collective-permute-done | bytes 294944 | tf_op jit(solution)/shard_map/ppermute | solution.py:29
  177.3 1.2 collective-permute-start.3
  178.5 4.1 %collective-permute-start.4 = (f32[384,256]{1,0:T(8,128)S(1)}, f32[384,256]{1,0:T(8,128)S(1)}, u32[]{:S(2)}, u32[]{:S(2)}) collective-permute-start(f32[384,256]{1,0:T(8,128)S(1)} %get-tuple-element.33.refs_11_), channel_id=1, source_target_pairs={{0,31},{1,0},{2,1},{3,2},{4,3},{5,4},{6,5},{7,6},{8,7},{9,8},{10,9... | collective-permute-start | bytes 1179656 | tf_op jit(solution)/shard_map/ppermute | solution.py:29
  182.6 10.5 %collective-permute-done.2.refs_3_.onward_ref = f32[384,768]{1,0:T(8,128)S(1)} collective-permute-done((f32[384,768]{1,0:T(8,128)S(1)}, f32[384,768]{1,0:T(8,128)S(1)}, u32[]{:S(2)}, u32[]{:S(2)}) %collective-permute-start.2) | collective-permute-done | bytes 1179680 | tf_op jit(solution)/shard_map/ppermute | solution.py:804
  193.2 15.4 %base.1.refs_4_ = f32[3,768,768]{2,1,0:T(8,128)} custom-call(s32[5]{0:T(128)S(1)} %gather_fusion, f32[576,768]{1,0:T(8,128)S(1)} %copy-done.3, f32[1,768]{1,0:T(1,128)S(1)} %copy-done.16, f32[384,768]{1,0:T(8,128)S(1)} %collective-permute-done.refs_2_.direct_ref, f32[384,768]{1,0:T(8,128)S(1)} %collective-permute-done.2.refs_3_.onward_ref, ...), custom_call_target="tpu_custom_call" | custom-call | flops 12000000000 | bytes 16515072 | tf_op jit(solution)/shard_map/base/pallas_call | solution.py:617
  208.6 13.4 %late.1 = (f32[3,768,768]{2,1,0:T(8,128)}, f32[4,768,768]{2,1,0:T(8,128)}) custom-call(s32[5]{0:T(128)S(1)} %gather_fusion, f32[576,768]{1,0:T(8,128)S(1)} %copy-done.3, f32[384,768]{1,0:T(8,128)S(1)} %collective-permute-done.refs_2_.direct_ref, ...), custom_call_target="tpu_custom_call", output_to_operand_aliasing={{0}: (9, {}), {1}: (10, {})} | custom-call | flops 4000000000 | bytes 9437184 | tf_op jit(solution)/shard_map/late/pallas_call | solution.py:743
  (57 shorter events, 1.8 us)
Async XLA Ops:
  0.6 102.9 %copy-start = (s32[32]{0:T(128)S(1)}, s32[32]{0:T(128)}, u32[]{:S(2)}) copy-start(s32[32]{0:T(128)} %param.8) | copy-start | bytes 388
  4.8 51.7 %all-to-all-start = ((f32[32,54,256]{2,1,0:T(8,128)}), f32[32,54,256]{2,1,0:T(8,128)S(1)}, u32[]{:S(2)}, u32[]{:S(2)}) async-start(f32[32,54,256]{2,1,0:T(8,128)} %bucket.1), calls=%async_computation | async-start | bytes 3670016 | tf_op jit(solution)/shard_map/all_to_all | solution.py:788
  12.1 45.6 %copy-start.16 = (f32[1,768]{1,0:T(1,128)S(1)}, f32[1,768]{1,0:T(1,128)}, u32[]{:S(2)}) copy-start(f32[1,768]{1,0:T(1,128)} %refs_1_.3) | copy-start | bytes 9220
  57.7 23.9 %copy-start.1 = (f32[576,768]{1,0:T(8,128)}, f32[576,768]{1,0:T(8,128)S(1)}, u32[]{:S(2)}) copy-start(f32[576,768]{1,0:T(8,128)S(1)} %get-tuple-element.24.refs_0_.x_ref) | copy-start | bytes 5308420
  57.7 61.5 %collective-permute-start.1 = (f32[384,768]{1,0:T(8,128)S(1)}, f32[384,768]{1,0:T(8,128)S(1)}, u32[]{:S(2)}, u32[]{:S(2)}) collective-permute-start(f32[384,768]{1,0:T(8,128)S(1)} %get-tuple-element.25), channel_id=1, source_target_pairs={{0,2},{1,3},{2,4},{3,5},{4,6},{5,7},{6,8},{7,9},{8,10},{9,11},{10,... | collective-permute-start | bytes 3538952 | tf_op jit(solution)/shard_map/ppermute | solution.py:29
  75.8 21.8 %copy-start.10 = (f32[384,256]{1,0:T(8,128)}, f32[384,256]{1,0:T(8,128)S(1)}, u32[]{:S(2)}) copy-start(f32[384,256]{1,0:T(8,128)S(1)} %get-tuple-element.27.refs_2_) | copy-start | bytes 1179652
  75.8 23.8 %collective-permute-start.12 = (f32[192,256]{1,0:T(8,128)S(1)}, f32[192,256]{1,0:T(8,128)S(1)}, u32[]{:S(2)}, u32[]{:S(2)}) collective-permute-start(f32[192,256]{1,0:T(8,128)S(1)} %get-tuple-element.42), channel_id=1, source_target_pairs={{0,2},{1,3},{2,4},{3,5},{4,6},{5,7},{6,8},{7,9},{8,10},{9,11},{10,... | collective-permute-start | bytes 589832 | tf_op jit(solution)/shard_map/ppermute | solution.py:29
  75.8 28.4 %collective-permute-start.13 = (f32[192,256]{1,0:T(8,128)}, f32[192,256]{1,0:T(8,128)}, u32[]{:S(2)}, u32[]{:S(2)}) collective-permute-start(f32[192,256]{1,0:T(8,128)} %get-tuple-element.28.refs_3_), channel_id=1, source_target_pairs={{0,30},{1,31},{2,0},{3,1},{4,2},{5,3},{6,4},{7,5},{8,6},{9,7},{10,... | collective-permute-start | bytes 589832 | tf_op jit(solution)/shard_map/ppermute | solution.py:29
  80.2 32.9 %collective-permute-start.11 = (f32[384,256]{1,0:T(8,128)S(1)}, f32[384,256]{1,0:T(8,128)S(1)}, u32[]{:S(2)}, u32[]{:S(2)}) collective-permute-start(f32[384,256]{1,0:T(8,128)S(1)} %get-tuple-element.40.refs_9_), channel_id=1, source_target_pairs={{0,31},{1,0},{2,1},{3,2},{4,3},{5,4},{6,5},{7,6},{8,7},{9,8},{10,9... | collective-permute-start | bytes 1179656 | tf_op jit(solution)/shard_map/ppermute | solution.py:29
  81.6 21.9 %copy-start.19 = (s32[5]{0:T(128)S(1)}, s32[5]{0:T(128)}, u32[]{:S(2)}) copy-start(s32[5]{0:T(128)} %constant.29.clone) | copy-start | bytes 64
  99.0 4.5 %copy-start.8 = (f32[384,256]{1,0:T(8,128)}, f32[384,256]{1,0:T(8,128)S(1)}, u32[]{:S(2)}) copy-start(f32[384,256]{1,0:T(8,128)S(1)} %get-tuple-element.41.refs_10_) | copy-start | bytes 1179652
  99.0 4.5 %copy-start.12 = (f32[384,256]{1,0:T(8,128)}, f32[384,256]{1,0:T(8,128)S(1)}, u32[]{:S(2)}) copy-start(f32[384,256]{1,0:T(8,128)S(1)} %get-tuple-element.30.refs_4_) | copy-start | bytes 1179652
  99.0 10.9 %collective-permute-start.16 = (f32[192,256]{1,0:T(8,128)}, f32[192,256]{1,0:T(8,128)}, u32[]{:S(2)}, u32[]{:S(2)}) collective-permute-start(f32[192,256]{1,0:T(8,128)} %get-tuple-element.43), channel_id=1, source_target_pairs={{0,2},{1,3},{2,4},{3,5},{4,6},{5,7},{6,8},{7,9},{8,10},{9,11},{10,... | collective-permute-start | bytes 589832 | tf_op jit(solution)/shard_map/ppermute | solution.py:29
  99.6 21.1 %copy-start.14 = (f32[192,256]{1,0:T(8,128)}, f32[192,256]{1,0:T(8,128)S(1)}, u32[]{:S(2)}) copy-start(f32[192,256]{1,0:T(8,128)S(1)} %collective-permute-done.12.refs_2_.refs_14_) | copy-start | bytes 589828
  99.6 13.5 %collective-permute-start.17 = (f32[192,256]{1,0:T(8,128)}, f32[192,256]{1,0:T(8,128)}, u32[]{:S(2)}, u32[]{:S(2)}) collective-permute-start(f32[192,256]{1,0:T(8,128)} %get-tuple-element.31.refs_5_), channel_id=1, source_target_pairs={{0,30},{1,31},{2,0},{3,1},{4,2},{5,3},{6,4},{7,5},{8,6},{9,7},{10,... | collective-permute-start | bytes 589832 | tf_op jit(solution)/shard_map/ppermute | solution.py:29
  104.2 74.4 %collective-permute-start = (f32[384,768]{1,0:T(8,128)S(1)}, f32[384,768]{1,0:T(8,128)S(1)}, u32[]{:S(2)}, u32[]{:S(2)}) collective-permute-start(f32[384,768]{1,0:T(8,128)S(1)} %get-tuple-element.25), channel_id=1, source_target_pairs={{0,1},{2,3},{4,5},{6,7},{8,9},{10,11},{12,13},{14,15},{16,17},{18,... | collective-permute-start | bytes 3538952 | tf_op jit(solution)/shard_map/ppermute | solution.py:794
  109.9 40.1 %collective-permute-start.10 = (f32[384,256]{1,0:T(8,128)}, f32[384,256]{1,0:T(8,128)S(1)}, u32[]{:S(2)}, u32[]{:S(2)}) collective-permute-start(f32[384,256]{1,0:T(8,128)} %copy-done.10), channel_id=1, source_target_pairs={{0,1},{1,2},{2,3},{3,4},{4,5},{5,6},{6,7},{7,8},{8,9},{9,10},{10,1... | collective-permute-start | bytes 1179656 | tf_op jit(solution)/shard_map/ppermute | solution.py:29
  113.1 45.4 %collective-permute-start.14 = (f32[384,256]{1,0:T(8,128)}, f32[384,256]{1,0:T(8,128)S(1)}, u32[]{:S(2)}, u32[]{:S(2)}) collective-permute-start(f32[384,256]{1,0:T(8,128)} %copy-done.12), channel_id=1, source_target_pairs={{0,1},{1,2},{2,3},{3,4},{4,5},{5,6},{6,7},{7,8},{8,9},{9,10},{10,1... | collective-permute-start | bytes 1179656 | tf_op jit(solution)/shard_map/ppermute | solution.py:29
  113.8 44.7 %collective-permute-start.15 = (f32[384,256]{1,0:T(8,128)}, f32[384,256]{1,0:T(8,128)S(1)}, u32[]{:S(2)}, u32[]{:S(2)}) collective-permute-start(f32[384,256]{1,0:T(8,128)} %copy-done.8), channel_id=1, source_target_pairs={{0,31},{1,0},{2,1},{3,2},{4,3},{5,4},{6,5},{7,6},{8,7},{9,8},{10,9... | collective-permute-start | bytes 1179656 | tf_op jit(solution)/shard_map/ppermute | solution.py:29
  119.1 74.0 %collective-permute-start.2 = (f32[384,768]{1,0:T(8,128)S(1)}, f32[384,768]{1,0:T(8,128)S(1)}, u32[]{:S(2)}, u32[]{:S(2)}) collective-permute-start(f32[384,768]{1,0:T(8,128)S(1)} %collective-permute-done.1.refs_4_.second_ref), channel_id=1, source_target_pairs={{1,0},{3,2},{5,4},{7,6},{9,8},{11,10},{13,12},{15,14},{17,16},{19,... | collective-permute-start | bytes 3538952 | tf_op jit(solution)/shard_map/ppermute | solution.py:804
  125.8 24.3 %copy-start.5 = (f32[192,768]{1,0:T(8,128)S(1)}, f32[192,768]{1,0:T(8,128)}, u32[]{:S(2)}) copy-start(f32[192,768]{1,0:T(8,128)} %copy-done.4) | copy-start | bytes 1769476
  125.8 35.2 %copy-start.7 = (f32[384,256]{1,0:T(8,128)S(1)}, f32[384,256]{1,0:T(8,128)}, u32[]{:S(2)}) copy-start(f32[384,256]{1,0:T(8,128)} %copy-done.6) | copy-start | bytes 1179652
  125.8 35.2 %copy-start.15 = (f32[192,256]{1,0:T(8,128)S(1)}, f32[192,256]{1,0:T(8,128)}, u32[]{:S(2)}) copy-start(f32[192,256]{1,0:T(8,128)} %copy-done.14) | copy-start | bytes 589828
  150.0 27.2 %collective-permute-start.7 = (f32[192,768]{1,0:T(8,128)S(1)}, f32[192,768]{1,0:T(8,128)S(1)}, u32[]{:S(2)}, u32[]{:S(2)}) collective-permute-start(f32[192,768]{1,0:T(8,128)S(1)} %copy-done.5), channel_id=1, source_target_pairs={{0,1},{1,2},{2,3},{3,4},{4,5},{5,6},{6,7},{7,8},{8,9},{9,10},{10,1... | collective-permute-start | bytes 1769480 | tf_op jit(solution)/shard_map/ppermute | solution.py:29
  158.5 13.5 %collective-permute-start.9 = (f32[192,192]{1,0:T(8,128)S(1)}, f32[192,192]{1,0:T(8,128)S(1)}, u32[]{:S(2)}, u32[]{:S(2)}) collective-permute-start(f32[192,192]{1,0:T(8,128)S(1)} %get-tuple-element.39), channel_id=1, source_target_pairs={{0,2},{1,3},{2,4},{3,5},{4,6},{5,7},{6,8},{7,9},{8,10},{9,11},{10,... | collective-permute-start | bytes 442376 | tf_op jit(solution)/shard_map/ppermute | solution.py:29
  158.5 34.7 %copy-start.3 = (f32[576,768]{1,0:T(8,128)S(1)}, f32[576,768]{1,0:T(8,128)}, u32[]{:S(2)}) copy-start(f32[576,768]{1,0:T(8,128)} %copy-done.1) | copy-start | bytes 5308420
  158.5 34.7 %copy-start.9 = (f32[384,256]{1,0:T(8,128)S(1)}, f32[384,256]{1,0:T(8,128)}, u32[]{:S(2)}) copy-start(f32[384,256]{1,0:T(8,128)} %copy-done.8) | copy-start | bytes 1179652
  158.5 18.8 %collective-permute-start.8 = (f32[192,384]{1,0:T(8,128)S(1)}, f32[192,384]{1,0:T(8,128)S(1)}, u32[]{:S(2)}, u32[]{:S(2)}) collective-permute-start(f32[192,384]{1,0:T(8,128)S(1)} %get-tuple-element.38), channel_id=1, source_target_pairs={{0,1},{1,2},{2,3},{3,4},{4,5},{5,6},{6,7},{7,8},{8,9},{9,10},{10,1... | collective-permute-start | bytes 884744 | tf_op jit(solution)/shard_map/ppermute | solution.py:29
  172.0 36.6 %collective-permute-start.5 = (f32[192,256]{1,0:T(8,128)S(1)}, f32[192,256]{1,0:T(8,128)S(1)}, u32[]{:S(2)}, u32[]{:S(2)}) collective-permute-start(f32[192,256]{1,0:T(8,128)S(1)} %get-tuple-element.34), channel_id=1, source_target_pairs={{0,2},{1,3},{2,4},{3,5},{4,6},{5,7},{6,8},{7,9},{8,10},{9,11},{10,... | collective-permute-start | bytes 589832 | tf_op jit(solution)/shard_map/ppermute | solution.py:29
  177.3 31.3 %collective-permute-start.6 = (f32[192,256]{1,0:T(8,128)S(1)}, f32[192,256]{1,0:T(8,128)S(1)}, u32[]{:S(2)}, u32[]{:S(2)}) collective-permute-start(f32[192,256]{1,0:T(8,128)S(1)} %get-tuple-element.35), channel_id=1, source_target_pairs={{0,30},{1,31},{2,0},{3,1},{4,2},{5,3},{6,4},{7,5},{8,6},{9,7},{10,... | collective-permute-start | bytes 589832 | tf_op jit(solution)/shard_map/ppermute | solution.py:29
  177.3 31.3 %collective-permute-start.3 = (f32[384,256]{1,0:T(8,128)S(1)}, f32[384,256]{1,0:T(8,128)S(1)}, u32[]{:S(2)}, u32[]{:S(2)}) collective-permute-start(f32[384,256]{1,0:T(8,128)S(1)} %get-tuple-element.32), channel_id=1, source_target_pairs={{0,1},{1,2},{2,3},{3,4},{4,5},{5,6},{6,7},{7,8},{8,9},{9,10},{10,1... | collective-permute-start | bytes 1179656 | tf_op jit(solution)/shard_map/ppermute | solution.py:29
  178.5 30.1 %collective-permute-start.4 = (f32[384,256]{1,0:T(8,128)S(1)}, f32[384,256]{1,0:T(8,128)S(1)}, u32[]{:S(2)}, u32[]{:S(2)}) collective-permute-start(f32[384,256]{1,0:T(8,128)S(1)} %get-tuple-element.33.refs_11_), channel_id=1, source_target_pairs={{0,31},{1,0},{2,1},{3,2},{4,3},{5,4},{6,5},{7,6},{8,7},{9,8},{10,9... | collective-permute-start | bytes 1179656 | tf_op jit(solution)/shard_map/ppermute | solution.py:29
  (7 other events, 8.1 us)

commit v4 on v0

--- a/solution.py
+++ b/solution.py
@@ -640,6 +640,48 @@
     )(flags, *inputs, partial)
 
 
+def relay_kernel(odd_ref, low_ref, high_ref, second_low_ref, second_high_ref, near_ref, far_ref):
+    side = near_ref.shape[0]
+    odd = odd_ref[0] > 0
+
+    @pl.when(odd)
+    def _():
+        near_ref[...] = low_ref[side:, :]
+        far_ref[...] = second_low_ref[...]
+
+    @pl.when(jnp.logical_not(odd))
+    def _():
+        near_ref[...] = high_ref[:side, :]
+        far_ref[...] = second_high_ref[...]
+
+
+def join_kernel(odd_ref, low_ref, high_ref, near_ref, far_ref, low_out_ref, high_out_ref):
+    side = near_ref.shape[0]
+    odd = odd_ref[0] > 0
+
+    @pl.when(odd)
+    def _():
+        low_out_ref[...] = low_ref[...]
+        high_out_ref[:side, :] = near_ref[...]
+        high_out_ref[side:, :] = far_ref[...]
+
+    @pl.when(jnp.logical_not(odd))
+    def _():
+        low_out_ref[:side, :] = far_ref[...]
+        low_out_ref[side:, :] = near_ref[...]
+        high_out_ref[...] = high_ref[...]
+
+
+def moved_about(kernel, odd, given, shapes):
+    return pl.pallas_call(
+        kernel,
+        out_shape=tuple(jax.ShapeDtypeStruct(shape, jnp.float32) for shape in shapes),
+        in_specs=[SMEM_SPEC] + [VMEM_SPEC] * len(given),
+        out_specs=(VMEM_SPEC,) * len(shapes),
+        compiler_params=pltpu.CompilerParams(vmem_limit_bytes=12 << 20),
+    )(odd, *given)
+
+
 def local(weighted_jacobian_strips, leading_pose_index, levenberg_shift, removal_flags):
     count = lax.axis_size(AXES)
     own = lax.axis_index(AXES)
@@ -665,23 +707,53 @@
 
     direct = lax.ppermute(two, AXES, [(k, k + 1) for k in range(0, count, 2)])
     second = passed_along(two, 2)
+    odd = (own % 2).astype(jnp.int32).reshape(1)
+    evens = range(0, count, 2)
+    swap = [(k, k ^ 1) for k in range(count)]
+    onwards = [(k, (k + 2 - 4 * (k % 2)) % count) for k in range(count)]
+
+    def paired(value, pairs):
+        return lax.ppermute(value, AXES, pairs)
+
+    def sent_short(part):
+        return [
+            paired(part[0], [(k, k + 1) for k in evens]),
+            paired(part[1], [(k + 1, k) for k in evens]),
+            passed_along(part[2], 2),
+            passed_along(part[3], -2),
+        ]
+
+    def relayed(part):
+        shape = part[2].shape
+        near, far = moved_about(relay_kernel, odd, part, (shape, shape))
+        return paired(near, onwards), paired(far, swap)
+
+    def joined(part, more):
+        low, high = moved_about(
+            join_kernel, odd, (*part[:2], *more), (part[0].shape, part[1].shape)
+        )
+        return [low, high, *part[2:]]
 
     def solved(number, start, known):
         before = [part[k] for part in known for k in (0, 3)]
         return factored_part(x, start, before, side, bounds, number)
 
+    extra = passed_along(last, 1)
     low, *part = solved(0, levenberg_shift, ())
     known = [part]
-    parts = [sent_parts(part)]
-    for number in range(1, PARTS - 1):
+    parts = [sent_short(part)]
+    more = []
+    for number in range(1, PARTS):
         low, *part = solved(number, low, known)
-        known.append(part)
-        parts.append(sent_parts(part))
-    onward = lax.ppermute(second, AXES, [(k + 1, k) for k in range(0, count, 2)])
-    extra = passed_along(last, 1)
-    low, *part, gram_one, gram_two = solved(PARTS - 1, low, known)
-    known.append(part)
-    parts.append(sent_parts(part))
+        known.append(part[:4])
+        if number < PARTS - 1:
+            parts.append(sent_short(part))
+        else:
+            parts.append(sent_parts(part[:4]))
+        more.append(relayed(parts[number - 1]))
+    onward = paired(second, [(k + 1, k) for k in evens])
+    gram_one, gram_two = part[4:]
+    parts = [joined(parts[k], more[k]) for k in range(PARTS - 1)] + parts[-1:]
     grams = (passed_along(gram_one, 1), passed_along(gram_two, 2))
     partial = early(x, parts[:-1], starts[:-1], side)
     schur, coupling = late(

time: 268 us -> 235 us (0.88)
  waiting for transfers between devices: 67.3 us -> 33.2 us
  starting transfers between devices: 41.9 us -> 58.2 us
  local copies, waits for them, and re-layouts: 14.6 us -> 4.44 us
  Pallas kernels: 89 us -> 86 us
    ppermute x16 -> x12, waiting for transfers between devices: 67.3 us -> 33.1 us  [passed_along(): return lax.ppermute(value, AXES, pairs)]
    ppermute x1 -> x9, starting transfers between devices: 1.28 us -> 23.9 us  [paired(): return lax.ppermute(value, AXES, pairs)]
    unnamed x66 -> x28, local copies, waits for them, and re-layouts: 14 us -> 3.8 us
    ppermute x16 -> x12, starting transfers between devices: 37.1 us -> 31.1 us  [passed_along(): return lax.ppermute(value, AXES, pairs)]
  transfers between devices with their start and end apart: 18 -> 22, of which waited for: 6 -> 6; matrix products, arithmetic and copies ran while one was open for 0% -> 0% of each run, Pallas kernels for 23% -> 18%
where the time goes in v4:
time: 235 us
  Pallas kernels  86 us (37%)
  starting transfers between devices  58.2 us (25%)
  blocking collectives  51.7 us (22%)
  waiting for transfers between devices  33.2 us (14%)
  local copies, waits for them, and re-layouts  4.44 us (2%)
    all_to_all x1, blocking collectives, local(): lax.all_to_all(chunks, AXES, split_axis=0, concat_axis=0, tiled=True)  51.7 us
    pallas_call x3, Pallas kernels, factored_part(): pl.pallas_call(functools.partial(part_kernel, side, bounds, number), out_...  48.7 us
    ppermute x12, waiting for transfers between devices, passed_along(): return lax.ppermute(value, AXES, pairs)  33.1 us
    ppermute x12, starting transfers between devices, passed_along(): return lax.ppermute(value, AXES, pairs)  31.1 us
    ppermute x9, starting transfers between devices, paired(): return lax.ppermute(value, AXES, pairs)  23.9 us
    pallas_call x1, Pallas kernels, late(): pl.pallas_call(functools.partial(late_kernel, side, starts), out_shape=(j...  21.6 us
    pallas_call x1, Pallas kernels, early(): pl.pallas_call(functools.partial(early_kernel, side, starts), out_shape=j...  9.91 us
  transfers between devices with their start and end apart: 22, of which 6 were waited for; matrix products, arithmetic and copies ran while one was open for 0% of the time, Pallas kernels for 18%

profile of v4, /device:TPU:0, one launch (start us, length us, event | category | flops | bytes accessed | tf_op | source)
XLA Modules:
  0.0 234.5 jit_solution(3762045636372199864)
XLA Ops:
  0.6 4.1 %bucket.1 = f32[32,54,256]{2,1,0:T(8,128)} custom-call(s32[1,128]{1,0:T(1,128)} %bitcast.6, f32[3,128,768]{2,1,0:T(8,128)} %bitcast.5), custom_call_target="tpu_custom_call" | custom-call | tf_op jit(solution)/shard_map/bucket/pallas_call | solution.py:85
  4.8 51.7 %all_to_all.5.in_ref = f32[32,54,256]{2,1,0:T(8,128)S(1)} all-to-all(f32[32,54,256]{2,1,0:T(8,128)} %bucket.1), channel_id=1, replica_groups=mesh['gx'=4,'gy'=8] {'gx','gy'}, dimensions={0} | all-to-all | bytes 3538944 | tf_op jit(solution)/shard_map/all_to_all | solution.py:702
  56.4 1.5 regroup.1
  58.7 17.4 %factor_part.3 = (f32[768,768]{1,0:T(8,128)S(1)}, f32[384,256]{1,0:T(8,128)S(1)}, f32[384,256]{1,0:T(8,128)S(1)}, f32[192,256]{1,0:T(8,128)S(1)}, f32[192,256]{1,0:T(8,128)S(1)}) custom-call(f32[576,768]{1,0:T(8,128)S(1)} %get-tuple-element.32.refs_0_.x_ref, f32[1,768]{1,0:T(1,128)S(1)} %copy-done.10), custom_call_target="tpu_custom_call" | custom-call | flops 20000000000 | bytes 5308416 | tf_op jit(solution)/shard_map/factor_part/pallas_call | solution.py:384
  76.8 3.8 %collective-permute-start.9 = (f32[192,256]{1,0:T(8,128)S(1)}, f32[192,256]{1,0:T(8,128)S(1)}, u32[]{:S(2)}, u32[]{:S(2)}) collective-permute-start(f32[192,256]{1,0:T(8,128)S(1)} %get-tuple-element.37.refs_3_), channel_id=1, source_target_pairs={{0,30},{1,31},{2,0},{3,1},{4,2},{5,3},{6,4},{7,5},{8,6},{9,7},{10,... | collective-permute-start | bytes 589832 | tf_op jit(solution)/shard_map/ppermute | solution.py:29
  80.6 1.3 collective-permute-start.7
  81.9 14.4 %factor_part.4 = (f32[768,768]{1,0:T(8,128)S(1)}, f32[384,256]{1,0:T(8,128)}, f32[384,256]{1,0:T(8,128)S(1)}, f32[192,256]{1,0:T(8,128)S(1)}, f32[192,256]{1,0:T(8,128)}) custom-call(f32[576,768]{1,0:T(8,128)S(1)} %get-tuple-element.32.refs_0_.x_ref, f32[768,768]{1,0:T(8,128)S(1)} %get-tuple-element.35.refs_1_, f32[384,256]{1,0:T(8,128)S(1)} %get-tuple-element.36.refs_2_, ...), custom_call_target="tpu_custom_call" | custom-call | flops 20000000000 | bytes 5308416 | tf_op jit(solution)/shard_map/factor_part/pallas_call | solution.py:384
  96.4 4.6 %collective-permute-start.6 = (f32[384,256]{1,0:T(8,128)S(1)}, f32[384,256]{1,0:T(8,128)S(1)}, u32[]{:S(2)}, u32[]{:S(2)}) collective-permute-start(f32[384,256]{1,0:T(8,128)S(1)} %get-tuple-element.36.refs_2_), channel_id=1, source_target_pairs={{0,1},{2,3},{4,5},{6,7},{8,9},{10,11},{12,13},{14,15},{16,17},{18,... | collective-permute-start | bytes 1179656 | tf_op jit(solution)/shard_map/ppermute | solution.py:716
  101.1 4.4 %collective-permute-start.15 = (f32[192,256]{1,0:T(8,128)}, f32[192,256]{1,0:T(8,128)S(1)}, u32[]{:S(2)}, u32[]{:S(2)}) collective-permute-start(f32[192,256]{1,0:T(8,128)} %get-tuple-element.40.refs_5_), channel_id=1, source_target_pairs={{0,30},{1,31},{2,0},{3,1},{4,2},{5,3},{6,4},{7,5},{8,6},{9,7},{10,... | collective-permute-start | bytes 589832 | tf_op jit(solution)/shard_map/ppermute | solution.py:29
  105.5 5.5 %collective-permute-start.12 = (f32[384,256]{1,0:T(8,128)}, f32[384,256]{1,0:T(8,128)S(1)}, u32[]{:S(2)}, u32[]{:S(2)}) collective-permute-start(f32[384,256]{1,0:T(8,128)} %get-tuple-element.39.refs_4_), channel_id=1, source_target_pairs={{0,1},{2,3},{4,5},{6,7},{8,9},{10,11},{12,13},{14,15},{16,17},{18,... | collective-permute-start | bytes 1179656 | tf_op jit(solution)/shard_map/ppermute | solution.py:716
  111.0 1.5 collective-permute-start.13
  112.5 16.9 %factor_part.5 = (f32[768,768]{1,0:T(8,128)S(1)}, f32[384,256]{1,0:T(8,128)S(1)}, f32[384,256]{1,0:T(8,128)S(1)}, f32[192,256]{1,0:T(8,128)}, f32[192,256]{1,0:T...) custom-call(f32[576,768]{1,0:T(8,128)S(1)} %get-tuple-element.32.refs_0_.x_ref, ...), custom_call_target="tpu_custom_call" | custom-call | flops 20000000000 | bytes 5308416 | tf_op jit(solution)/shard_map/factor_part/pallas_call | solution.py:384
  130.9 1.4 copy-done.11
  132.4 1.5 collective-permute-done.15.second_high_ref.refs_7_.refs_19_
  133.9 1.2 collective-permute-start.10
  135.2 4.4 %collective-permute-start.11 = (f32[192,256]{1,0:T(8,128)S(1)}, f32[192,256]{1,0:T(8,128)S(1)}, u32[]{:S(2)}, u32[]{:S(2)}) collective-permute-start(f32[192,256]{1,0:T(8,128)S(1)} %get-tuple-element.49), channel_id=1, source_target_pairs={{0,1},{1,0},{2,3},{3,2},{4,5},{5,4},{6,7},{7,6},{8,9},{9,8},{10,11... | collective-permute-start | bytes 589832 | tf_op jit(solution)/shard_map/ppermute | solution.py:716
  139.7 1.4 collective-permute-done.5.refs_8_
  141.0 4.1 %collective-permute-start.17 = (f32[192,256]{1,0:T(8,128)S(1)}, f32[192,256]{1,0:T(8,128)S(1)}, u32[]{:S(2)}, u32[]{:S(2)}) collective-permute-start(f32[192,256]{1,0:T(8,128)S(1)} %get-tuple-element.54), channel_id=1, source_target_pairs={{0,1},{1,0},{2,3},{3,2},{4,5},{5,4},{6,7},{7,6},{8,9},{9,8},{10,11... | collective-permute-start | bytes 589832 | tf_op jit(solution)/shard_map/ppermute | solution.py:716
  145.2 3.2 %collective-permute-start = (f32[384,768]{1,0:T(8,128)}, f32[384,768]{1,0:T(8,128)}, u32[]{:S(2)}, u32[]{:S(2)}) collective-permute-start(f32[384,768]{1,0:T(8,128)} %get-tuple-element.33), channel_id=1, source_target_pairs={{0,1},{2,3},{4,5},{6,7},{8,9},{10,11},{12,13},{14,15},{16,17},{18,... | collective-permute-start | bytes 3538952 | tf_op jit(solution)/shard_map/ppermute | solution.py:708
  148.4 1.3 collective-permute-start.2
  149.7 1.3 collective-permute-start.20
  151.0 3.2 %collective-permute-start.21 = (f32[192,256]{1,0:T(8,128)}, f32[192,256]{1,0:T(8,128)}, u32[]{:S(2)}, u32[]{:S(2)}) collective-permute-start(f32[192,256]{1,0:T(8,128)} %get-tuple-element.59), channel_id=1, source_target_pairs={{0,30},{1,31},{2,0},{3,1},{4,2},{5,3},{6,4},{7,5},{8,6},{9,7},{10,... | collective-permute-start | bytes 589832 | tf_op jit(solution)/shard_map/ppermute | solution.py:29
  154.2 3.6 %collective-permute-start.4 = (f32[192,384]{1,0:T(8,128)}, f32[192,384]{1,0:T(8,128)}, u32[]{:S(2)}, u32[]{:S(2)}) collective-permute-start(f32[192,384]{1,0:T(8,128)} %get-tuple-element.42), channel_id=1, source_target_pairs={{0,1},{1,2},{2,3},{3,4},{4,5},{5,6},{6,7},{7,8},{8,9},{9,10},{10,1... | collective-permute-start | bytes 884744 | tf_op jit(solution)/shard_map/ppermute | solution.py:29
  158.6 1.3 collective-permute-done.20.refs_22_
  160.0 3.6 %collective-permute-start.3 = (f32[192,768]{1,0:T(8,128)S(1)}, f32[192,768]{1,0:T(8,128)S(1)}, u32[]{:S(2)}, u32[]{:S(2)}) collective-permute-start(f32[192,768]{1,0:T(8,128)S(1)} %copy-done.4), channel_id=1, source_target_pairs={{0,1},{1,2},{2,3},{3,4},{4,5},{5,6},{6,7},{7,8},{8,9},{9,10},{10,1... | collective-permute-start | bytes 1769480 | tf_op jit(solution)/shard_map/ppermute | solution.py:29
  163.6 3.7 %collective-permute-start.18 = (f32[384,256]{1,0:T(8,128)}, f32[384,256]{1,0:T(8,128)S(1)}, u32[]{:S(2)}, u32[]{:S(2)}) collective-permute-start(f32[384,256]{1,0:T(8,128)} %copy-done.9), channel_id=1, source_target_pairs={{0,1},{1,2},{2,3},{3,4},{4,5},{5,6},{6,7},{7,8},{8,9},{9,10},{10,1... | collective-permute-start | bytes 1179656 | tf_op jit(solution)/shard_map/ppermute | solution.py:29
  167.3 14.7 %collective-permute-done.4.refs_7_ = f32[192,384]{1,0:T(8,128)} collective-permute-done((f32[192,384]{1,0:T(8,128)}, f32[192,384]{1,0:T(8,128)}, u32[]{:S(2)}, u32[]{:S(2)}) %collective-permute-start.4) | collective-permute-done | bytes 294944 | tf_op jit(solution)/shard_map/ppermute | solution.py:29
  181.9 6.6 %collective-permute-start.19 = (f32[384,256]{1,0:T(8,128)}, f32[384,256]{1,0:T(8,128)S(1)}, u32[]{:S(2)}, u32[]{:S(2)}) collective-permute-start(f32[384,256]{1,0:T(8,128)} %copy-done.7), channel_id=1, source_target_pairs={{0,31},{1,0},{2,1},{3,2},{4,3},{5,4},{6,5},{7,6},{8,7},{9,8},{10,9... | collective-permute-start | bytes 1179656 | tf_op jit(solution)/shard_map/ppermute | solution.py:29
  188.6 9.9 %early.1.refs_24_ = f32[4,768,768]{2,1,0:T(8,128)} custom-call(f32[576,768]{1,0:T(8,128)S(1)} %copy-done.2, f32[384,256]{1,0:T(8,128)S(1)} %get-tuple-element.50.refs_0_.refs_12_, f32[384,256]{1,0:T(8,128)S(1)} %get-tuple-element.51.refs_1_.refs_13_, f32[192,256]{1,0:T(8,128)S(1)} %collective-permute-done.8.second_low_ref.refs_2_.refs_14_, ...), custom_call_target="tpu_custom_call" | custom-call | flops 8000000000 | bytes 9437184 | tf_op jit(solution)/shard_map/early/pallas_call | solution.py:453
  198.5 11.0 %collective-permute-done.18.refs_20_ = f32[384,256]{1,0:T(8,128)S(1)} collective-permute-done((f32[384,256]{1,0:T(8,128)}, f32[384,256]{1,0:T(8,128)S(1)}, u32[]{:S(2)}, u32[]{:S(2)}) %collective-permute-start.18) | collective-permute-done | bytes 393248 | tf_op jit(solution)/shard_map/ppermute | solution.py:29
  209.5 3.2 %collective-permute-done.19.refs_21_ = f32[384,256]{1,0:T(8,128)S(1)} collective-permute-done((f32[384,256]{1,0:T(8,128)}, f32[384,256]{1,0:T(8,128)S(1)}, u32[]{:S(2)}, u32[]{:S(2)}) %collective-permute-start.19) | collective-permute-done | bytes 393248 | tf_op jit(solution)/shard_map/ppermute | solution.py:29
  212.8 21.6 %late.1 = (f32[3,768,768]{2,1,0:T(8,128)}, f32[4,768,768]{2,1,0:T(8,128)}) custom-call(s32[5]{0:T(128)S(1)} %gather_fusion, f32[576,768]{1,0:T(8,128)S(1)} %copy-done.2, f32[1,768]{1,0:T(1,128)S(1)} %copy-done.10, f32[384,768]{1,0:T(8,128)} %collective-permute-done.refs_2_, ...), custom_call_target="tpu_custom_call", output_to_operand_aliasing={{1}: (25, {})} | custom-call | flops 12000000000 | bytes 16515072 | tf_op jit(solution)/shard_map/late/pallas_call | solution.py:615
  (55 shorter events, 4.2 us)
Async XLA Ops:
  0.6 157.2 %copy-start = (s32[32]{0:T(128)S(1)}, s32[32]{0:T(128)}, u32[]{:S(2)}) copy-start(s32[32]{0:T(128)} %param.8) | copy-start | bytes 388
  56.4 2.3 copy-start.10
  58.7 53.8 %copy-start.1 = (f32[576,768]{1,0:T(8,128)}, f32[576,768]{1,0:T(8,128)S(1)}, u32[]{:S(2)}) copy-start(f32[576,768]{1,0:T(8,128)S(1)} %get-tuple-element.32.refs_0_.x_ref) | copy-start | bytes 5308420
  76.1 24.9 %collective-permute-start.8 = (f32[192,256]{1,0:T(8,128)S(1)}, f32[192,256]{1,0:T(8,128)S(1)}, u32[]{:S(2)}, u32[]{:S(2)}) collective-permute-start(f32[192,256]{1,0:T(8,128)S(1)} %get-tuple-element.47), channel_id=1, source_target_pairs={{0,2},{1,3},{2,4},{3,5},{4,6},{5,7},{6,8},{7,9},{8,10},{9,11},{10,... | collective-permute-start | bytes 589832 | tf_op jit(solution)/shard_map/ppermute | solution.py:29
  76.8 24.3 %collective-permute-start.9 = (f32[192,256]{1,0:T(8,128)S(1)}, f32[192,256]{1,0:T(8,128)S(1)}, u32[]{:S(2)}, u32[]{:S(2)}) collective-permute-start(f32[192,256]{1,0:T(8,128)S(1)} %get-tuple-element.37.refs_3_), channel_id=1, source_target_pairs={{0,30},{1,31},{2,0},{3,1},{4,2},{5,3},{6,4},{7,5},{8,6},{9,7},{10,... | collective-permute-start | bytes 589832 | tf_op jit(solution)/shard_map/ppermute | solution.py:29
  80.6 30.4 %collective-permute-start.7 = (f32[384,256]{1,0:T(8,128)S(1)}, f32[384,256]{1,0:T(8,128)S(1)}, u32[]{:S(2)}, u32[]{:S(2)}) collective-permute-start(f32[384,256]{1,0:T(8,128)S(1)} %get-tuple-element.44.refs_9_), channel_id=1, source_target_pairs={{1,0},{3,2},{5,4},{7,6},{9,8},{11,10},{13,12},{15,14},{17,16},{19,... | collective-permute-start | bytes 1179656 | tf_op jit(solution)/shard_map/ppermute | solution.py:716
  96.3 33.1 %copy-start.5 = (f32[384,256]{1,0:T(8,128)}, f32[384,256]{1,0:T(8,128)S(1)}, u32[]{:S(2)}) copy-start(f32[384,256]{1,0:T(8,128)S(1)} %get-tuple-element.45.refs_10_) | copy-start | bytes 1179652
  96.3 9.2 %collective-permute-start.14 = (f32[192,256]{1,0:T(8,128)S(1)}, f32[192,256]{1,0:T(8,128)S(1)}, u32[]{:S(2)}, u32[]{:S(2)}) collective-permute-start(f32[192,256]{1,0:T(8,128)S(1)} %get-tuple-element.52), channel_id=1, source_target_pairs={{0,2},{1,3},{2,4},{3,5},{4,6},{5,7},{6,8},{7,9},{8,10},{9,11},{10,... | collective-permute-start | bytes 589832 | tf_op jit(solution)/shard_map/ppermute | solution.py:29
  96.4 35.9 %collective-permute-start.6 = (f32[384,256]{1,0:T(8,128)S(1)}, f32[384,256]{1,0:T(8,128)S(1)}, u32[]{:S(2)}, u32[]{:S(2)}) collective-permute-start(f32[384,256]{1,0:T(8,128)S(1)} %get-tuple-element.36.refs_2_), channel_id=1, source_target_pairs={{0,1},{2,3},{4,5},{6,7},{8,9},{10,11},{12,13},{14,15},{16,17},{18,... | collective-permute-start | bytes 1179656 | tf_op jit(solution)/shard_map/ppermute | solution.py:716
  101.0 47.4 %collective-permute-start.1 = (f32[384,768]{1,0:T(8,128)}, f32[384,768]{1,0:T(8,128)}, u32[]{:S(2)}, u32[]{:S(2)}) collective-permute-start(f32[384,768]{1,0:T(8,128)} %get-tuple-element.33), channel_id=1, source_target_pairs={{0,2},{1,3},{2,4},{3,5},{4,6},{5,7},{6,8},{7,9},{8,10},{9,11},{10,... | collective-permute-start | bytes 3538952 | tf_op jit(solution)/shard_map/ppermute | solution.py:29
  101.1 32.9 %collective-permute-start.15 = (f32[192,256]{1,0:T(8,128)}, f32[192,256]{1,0:T(8,128)S(1)}, u32[]{:S(2)}, u32[]{:S(2)}) collective-permute-start(f32[192,256]{1,0:T(8,128)} %get-tuple-element.40.refs_5_), channel_id=1, source_target_pairs={{0,30},{1,31},{2,0},{3,1},{4,2},{5,3},{6,4},{7,5},{8,6},{9,7},{10,... | collective-permute-start | bytes 589832 | tf_op jit(solution)/shard_map/ppermute | solution.py:29
  105.5 29.6 %collective-permute-start.12 = (f32[384,256]{1,0:T(8,128)}, f32[384,256]{1,0:T(8,128)S(1)}, u32[]{:S(2)}, u32[]{:S(2)}) collective-permute-start(f32[384,256]{1,0:T(8,128)} %get-tuple-element.39.refs_4_), channel_id=1, source_target_pairs={{0,1},{2,3},{4,5},{6,7},{8,9},{10,11},{12,13},{14,15},{16,17},{18,... | collective-permute-start | bytes 1179656 | tf_op jit(solution)/shard_map/ppermute | solution.py:716
  111.0 28.6 %collective-permute-start.13 = (f32[384,256]{1,0:T(8,128)S(1)}, f32[384,256]{1,0:T(8,128)S(1)}, u32[]{:S(2)}, u32[]{:S(2)}) collective-permute-start(f32[384,256]{1,0:T(8,128)S(1)} %get-tuple-element.45.refs_10_), channel_id=1, source_target_pairs={{1,0},{3,2},{5,4},{7,6},{9,8},{11,10},{13,12},{15,14},{17,16},{19,... | collective-permute-start | bytes 1179656 | tf_op jit(solution)/shard_map/ppermute | solution.py:716
  132.3 25.4 %copy-start.13 = (s32[5]{0:T(128)S(1)}, s32[5]{0:T(128)}, u32[]{:S(2)}) copy-start(s32[5]{0:T(128)} %constant.41.clone) | copy-start | bytes 64
  132.3 8.7 %collective-permute-start.5 = (f32[192,192]{1,0:T(8,128)}, f32[192,192]{1,0:T(8,128)}, u32[]{:S(2)}, u32[]{:S(2)}) collective-permute-start(f32[192,192]{1,0:T(8,128)} %get-tuple-element.43), channel_id=1, source_target_pairs={{0,2},{1,3},{2,4},{3,5},{4,6},{5,7},{6,8},{7,9},{8,10},{9,11},{10,... | collective-permute-start | bytes 442376 | tf_op jit(solution)/shard_map/ppermute | solution.py:29
  133.9 11.2 %collective-permute-start.10 = (f32[192,256]{1,0:T(8,128)S(1)}, f32[192,256]{1,0:T(8,128)S(1)}, u32[]{:S(2)}, u32[]{:S(2)}) collective-permute-start(f32[192,256]{1,0:T(8,128)S(1)} %get-tuple-element.48), channel_id=1, source_target_pairs={{0,2},{1,31},{2,4},{3,1},{4,6},{5,3},{6,8},{7,5},{8,10},{9,7},{10,... | collective-permute-start | bytes 589832 | tf_op jit(solution)/shard_map/ppermute | solution.py:716
  135.2 14.5 %collective-permute-start.11 = (f32[192,256]{1,0:T(8,128)S(1)}, f32[192,256]{1,0:T(8,128)S(1)}, u32[]{:S(2)}, u32[]{:S(2)}) collective-permute-start(f32[192,256]{1,0:T(8,128)S(1)} %get-tuple-element.49), channel_id=1, source_target_pairs={{0,1},{1,0},{2,3},{3,2},{4,5},{5,4},{6,7},{7,6},{8,9},{9,8},{10,11... | collective-permute-start | bytes 589832 | tf_op jit(solution)/shard_map/ppermute | solution.py:716
  139.6 11.4 %collective-permute-start.16 = (f32[192,256]{1,0:T(8,128)S(1)}, f32[192,256]{1,0:T(8,128)S(1)}, u32[]{:S(2)}, u32[]{:S(2)}) collective-permute-start(f32[192,256]{1,0:T(8,128)S(1)} %get-tuple-element.53), channel_id=1, source_target_pairs={{0,2},{1,31},{2,4},{3,1},{4,6},{5,3},{6,8},{7,5},{8,10},{9,7},{10,... | collective-permute-start | bytes 589832 | tf_op jit(solution)/shard_map/ppermute | solution.py:716
  141.0 13.2 %collective-permute-start.17 = (f32[192,256]{1,0:T(8,128)S(1)}, f32[192,256]{1,0:T(8,128)S(1)}, u32[]{:S(2)}, u32[]{:S(2)}) collective-permute-start(f32[192,256]{1,0:T(8,128)S(1)} %get-tuple-element.54), channel_id=1, source_target_pairs={{0,1},{1,0},{2,3},{3,2},{4,5},{5,4},{6,7},{7,6},{8,9},{9,8},{10,11... | collective-permute-start | bytes 589832 | tf_op jit(solution)/shard_map/ppermute | solution.py:716
  145.2 67.6 %collective-permute-start = (f32[384,768]{1,0:T(8,128)}, f32[384,768]{1,0:T(8,128)}, u32[]{:S(2)}, u32[]{:S(2)}) collective-permute-start(f32[384,768]{1,0:T(8,128)} %get-tuple-element.33), channel_id=1, source_target_pairs={{0,1},{2,3},{4,5},{6,7},{8,9},{10,11},{12,13},{14,15},{16,17},{18,... | collective-permute-start | bytes 3538952 | tf_op jit(solution)/shard_map/ppermute | solution.py:708
  148.4 64.3 %collective-permute-start.2 = (f32[384,768]{1,0:T(8,128)}, f32[384,768]{1,0:T(8,128)}, u32[]{:S(2)}, u32[]{:S(2)}) collective-permute-start(f32[384,768]{1,0:T(8,128)} %collective-permute-done.1.refs_4_), channel_id=1, source_target_pairs={{1,0},{3,2},{5,4},{7,6},{9,8},{11,10},{13,12},{15,14},{17,16},{19,... | collective-permute-start | bytes 3538952 | tf_op jit(solution)/shard_map/ppermute | solution.py:716
  149.7 10.3 %collective-permute-start.20 = (f32[192,256]{1,0:T(8,128)}, f32[192,256]{1,0:T(8,128)}, u32[]{:S(2)}, u32[]{:S(2)}) collective-permute-start(f32[192,256]{1,0:T(8,128)} %get-tuple-element.58), channel_id=1, source_target_pairs={{0,2},{1,3},{2,4},{3,5},{4,6},{5,7},{6,8},{7,9},{8,10},{9,11},{10,... | collective-permute-start | bytes 589832 | tf_op jit(solution)/shard_map/ppermute | solution.py:29
  151.0 12.6 %collective-permute-start.21 = (f32[192,256]{1,0:T(8,128)}, f32[192,256]{1,0:T(8,128)}, u32[]{:S(2)}, u32[]{:S(2)}) collective-permute-start(f32[192,256]{1,0:T(8,128)} %get-tuple-element.59), channel_id=1, source_target_pairs={{0,30},{1,31},{2,0},{3,1},{4,2},{5,3},{6,4},{7,5},{8,6},{9,7},{10,... | collective-permute-start | bytes 589832 | tf_op jit(solution)/shard_map/ppermute | solution.py:29
  154.2 27.7 %collective-permute-start.4 = (f32[192,384]{1,0:T(8,128)}, f32[192,384]{1,0:T(8,128)}, u32[]{:S(2)}, u32[]{:S(2)}) collective-permute-start(f32[192,384]{1,0:T(8,128)} %get-tuple-element.42), channel_id=1, source_target_pairs={{0,1},{1,2},{2,3},{3,4},{4,5},{5,6},{6,7},{7,8},{8,9},{9,10},{10,1... | collective-permute-start | bytes 884744 | tf_op jit(solution)/shard_map/ppermute | solution.py:29
  158.5 1.5 copy-start.4
  158.5 30.1 %copy-start.2 = (f32[576,768]{1,0:T(8,128)S(1)}, f32[576,768]{1,0:T(8,128)}, u32[]{:S(2)}) copy-start(f32[576,768]{1,0:T(8,128)} %copy-done.1) | copy-start | bytes 5308420
  160.0 52.7 %collective-permute-start.3 = (f32[192,768]{1,0:T(8,128)S(1)}, f32[192,768]{1,0:T(8,128)S(1)}, u32[]{:S(2)}, u32[]{:S(2)}) collective-permute-start(f32[192,768]{1,0:T(8,128)S(1)} %copy-done.4), channel_id=1, source_target_pairs={{0,1},{1,2},{2,3},{3,4},{4,5},{5,6},{6,7},{7,8},{8,9},{9,10},{10,1... | collective-permute-start | bytes 1769480 | tf_op jit(solution)/shard_map/ppermute | solution.py:29
  163.6 46.0 %collective-permute-start.18 = (f32[384,256]{1,0:T(8,128)}, f32[384,256]{1,0:T(8,128)S(1)}, u32[]{:S(2)}, u32[]{:S(2)}) collective-permute-start(f32[384,256]{1,0:T(8,128)} %copy-done.9), channel_id=1, source_target_pairs={{0,1},{1,2},{2,3},{3,4},{4,5},{5,6},{6,7},{7,8},{8,9},{9,10},{10,1... | collective-permute-start | bytes 1179656 | tf_op jit(solution)/shard_map/ppermute | solution.py:29
  181.9 30.8 %collective-permute-start.19 = (f32[384,256]{1,0:T(8,128)}, f32[384,256]{1,0:T(8,128)S(1)}, u32[]{:S(2)}, u32[]{:S(2)}) collective-permute-start(f32[384,256]{1,0:T(8,128)} %copy-done.7), channel_id=1, source_target_pairs={{0,31},{1,0},{2,1},{3,2},{4,3},{5,4},{6,5},{7,6},{8,7},{9,8},{10,9... | collective-permute-start | bytes 1179656 | tf_op jit(solution)/shard_map/ppermute | solution.py:29
  188.6 24.2 %copy-start.6 = (f32[384,256]{1,0:T(8,128)S(1)}, f32[384,256]{1,0:T(8,128)}, u32[]{:S(2)}) copy-start(f32[384,256]{1,0:T(8,128)} %copy-done.5) | copy-start | bytes 1179652
  188.6 24.2 %copy-start.8 = (f32[384,256]{1,0:T(8,128)S(1)}, f32[384,256]{1,0:T(8,128)}, u32[]{:S(2)}) copy-start(f32[384,256]{1,0:T(8,128)} %copy-done.7) | copy-start | bytes 1179652
  188.6 24.2 %copy-start.12 = (f32[768,768]{1,0:T(8,128)S(1)}, f32[768,768]{1,0:T(8,128)}, u32[]{:S(2)}) copy-start(f32[768,768]{1,0:T(8,128)} %copy-done.11) | copy-start | bytes 7077892
  (4 other events, 3.8 us)

commit v5 on v0

--- a/solution.py
+++ b/solution.py
@@ -399,11 +399,14 @@
     return product_of_halves(halves(left), halves(right), dims)
 
 
+COUPLINGS = ((3, 0, 1), (1, 0, 2), (0, 1, 3), (2, 2, 3))
+
+
 def put_coupling(side, start, y_refs, x_ref, buffer_ref, left_refs, out_ref, sems):
     rows = buffer_ref.shape[1]
     width = x_ref.shape[1]
     copies = []
-    for place, (number, begin, end) in enumerate(((3, 0, 1), (1, 0, 2), (0, 1, 3), (2, 2, 3))):
+    for place, (number, begin, end) in enumerate(COUPLINGS):
         keep_halves(left_refs, y_refs[number][...].T)
 
         def put(lanes, value, place=place):
@@ -469,42 +472,27 @@
     )(x, *[piece for part in parts for piece in part])
 
 
-def late_kernel(side, starts, flags_ref, *refs):
-    (
-        x_ref,
-        shift_ref,
-        direct_ref,
-        onward_ref,
-        second_ref,
-        extra_ref,
-        low_ref,
-        gram_one_ref,
-        gram_two_ref,
-    ) = refs[:9]
-    parts = len(starts)
-    refs = refs[9:]
-    mine, refs = refs[:parts], refs[parts:]
-    pieces, refs = [refs[4 * k : 4 * k + 4] for k in range(parts)], refs[4 * parts :]
-    lasts = pieces[-1]
-    partial_ref, schur_ref, coupling_ref = refs[:3]
-    buffer_ref, tile_ref, rest_ref, near_ref, far_ref, high_ref, less_ref, sems, outs = refs[3:]
-    left_refs = (high_ref, less_ref)
+def before_kernel(side, flags_ref, x_ref, gram_one_ref, gram_two_ref, *refs):
+    mine, refs = refs[:PARTS], refs[PARTS:]
+    pieces, refs = [refs[4 * k : 4 * k + 4] for k in range(PARTS - 1)], refs[4 * PARTS - 4 :]
+    rest_ref, near_ref, far_ref, high_ref, less_ref = refs
     width = x_ref.shape[1]
-    cut = starts[-1]
-    copies = put_coupling(side, cut, lasts, x_ref, buffer_ref, left_refs, coupling_ref, sems)
     own, above, second_above, under, second_under = [flags_ref[k] > 0 for k in range(5)]
     one, two, three = slice(0, side), slice(side, 2 * side), slice(2 * side, 3 * side)
     pair, tail = slice(0, 2 * side), slice(side, 3 * side)
+    keep_halves((high_ref, less_ref), x_ref[...].T)
     rest_ref[...] = x_ref[...]
     near_ref[three, :] = jnp.zeros((side, width), jnp.float32)
     far_ref[two, :] = jnp.zeros((side, width), jnp.float32)
 
     @pl.when(own)
     def _():
-        for start, ref in zip(starts, mine):
+        start = 0
+        for ref in mine:
             lanes = slice(start, start + ref.shape[1])
             near_ref[pair, lanes] = ref[...]
             far_ref[one, lanes] = ref[side:, :]
+            start += ref.shape[1]
 
     @pl.when(jnp.logical_not(own))
     def _():
@@ -542,20 +530,75 @@
         near_ref[two, :] = near_ref[two, :] - term
         near_ref[three, :] = -near_product(gram_two_ref[...], x_ref[three, :], NN)
 
+
+def before_last(flags, x, grams, mine, parts, side):
+    depth, width = x.shape
+    inputs = [x, *grams, *mine] + [piece for part in parts for piece in part]
+    return pl.pallas_call(
+        functools.partial(before_kernel, side),
+        out_shape=(
+            jax.ShapeDtypeStruct((depth, width), jnp.float32),
+            jax.ShapeDtypeStruct((depth, width), jnp.float32),
+            jax.ShapeDtypeStruct((2 * side, width), jnp.float32),
+            jax.ShapeDtypeStruct((width, depth), jnp.bfloat16),
+            jax.ShapeDtypeStruct((width, depth), jnp.bfloat16),
+        ),
+        in_specs=[SMEM_SPEC] + [VMEM_SPEC] * len(inputs),
+        out_specs=(VMEM_SPEC,) * 5,
+        compiler_params=pltpu.CompilerParams(vmem_limit_bytes=24 << 20),
+        cost_estimate=pl.CostEstimate(
+            flops=4_000_000_000, bytes_accessed=4 * width * width * 4, transcendentals=0
+        ),
+        name="before_last",
+    )(flags, *inputs)
+
+
+def late_kernel(side, cut, flags_ref, *refs):
+    x_ref, shift_ref, direct_ref, onward_ref, second_ref, extra_ref, low_ref = refs[:7]
+    lasts, ready, refs = refs[7:11], refs[11:16], refs[16:]
+    partial_ref, schur_ref, coupling_ref = refs[:3]
+    buffer_ref, tile_ref, rest_ref, near_ref, far_ref, high_ref, less_ref, sems, outs = refs[3:]
+    left_refs = (high_ref, less_ref)
+    width = x_ref.shape[1]
+    rows = width - cut
+    copies = put_coupling(side, cut, lasts, x_ref, buffer_ref, left_refs, coupling_ref, sems)
+    own, above, second_above, under, second_under = [flags_ref[k] > 0 for k in range(5)]
+    for ref, given in zip((rest_ref, near_ref, far_ref), ready):
+        ref[...] = given[...]
+
+    def take_off(flag, place, targets):
+        number, begin, end = COUPLINGS[place]
+        height = (end - begin) * side
+
+        @pl.when(flag)
+        def _():
+            keep_halves(left_refs, lasts[number][...])
+
+            def put(lanes, value):
+                for ref, there, here, amount in targets:
+                    ref[there : there + amount, lanes] = (
+                        ref[there : there + amount, lanes] - value[here : here + amount]
+                    )
+
+            tall_product(
+                left_refs, height, rows, lambda lanes: buffer_ref[place, :, lanes], put, width
+            )
+
+    take_off(second_above, 0, ((rest_ref, 0, 0, side),))
+    take_off(above, 1, ((rest_ref, 0, 0, 2 * side), (near_ref, 0, side, side)))
+    take_off(under, 2, ((rest_ref, side, 0, 2 * side), (far_ref, 0, side, side)))
+    take_off(second_under, 3, ((rest_ref, 2 * side, 0, side), (near_ref, side, 0, side)))
+
     def put(place):
         copy = pltpu.make_async_copy(tile_ref.at[place], schur_ref.at[place], outs.at[place])
         copy.start()
         return copy
 
-    def fill(place, left, right_ref):
-        keep_halves(left_refs, left.T)
-
-        def put(lanes, value):
+    def fill(place, halved, depth, right_ref):
+        def store(lanes, value):
             tile_ref[place, :, lanes] = value
 
-        tall_product(
-            left_refs, width, left.shape[0], lambda lanes: right_ref[:, lanes], put, width
-        )
+        tall_product(halved, width, depth, lambda lanes: right_ref[:, lanes], store, width)
 
     def from_coupling(place, member):
         copy = pltpu.make_async_copy(
@@ -573,7 +616,7 @@
 
     @pl.when(jnp.logical_not(own))
     def _():
-        fill(2, x_ref[...], rest_ref)
+        fill(2, ready[3:], 3 * side, rest_ref)
         for i in range(width // TILE):
             rows = slice(i * TILE, (i + 1) * TILE)
             row = lax.broadcasted_iota(jnp.int32, (TILE, TILE), 0)
@@ -591,7 +634,8 @@
     @pl.when(jnp.logical_not(under))
     def _():
         below = direct_ref[...] + onward_ref[...]
-        fill(1, jnp.concatenate([below, extra_ref[...]], axis=0), near_ref)
+        keep_halves(left_refs, jnp.concatenate([below, extra_ref[...]], axis=0).T)
+        fill(1, left_refs, 3 * side, near_ref)
 
     copies.append(put(1))
 
@@ -601,19 +645,20 @@
 
     @pl.when(jnp.logical_not(second_under))
     def _():
-        fill(0, second_ref[...], far_ref)
+        keep_halves(left_refs, second_ref[...].T)
+        fill(0, left_refs, 2 * side, far_ref)
 
     copies.append(put(0))
     for copy in copies:
         copy.wait()
 
 
-def late(flags, x, shift, received, low, grams, mine, parts, partial, starts, side):
+def late(flags, x, shift, received, low, lasts, ready, partial, cut, side):
     depth, width = x.shape
-    rest = parts[-1][0].shape[1]
-    inputs = [x, shift, *received, low, *grams, *mine] + [piece for part in parts for piece in part]
+    rows = width - cut
+    inputs = [x, shift, *received, low, *lasts, *ready]
     return pl.pallas_call(
-        functools.partial(late_kernel, side, starts),
+        functools.partial(late_kernel, side, cut),
         out_shape=(
             jax.ShapeDtypeStruct((3, width, width), jnp.float32),
             jax.ShapeDtypeStruct((4, width, width), jnp.float32),
@@ -622,7 +667,7 @@
         out_specs=(ANY_SPEC, ANY_SPEC),
         input_output_aliases={1 + len(inputs): 1},
         scratch_shapes=[
-            pltpu.VMEM((4, rest, width), jnp.float32),
+            pltpu.VMEM((4, rows, width), jnp.float32),
             pltpu.VMEM((3, width, width), jnp.float32),
             pltpu.VMEM((depth, width), jnp.float32),
             pltpu.VMEM((depth, width), jnp.float32),
@@ -632,7 +677,7 @@
             pltpu.SemaphoreType.DMA((4,)),
             pltpu.SemaphoreType.DMA((3,)),
         ],
-        compiler_params=pltpu.CompilerParams(vmem_limit_bytes=40 << 20),
+        compiler_params=pltpu.CompilerParams(vmem_limit_bytes=34 << 20),
         cost_estimate=pl.CostEstimate(
             flops=12_000_000_000, bytes_accessed=7 * width * width * 4, transcendentals=0
         ),
@@ -684,17 +729,17 @@
     parts.append(sent_parts(part))
     grams = (passed_along(gram_one, 1), passed_along(gram_two, 2))
     partial = early(x, parts[:-1], starts[:-1], side)
+    ready = before_last(flags, x, grams, [part[1] for part in known], parts[:-1], side)
     schur, coupling = late(
         flags,
         x,
         levenberg_shift,
         (direct, onward, second, extra),
         low,
-        grams,
-        [part[1] for part in known],
-        parts,
+        parts[-1],
+        ready,
         partial,
-        starts,
+        starts[-1],
         side,
     )
     return schur[None], coupling[None]

time: 268 us -> 252 us (0.940)
  waiting for transfers between devices: 67.3 us -> 48.1 us
  Pallas kernels: 89 us -> 92.1 us
    ppermute x16, waiting for transfers between devices: 67.3 us -> 48.1 us  [passed_along(): return lax.ppermute(value, AXES, pairs)]
    pallas_call x1 -> x2, Pallas kernels: 21.4 us -> 24.4 us  [the longest x1 18.4 us: late(): pl.pallas_call(functools.partial(late_kernel, side, cut), out_shape=(jax....]
    unnamed x66 -> x56, local copies, waits for them, and re-layouts: 14 us -> 12.2 us
  transfers between devices with their start and end apart: 18 -> 18, of which waited for: 6 -> 6; matrix products, arithmetic and copies ran while one was open for 0% -> 0% of each run, Pallas kernels for 23% -> 27%
where the time goes in v5:
time: 252 us; the launch traced here: 248 us
  Pallas kernels  92.1 us (37%)
  blocking collectives  51.7 us (21%)
  waiting for transfers between devices  48.1 us (19%)
  starting transfers between devices  42.6 us (17%)
  local copies, waits for them, and re-layouts  12.8 us (5%)
    all_to_all x1, blocking collectives, local(): lax.all_to_all(chunks, AXES, split_axis=0, concat_axis=0, tiled=True)  51.7 us
    pallas_call x3, Pallas kernels, factored_part(): pl.pallas_call(functools.partial(part_kernel, side, bounds, number), out_...  50.7 us
    ppermute x16, waiting for transfers between devices, passed_along(): return lax.ppermute(value, AXES, pairs)  48.1 us
    ppermute x16, starting transfers between devices, passed_along(): return lax.ppermute(value, AXES, pairs)  39 us
    pallas_call x1, Pallas kernels, late(): pl.pallas_call(functools.partial(late_kernel, side, cut), out_shape=(jax....  18.4 us
    unnamed x56, local copies, waits for them, and re-layouts  12.2 us
    pallas_call x1, Pallas kernels, early(): pl.pallas_call(functools.partial(early_kernel, side, starts), out_shape=j...  11.3 us
    pallas_call x1, Pallas kernels, before_last(): pl.pallas_call(functools.partial(before_kernel, side), out_shape=(jax.Sha...  6.03 us
  transfers between devices with their start and end apart: 18, of which 6 were waited for; matrix products, arithmetic and copies ran while one was open for 0% of the time, Pallas kernels for 27%

profile of v5, /device:TPU:0, one launch (start us, length us, event | category | flops | bytes accessed | tf_op | source)
XLA Modules:
  0.0 248.4 jit_solution(13334823665038651847)
XLA Ops:
  0.6 4.1 %bucket.1 = f32[32,54,256]{2,1,0:T(8,128)} custom-call(s32[1,128]{1,0:T(1,128)} %bitcast.5, f32[3,128,768]{2,1,0:T(8,128)} %bitcast.4), custom_call_target="tpu_custom_call" | custom-call | tf_op jit(solution)/shard_map/bucket/pallas_call | solution.py:85
  4.8 51.7 %all_to_all.5.in_ref = f32[32,54,256]{2,1,0:T(8,128)S(1)} all-to-all(f32[32,54,256]{2,1,0:T(8,128)} %bucket.1), channel_id=1, replica_groups=mesh['gx'=4,'gy'=8] {'gx','gy'}, dimensions={0} | all-to-all | bytes 3538944 | tf_op jit(solution)/shard_map/all_to_all | solution.py:705
  56.4 1.5 regroup.1
  58.5 18.3 %factor_part.3 = (f32[768,768]{1,0:T(8,128)S(1)}, f32[384,256]{1,0:T(8,128)}, f32[384,256]{1,0:T(8,128)}, f32[192,256]{1,0:T(8,128)S(1)}, f32[192,256]{1,0:T(8,128)S(1)}) custom-call(f32[576,768]{1,0:T(8,128)S(1)} %get-tuple-element.29.refs_0_.x_ref, f32[1,768]{1,0:T(1,128)S(1)} %copy-done.24), custom_call_target="tpu_custom_call" | custom-call | flops 20000000000 | bytes 5308416 | tf_op jit(solution)/shard_map/factor_part/pallas_call | solution.py:384
  76.8 16.1 %factor_part.4 = (f32[768,768]{1,0:T(8,128)S(1)}, f32[384,256]{1,0:T(8,128)}, f32[384,256]{1,0:T(8,128)}, f32[192,256]{1,0:T(8,128)S(1)}, f32[192,256]{1,0:T(8,128)S(1)}) custom-call(f32[576,768]{1,0:T(8,128)S(1)} %get-tuple-element.29.refs_0_.x_ref, f32[768,768]{1,0:T(8,128)S(1)} %get-tuple-element.32.refs_1_, f32[384,256]{1,0:T(8,128)} %get-tuple-element.33.refs_2_, ...), custom_call_target="tpu_custom_call" | custom-call | flops 20000000000 | bytes 5308416 | tf_op jit(solution)/shard_map/factor_part/pallas_call | solution.py:384
  93.0 16.3 %factor_part.5 = (f32[768,768]{1,0:T(8,128)S(1)}, f32[384,256]{1,0:T(8,128)S(1)}, f32[384,256]{1,0:T(8,128)S(1)}, f32[192,256]{1,0:T(8,128)S(1)}, f32[192,256]{1...) custom-call(f32[576,768]{1,0:T(8,128)S(1)} %get-tuple-element.29.refs_0_.x_ref, ...), custom_call_target="tpu_custom_call" | custom-call | flops 20000000000 | bytes 5308416 | tf_op jit(solution)/shard_map/factor_part/pallas_call | solution.py:384
  110.8 1.4 copy-done.25
  112.2 1.6 collective-permute-start.9
  113.8 2.8 %collective-permute-start.13 = (f32[192,256]{1,0:T(8,128)S(1)}, f32[192,256]{1,0:T(8,128)S(1)}, u32[]{:S(2)}, u32[]{:S(2)}) collective-permute-start(f32[192,256]{1,0:T(8,128)S(1)} %get-tuple-element.34.refs_3_), channel_id=1, source_target_pairs={{0,30},{1,31},{2,0},{3,1},{4,2},{5,3},{6,4},{7,5},{8,6},{9,7},{10,... | collective-permute-start | bytes 589832 | tf_op jit(solution)/shard_map/ppermute | solution.py:29
  116.6 5.4 %collective-permute-done.9.gram_two_ref = f32[192,192]{1,0:T(8,128)S(1)} collective-permute-done((f32[192,192]{1,0:T(8,128)S(1)}, f32[192,192]{1,0:T(8,128)S(1)}, u32[]{:S(2)}, u32[]{:S(2)}) %collective-permute-start.9) | collective-permute-done | bytes 147488 | tf_op jit(solution)/shard_map/ppermute | solution.py:29
  122.7 5.2 %collective-permute-start.17 = (f32[192,256]{1,0:T(8,128)S(1)}, f32[192,256]{1,0:T(8,128)S(1)}, u32[]{:S(2)}, u32[]{:S(2)}) collective-permute-start(f32[192,256]{1,0:T(8,128)S(1)} %get-tuple-element.37.refs_5_), channel_id=1, source_target_pairs={{0,30},{1,31},{2,0},{3,1},{4,2},{5,3},{6,4},{7,5},{8,6},{9,7},{10,... | collective-permute-start | bytes 589832 | tf_op jit(solution)/shard_map/ppermute | solution.py:29
  130.8 4.4 %collective-permute-start.7 = (f32[192,256]{1,0:T(8,128)S(1)}, f32[192,256]{1,0:T(8,128)S(1)}, u32[]{:S(2)}, u32[]{:S(2)}) collective-permute-start(f32[192,256]{1,0:T(8,128)S(1)} %get-tuple-element.42), channel_id=1, source_target_pairs={{0,30},{1,31},{2,0},{3,1},{4,2},{5,3},{6,4},{7,5},{8,6},{9,7},{10,... | collective-permute-start | bytes 589832 | tf_op jit(solution)/shard_map/ppermute | solution.py:29
  135.9 2.8 %collective-permute-start.11 = (f32[384,256]{1,0:T(8,128)}, f32[384,256]{1,0:T(8,128)}, u32[]{:S(2)}, u32[]{:S(2)}) collective-permute-start(f32[384,256]{1,0:T(8,128)} %get-tuple-element.45.refs_0_), channel_id=1, source_target_pairs={{0,31},{1,0},{2,1},{3,2},{4,3},{5,4},{6,5},{7,6},{8,7},{9,8},{10,9... | collective-permute-start | bytes 1179656 | tf_op jit(solution)/shard_map/ppermute | solution.py:29
  140.1 7.0 %collective-permute-start.10 = (f32[384,256]{1,0:T(8,128)}, f32[384,256]{1,0:T(8,128)}, u32[]{:S(2)}, u32[]{:S(2)}) collective-permute-start(f32[384,256]{1,0:T(8,128)} %get-tuple-element.33.refs_2_), channel_id=1, source_target_pairs={{0,1},{1,2},{2,3},{3,4},{4,5},{5,6},{6,7},{7,8},{8,9},{9,10},{10,1... | collective-permute-start | bytes 1179656 | tf_op jit(solution)/shard_map/ppermute | solution.py:29
  147.7 2.1 collective-permute-start.14
  150.5 3.3 %collective-permute-start.15 = (f32[384,256]{1,0:T(8,128)}, f32[384,256]{1,0:T(8,128)}, u32[]{:S(2)}, u32[]{:S(2)}) collective-permute-start(f32[384,256]{1,0:T(8,128)} %get-tuple-element.46.refs_1_), channel_id=1, source_target_pairs={{0,31},{1,0},{2,1},{3,2},{4,3},{5,4},{6,5},{7,6},{8,7},{9,8},{10,9... | collective-permute-start | bytes 1179656 | tf_op jit(solution)/shard_map/ppermute | solution.py:29
  153.8 2.3 collective-permute-start
  156.2 1.3 collective-permute-start.2
  158.1 8.5 %collective-permute-done.10.refs_3_.refs_0_ = f32[384,256]{1,0:T(8,128)} collective-permute-done((f32[384,256]{1,0:T(8,128)}, f32[384,256]{1,0:T(8,128)}, u32[]{:S(2)}, u32[]{:S(2)}) %collective-permute-start.10) | collective-permute-done | bytes 393248 | tf_op jit(solution)/shard_map/ppermute | solution.py:29
  166.6 2.5 collective-permute-start.3
  169.1 5.9 %collective-permute-done.14.refs_7_.refs_4_ = f32[384,256]{1,0:T(8,128)} collective-permute-done((f32[384,256]{1,0:T(8,128)}, f32[384,256]{1,0:T(8,128)}, u32[]{:S(2)}, u32[]{:S(2)}) %collective-permute-start.14) | collective-permute-done | bytes 393248 | tf_op jit(solution)/shard_map/ppermute | solution.py:29
  175.1 2.5 collective-permute-start.4
  177.5 18.6 %collective-permute-done.15.refs_8_.refs_5_ = f32[384,256]{1,0:T(8,128)} collective-permute-done((f32[384,256]{1,0:T(8,128)}, f32[384,256]{1,0:T(8,128)}, u32[]{:S(2)}, u32[]{:S(2)}) %collective-permute-start.15) | collective-permute-done | bytes 393248 | tf_op jit(solution)/shard_map/ppermute | solution.py:29
  196.2 3.5 %collective-permute-start.5 = (f32[384,256]{1,0:T(8,128)}, f32[384,256]{1,0:T(8,128)S(1)}, u32[]{:S(2)}, u32[]{:S(2)}) collective-permute-start(f32[384,256]{1,0:T(8,128)} %copy-done.1), channel_id=1, source_target_pairs={{0,31},{1,0},{2,1},{3,2},{4,3},{5,4},{6,5},{7,6},{8,7},{9,8},{10,9... | collective-permute-start | bytes 1179656 | tf_op jit(solution)/shard_map/ppermute | solution.py:29
  199.7 0.9 copy-done.7
  200.6 0.9 copy-done.14
  201.5 0.9 copy-done.19
  202.5 0.9 copy-done.22
  203.4 11.3 %early.1.refs_16_ = f32[4,768,768]{2,1,0:T(8,128)} custom-call(f32[576,768]{1,0:T(8,128)S(1)} %get-tuple-element.29.refs_0_.x_ref, f32[384,256]{1,0:T(8,128)} %collective-permute-done.10.refs_3_.refs_0_, f32[384,256]{1,0:T(8,128)} %collective-permute-done.11.refs_4_.refs_1_, f32[192,256]{1,0:T(8,128)S(1)} %copy-done.7, f32[192,256]{1,0:T(8,128)S(1)} %copy-done.14, ...), custom_call_target="tpu_custom_call" | custom-call | flops 8000000000 | bytes 9437184 | tf_op jit(solution)/shard_map/early/pallas_call | solution.py:456
  214.9 6.0 %before_last.1 = (f32[576,768]{1,0:T(8,128)S(1)}, f32[576,768]{1,0:T(8,128)S(1)}, f32[384,768]{1,0:T(8,128)S(1)}, bf16[768,576]{1,0:T(8,128)(2,1)S(1)}, bf16[768,576]{1,0:T(8,128)(2,1)S(1)}) custom-call(s32[5]{0:T(128)S(1)} %gather_fusion, f32[576,768]{1,0:T(8,128)S(1)} %get-tuple-element.29.refs_0_.x_ref, f32[192,384]{1,0:T(8,128)S(1)} %copy-done.5, ...), custom_call_target="tpu_custom_call" | custom-call | flops 4000000000 | bytes 9437184 | tf_op jit(solution)/shard_map/before_last/pallas_call | solution.py:537
  220.9 8.9 %collective-permute-done.4.refs_7_ = f32[384,256]{1,0:T(8,128)S(1)} collective-permute-done((f32[384,256]{1,0:T(8,128)}, f32[384,256]{1,0:T(8,128)S(1)}, u32[]{:S(2)}, u32[]{:S(2)}) %collective-permute-start.4) | collective-permute-done | bytes 393248 | tf_op jit(solution)/shard_map/ppermute | solution.py:29
  229.8 18.4 %late.1 = (f32[3,768,768]{2,1,0:T(8,128)}, f32[4,768,768]{2,1,0:T(8,128)}) custom-call(s32[5]{0:T(128)S(1)} %gather_fusion, f32[576,768]{1,0:T(8,128)S(1)} %get-tuple-element.29.refs_0_.x_ref, f32[1,768]{1,0:T(1,128)S(1)} %copy-done.24, f32[384,768]{1,0:T(8,128)} %collective-permute-done.refs_2_, ...), custom_call_target="tpu_custom_call", output_to_operand_aliasing={{1}: (17, {})} | custom-call | flops 12000000000 | bytes 16515072 | tf_op jit(solution)/shard_map/late/pallas_call | solution.py:660
  (72 shorter events, 9.9 us)
Async XLA Ops:
  0.6 156.8 %copy-start = (s32[32]{0:T(128)S(1)}, s32[32]{0:T(128)}, u32[]{:S(2)}) copy-start(s32[32]{0:T(128)} %param.8) | copy-start | bytes 388
  56.4 2.1 copy-start.24
  57.9 98.2 %collective-permute-start.1 = (f32[384,768]{1,0:T(8,128)}, f32[384,768]{1,0:T(8,128)S(1)}, u32[]{:S(2)}, u32[]{:S(2)}) collective-permute-start(f32[384,768]{1,0:T(8,128)} %get-tuple-element.30), channel_id=1, source_target_pairs={{0,2},{1,3},{2,4},{3,5},{4,6},{5,7},{6,8},{7,9},{8,10},{9,11},{10,... | collective-permute-start | bytes 3538952 | tf_op jit(solution)/shard_map/ppermute | solution.py:29
  76.8 51.1 %collective-permute-start.12 = (f32[192,256]{1,0:T(8,128)S(1)}, f32[192,256]{1,0:T(8,128)S(1)}, u32[]{:S(2)}, u32[]{:S(2)}) collective-permute-start(f32[192,256]{1,0:T(8,128)S(1)} %get-tuple-element.47), channel_id=1, source_target_pairs={{0,2},{1,3},{2,4},{3,5},{4,6},{5,7},{6,8},{7,9},{8,10},{9,11},{10,... | collective-permute-start | bytes 589832 | tf_op jit(solution)/shard_map/ppermute | solution.py:29
  93.0 60.8 %copy-start.27 = (s32[5]{0:T(128)S(1)}, s32[5]{0:T(128)}, u32[]{:S(2)}) copy-start(s32[5]{0:T(128)} %constant.29.clone) | copy-start | bytes 64
  110.8 1.4 copy-start.25
  112.2 9.9 %collective-permute-start.9 = (f32[192,192]{1,0:T(8,128)S(1)}, f32[192,192]{1,0:T(8,128)S(1)}, u32[]{:S(2)}, u32[]{:S(2)}) collective-permute-start(f32[192,192]{1,0:T(8,128)S(1)} %get-tuple-element.44), channel_id=1, source_target_pairs={{0,2},{1,3},{2,4},{3,5},{4,6},{5,7},{6,8},{7,9},{8,10},{9,11},{10,... | collective-permute-start | bytes 442376 | tf_op jit(solution)/shard_map/ppermute | solution.py:29
  113.8 15.6 %collective-permute-start.13 = (f32[192,256]{1,0:T(8,128)S(1)}, f32[192,256]{1,0:T(8,128)S(1)}, u32[]{:S(2)}, u32[]{:S(2)}) collective-permute-start(f32[192,256]{1,0:T(8,128)S(1)} %get-tuple-element.34.refs_3_), channel_id=1, source_target_pairs={{0,30},{1,31},{2,0},{3,1},{4,2},{5,3},{6,4},{7,5},{8,6},{9,7},{10,... | collective-permute-start | bytes 589832 | tf_op jit(solution)/shard_map/ppermute | solution.py:29
  116.6 13.5 %collective-permute-start.16 = (f32[192,256]{1,0:T(8,128)S(1)}, f32[192,256]{1,0:T(8,128)S(1)}, u32[]{:S(2)}, u32[]{:S(2)}) collective-permute-start(f32[192,256]{1,0:T(8,128)S(1)} %get-tuple-element.48), channel_id=1, source_target_pairs={{0,2},{1,3},{2,4},{3,5},{4,6},{5,7},{6,8},{7,9},{8,10},{9,11},{10,... | collective-permute-start | bytes 589832 | tf_op jit(solution)/shard_map/ppermute | solution.py:29
  122.7 12.5 %collective-permute-start.17 = (f32[192,256]{1,0:T(8,128)S(1)}, f32[192,256]{1,0:T(8,128)S(1)}, u32[]{:S(2)}, u32[]{:S(2)}) collective-permute-start(f32[192,256]{1,0:T(8,128)S(1)} %get-tuple-element.37.refs_5_), channel_id=1, source_target_pairs={{0,30},{1,31},{2,0},{3,1},{4,2},{5,3},{6,4},{7,5},{8,6},{9,7},{10,... | collective-permute-start | bytes 589832 | tf_op jit(solution)/shard_map/ppermute | solution.py:29
  128.6 21.2 %collective-permute-start.8 = (f32[192,384]{1,0:T(8,128)S(1)}, f32[192,384]{1,0:T(8,128)S(1)}, u32[]{:S(2)}, u32[]{:S(2)}) collective-permute-start(f32[192,384]{1,0:T(8,128)S(1)} %get-tuple-element.43), channel_id=1, source_target_pairs={{0,1},{1,2},{2,3},{3,4},{4,5},{5,6},{6,7},{7,8},{8,9},{9,10},{10,1... | collective-permute-start | bytes 884744 | tf_op jit(solution)/shard_map/ppermute | solution.py:29
  130.1 9.3 %collective-permute-start.6 = (f32[192,256]{1,0:T(8,128)S(1)}, f32[192,256]{1,0:T(8,128)S(1)}, u32[]{:S(2)}, u32[]{:S(2)}) collective-permute-start(f32[192,256]{1,0:T(8,128)S(1)} %get-tuple-element.41), channel_id=1, source_target_pairs={{0,2},{1,3},{2,4},{3,5},{4,6},{5,7},{6,8},{7,9},{8,10},{9,11},{10,... | collective-permute-start | bytes 589832 | tf_op jit(solution)/shard_map/ppermute | solution.py:29
  130.8 16.3 %collective-permute-start.7 = (f32[192,256]{1,0:T(8,128)S(1)}, f32[192,256]{1,0:T(8,128)S(1)}, u32[]{:S(2)}, u32[]{:S(2)}) collective-permute-start(f32[192,256]{1,0:T(8,128)S(1)} %get-tuple-element.42), channel_id=1, source_target_pairs={{0,30},{1,31},{2,0},{3,1},{4,2},{5,3},{6,4},{7,5},{8,6},{9,7},{10,... | collective-permute-start | bytes 589832 | tf_op jit(solution)/shard_map/ppermute | solution.py:29
  135.9 17.9 %collective-permute-start.11 = (f32[384,256]{1,0:T(8,128)}, f32[384,256]{1,0:T(8,128)}, u32[]{:S(2)}, u32[]{:S(2)}) collective-permute-start(f32[384,256]{1,0:T(8,128)} %get-tuple-element.45.refs_0_), channel_id=1, source_target_pairs={{0,31},{1,0},{2,1},{3,2},{4,3},{5,4},{6,5},{7,6},{8,7},{9,8},{10,9... | collective-permute-start | bytes 1179656 | tf_op jit(solution)/shard_map/ppermute | solution.py:29
  140.1 26.5 %collective-permute-start.10 = (f32[384,256]{1,0:T(8,128)}, f32[384,256]{1,0:T(8,128)}, u32[]{:S(2)}, u32[]{:S(2)}) collective-permute-start(f32[384,256]{1,0:T(8,128)} %get-tuple-element.33.refs_2_), channel_id=1, source_target_pairs={{0,1},{1,2},{2,3},{3,4},{4,5},{5,6},{6,7},{7,8},{8,9},{9,10},{10,1... | collective-permute-start | bytes 1179656 | tf_op jit(solution)/shard_map/ppermute | solution.py:29
  147.7 27.3 %collective-permute-start.14 = (f32[384,256]{1,0:T(8,128)}, f32[384,256]{1,0:T(8,128)}, u32[]{:S(2)}, u32[]{:S(2)}) collective-permute-start(f32[384,256]{1,0:T(8,128)} %get-tuple-element.36.refs_4_), channel_id=1, source_target_pairs={{0,1},{1,2},{2,3},{3,4},{4,5},{5,6},{6,7},{7,8},{8,9},{9,10},{10,1... | collective-permute-start | bytes 1179656 | tf_op jit(solution)/shard_map/ppermute | solution.py:29
  150.5 45.6 %collective-permute-start.15 = (f32[384,256]{1,0:T(8,128)}, f32[384,256]{1,0:T(8,128)}, u32[]{:S(2)}, u32[]{:S(2)}) collective-permute-start(f32[384,256]{1,0:T(8,128)} %get-tuple-element.46.refs_1_), channel_id=1, source_target_pairs={{0,31},{1,0},{2,1},{3,2},{4,3},{5,4},{6,5},{7,6},{8,7},{9,8},{10,9... | collective-permute-start | bytes 1179656 | tf_op jit(solution)/shard_map/ppermute | solution.py:29
  153.8 75.9 %collective-permute-start = (f32[384,768]{1,0:T(8,128)}, f32[384,768]{1,0:T(8,128)}, u32[]{:S(2)}, u32[]{:S(2)}) collective-permute-start(f32[384,768]{1,0:T(8,128)} %get-tuple-element.30), channel_id=1, source_target_pairs={{0,1},{2,3},{4,5},{6,7},{8,9},{10,11},{12,13},{14,15},{16,17},{18,... | collective-permute-start | bytes 3538952 | tf_op jit(solution)/shard_map/ppermute | solution.py:711
  156.2 73.6 %collective-permute-start.2 = (f32[384,768]{1,0:T(8,128)S(1)}, f32[384,768]{1,0:T(8,128)}, u32[]{:S(2)}, u32[]{:S(2)}) collective-permute-start(f32[384,768]{1,0:T(8,128)S(1)} %collective-permute-done.1.refs_4_), channel_id=1, source_target_pairs={{1,0},{3,2},{5,4},{7,6},{9,8},{11,10},{13,12},{15,14},{17,16},{19,... | collective-permute-start | bytes 3538952 | tf_op jit(solution)/shard_map/ppermute | solution.py:725
  166.6 63.1 %collective-permute-start.3 = (f32[192,768]{1,0:T(8,128)S(1)}, f32[192,768]{1,0:T(8,128)S(1)}, u32[]{:S(2)}, u32[]{:S(2)}) collective-permute-start(f32[192,768]{1,0:T(8,128)S(1)} %get-tuple-element.31), channel_id=1, source_target_pairs={{0,1},{1,2},{2,3},{3,4},{4,5},{5,6},{6,7},{7,8},{8,9},{9,10},{10,1... | collective-permute-start | bytes 1769480 | tf_op jit(solution)/shard_map/ppermute | solution.py:29
  175.1 54.7 %collective-permute-start.4 = (f32[384,256]{1,0:T(8,128)}, f32[384,256]{1,0:T(8,128)S(1)}, u32[]{:S(2)}, u32[]{:S(2)}) collective-permute-start(f32[384,256]{1,0:T(8,128)} %copy-done.3), channel_id=1, source_target_pairs={{0,1},{1,2},{2,3},{3,4},{4,5},{5,6},{6,7},{7,8},{8,9},{9,10},{10,1... | collective-permute-start | bytes 1179656 | tf_op jit(solution)/shard_map/ppermute | solution.py:29
  196.2 18.6 %copy-start.2 = (f32[384,256]{1,0:T(8,128)S(1)}, f32[384,256]{1,0:T(8,128)}, u32[]{:S(2)}) copy-start(f32[384,256]{1,0:T(8,128)} %copy-done.1) | copy-start | bytes 1179652
  196.2 18.6 %copy-start.5 = (f32[192,384]{1,0:T(8,128)S(1)}, f32[192,384]{1,0:T(8,128)}, u32[]{:S(2)}) copy-start(f32[192,384]{1,0:T(8,128)} %copy-done.4) | copy-start | bytes 884740
  196.2 33.6 %collective-permute-start.5 = (f32[384,256]{1,0:T(8,128)}, f32[384,256]{1,0:T(8,128)S(1)}, u32[]{:S(2)}, u32[]{:S(2)}) collective-permute-start(f32[384,256]{1,0:T(8,128)} %copy-done.1), channel_id=1, source_target_pairs={{0,31},{1,0},{2,1},{3,2},{4,3},{5,4},{6,5},{7,6},{8,7},{9,8},{10,9... | collective-permute-start | bytes 1179656 | tf_op jit(solution)/shard_map/ppermute | solution.py:29
  203.4 11.4 %copy-start.8 = (f32[192,256]{1,0:T(8,128)S(1)}, f32[192,256]{1,0:T(8,128)}, u32[]{:S(2)}) copy-start(f32[192,256]{1,0:T(8,128)} %copy-done.6) | copy-start | bytes 589828
  203.4 11.4 %copy-start.12 = (f32[192,192]{1,0:T(8,128)S(1)}, f32[192,192]{1,0:T(8,128)}, u32[]{:S(2)}) copy-start(f32[192,192]{1,0:T(8,128)} %copy-done.11) | copy-start | bytes 442372
  203.4 11.4 %copy-start.15 = (f32[192,256]{1,0:T(8,128)S(1)}, f32[192,256]{1,0:T(8,128)}, u32[]{:S(2)}) copy-start(f32[192,256]{1,0:T(8,128)} %copy-done.13) | copy-start | bytes 589828
  203.4 11.4 %copy-start.20 = (f32[192,256]{1,0:T(8,128)S(1)}, f32[192,256]{1,0:T(8,128)}, u32[]{:S(2)}) copy-start(f32[192,256]{1,0:T(8,128)} %copy-done.18) | copy-start | bytes 589828
  203.4 11.4 %copy-start.23 = (f32[192,256]{1,0:T(8,128)S(1)}, f32[192,256]{1,0:T(8,128)}, u32[]{:S(2)}) copy-start(f32[192,256]{1,0:T(8,128)} %copy-done.21) | copy-start | bytes 589828
  214.8 14.9 %copy-start.10 = (f32[192,256]{1,0:T(8,128)S(1)}, f32[192,256]{1,0:T(8,128)}, u32[]{:S(2)}) copy-start(f32[192,256]{1,0:T(8,128)} %copy-done.9) | copy-start | bytes 589828
  214.8 14.9 %copy-start.17 = (f32[192,256]{1,0:T(8,128)S(1)}, f32[192,256]{1,0:T(8,128)}, u32[]{:S(2)}) copy-start(f32[192,256]{1,0:T(8,128)} %copy-done.16) | copy-start | bytes 589828
  214.8 14.9 %copy-start.26 = (f32[768,768]{1,0:T(8,128)S(1)}, f32[768,768]{1,0:T(8,128)}, u32[]{:S(2)}) copy-start(f32[768,768]{1,0:T(8,128)} %copy-done.25) | copy-start | bytes 7077892
  (14 other events, 10.7 us)

commit v6 on v5

--- a/solution.py
+++ b/solution.py
@@ -402,15 +402,17 @@
 COUPLINGS = ((3, 0, 1), (1, 0, 2), (0, 1, 3), (2, 2, 3))
 
 
-def put_coupling(side, start, y_refs, x_ref, buffer_ref, left_refs, out_ref, sems):
+def put_coupling(side, start, y_refs, x_ref, buffer_ref, left_refs, out_ref, sems, places=range(4)):
     rows = buffer_ref.shape[1]
     width = x_ref.shape[1]
     copies = []
-    for place, (number, begin, end) in enumerate(COUPLINGS):
+    for place in places:
+        number, begin, end = COUPLINGS[place]
+        slot = place % buffer_ref.shape[0]
         keep_halves(left_refs, y_refs[number][...].T)
 
-        def put(lanes, value, place=place):
-            buffer_ref[place, :, lanes] = value
+        def put(lanes, value, slot=slot):
+            buffer_ref[slot, :, lanes] = value
 
         tall_product(
             left_refs,
@@ -421,7 +423,7 @@
             width,
         )
         copy = pltpu.make_async_copy(
-            buffer_ref.at[place], out_ref.at[place, pl.ds(start, rows), :], sems.at[place]
+            buffer_ref.at[slot], out_ref.at[place, pl.ds(start, rows), :], sems.at[place]
         )
         copy.start()
         copies.append(copy)
@@ -554,15 +556,17 @@
 
 
 def late_kernel(side, cut, flags_ref, *refs):
-    x_ref, shift_ref, direct_ref, onward_ref, second_ref, extra_ref, low_ref = refs[:7]
-    lasts, ready, refs = refs[7:11], refs[11:16], refs[16:]
-    partial_ref, schur_ref, coupling_ref = refs[:3]
-    buffer_ref, tile_ref, rest_ref, near_ref, far_ref, high_ref, less_ref, sems, outs = refs[3:]
+    x_ref, shift_ref, second_ref, low_ref = refs[:4]
+    lasts, ready, refs = (refs[4], None, *refs[5:7]), refs[7:12], refs[12:]
+    partial_ref, schur_ref, coupling_ref, near_ref = refs[:4]
+    buffer_ref, tile_ref, rest_ref, far_ref, high_ref, less_ref, sems, outs = refs[4:]
     left_refs = (high_ref, less_ref)
     width = x_ref.shape[1]
     rows = width - cut
-    copies = put_coupling(side, cut, lasts, x_ref, buffer_ref, left_refs, coupling_ref, sems)
-    own, above, second_above, under, second_under = [flags_ref[k] > 0 for k in range(5)]
+    copies = put_coupling(
+        side, cut, lasts, x_ref, buffer_ref, left_refs, coupling_ref, sems, (0, 3, 2)
+    )
+    own, _, second_above, under, second_under = [flags_ref[k] > 0 for k in range(5)]
     for ref, given in zip((rest_ref, near_ref, far_ref), ready):
         ref[...] = given[...]
 
@@ -585,14 +589,11 @@
             )
 
     take_off(second_above, 0, ((rest_ref, 0, 0, side),))
-    take_off(above, 1, ((rest_ref, 0, 0, 2 * side), (near_ref, 0, side, side)))
     take_off(under, 2, ((rest_ref, side, 0, 2 * side), (far_ref, 0, side, side)))
     take_off(second_under, 3, ((rest_ref, 2 * side, 0, side), (near_ref, side, 0, side)))
 
     def put(place):
-        copy = pltpu.make_async_copy(tile_ref.at[place], schur_ref.at[place], outs.at[place])
-        copy.start()
-        return copy
+        return pltpu.make_async_copy(tile_ref.at[place], schur_ref.at[place], outs.at[place])
 
     def fill(place, halved, depth, right_ref):
         def store(lanes, value):
@@ -625,19 +626,15 @@
                 row == col, jnp.broadcast_to(shift_ref[:, rows], (TILE, TILE)), 0.0
             )
 
-    copies.append(put(2))
+    put(2).start()
 
     @pl.when(under)
     def _():
         from_coupling(1, 2)
 
-    @pl.when(jnp.logical_not(under))
-    def _():
-        below = direct_ref[...] + onward_ref[...]
-        keep_halves(left_refs, jnp.concatenate([below, extra_ref[...]], axis=0).T)
-        fill(1, left_refs, 3 * side, near_ref)
-
-    copies.append(put(1))
+    @pl.when(under)
+    def _():
+        put(1).start()
 
     @pl.when(second_under)
     def _():
@@ -648,28 +645,35 @@
         keep_halves(left_refs, second_ref[...].T)
         fill(0, left_refs, 2 * side, far_ref)
 
-    copies.append(put(0))
+    put(0).start()
+
+    @pl.when(under)
+    def _():
+        put(1).wait()
+
+    put(2).wait()
+    put(0).wait()
     for copy in copies:
         copy.wait()
 
 
-def late(flags, x, shift, received, low, lasts, ready, partial, cut, side):
+def late(flags, x, shift, second, low, lasts, ready, partial, cut, side):
     depth, width = x.shape
     rows = width - cut
-    inputs = [x, shift, *received, low, *lasts, *ready]
+    inputs = [x, shift, second, low, lasts[0], *lasts[2:], *ready]
     return pl.pallas_call(
         functools.partial(late_kernel, side, cut),
         out_shape=(
             jax.ShapeDtypeStruct((3, width, width), jnp.float32),
             jax.ShapeDtypeStruct((4, width, width), jnp.float32),
+            jax.ShapeDtypeStruct((depth, width), jnp.float32),
         ),
         in_specs=[SMEM_SPEC] + [VMEM_SPEC] * len(inputs) + [ANY_SPEC],
-        out_specs=(ANY_SPEC, ANY_SPEC),
+        out_specs=(ANY_SPEC, ANY_SPEC, VMEM_SPEC),
         input_output_aliases={1 + len(inputs): 1},
         scratch_shapes=[
             pltpu.VMEM((4, rows, width), jnp.float32),
             pltpu.VMEM((3, width, width), jnp.float32),
-            pltpu.VMEM((depth, width), jnp.float32),
             pltpu.VMEM((depth, width), jnp.float32),
             pltpu.VMEM((2 * side, width), jnp.float32),
             pltpu.VMEM((width, depth), jnp.bfloat16),
@@ -683,6 +687,101 @@
         ),
         name="late",
     )(flags, *inputs, partial)
+
+
+def final_kernel(side, flags_ref, x_ref, direct_ref, onward_ref, extra_ref, y_ref, given_ref, *refs):
+    tiles_ref, _, schur_ref, coupling_ref = refs[:4]
+    buffer_ref, tile_ref, near_ref, high_ref, less_ref, sems, ins, outs = refs[4:]
+    left_refs = (high_ref, less_ref)
+    rows, width = buffer_ref.shape[1:]
+    above, under = flags_ref[1] > 0, flags_ref[3] > 0
+    taken = pltpu.make_async_copy(tiles_ref.at[2], tile_ref.at[1], ins)
+    back = pltpu.make_async_copy(tile_ref.at[1], schur_ref.at[2], outs.at[1])
+    beside = pltpu.make_async_copy(tile_ref.at[0], schur_ref.at[1], outs.at[0])
+
+    @pl.when(above)
+    def _():
+        taken.start()
+
+    copies = put_coupling(
+        side,
+        width - rows,
+        (None, y_ref, None, None),
+        x_ref,
+        buffer_ref,
+        left_refs,
+        coupling_ref,
+        sems,
+        (1,),
+    )
+    near_ref[...] = given_ref[...]
+
+    @pl.when(above)
+    def _():
+        keep_halves(left_refs, y_ref[side:, :])
+
+        def put_near(lanes, value):
+            near_ref[:side, lanes] = near_ref[:side, lanes] - value
+
+        tall_product(left_refs, side, rows, lambda lanes: buffer_ref[0, :, lanes], put_near, width)
+        keep_halves(left_refs, buffer_ref[0].T)
+        taken.wait()
+
+        def put_diag(lanes, value):
+            tile_ref[1, :, lanes] = tile_ref[1, :, lanes] - value
+
+        tall_product(left_refs, width, rows, lambda lanes: buffer_ref[0, :, lanes], put_diag, width)
+        back.start()
+
+    @pl.when(jnp.logical_not(under))
+    def _():
+        below = direct_ref[...] + onward_ref[...]
+        keep_halves(left_refs, jnp.concatenate([below, extra_ref[...]], axis=0).T)
+
+        def put_beside(lanes, value):
+            tile_ref[0, :, lanes] = value
+
+        tall_product(left_refs, width, 3 * side, lambda lanes: near_ref[:, lanes], put_beside, width)
+        beside.start()
+        beside.wait()
+
+    @pl.when(above)
+    def _():
+        back.wait()
+
+    for copy in copies:
+        copy.wait()
+
+
+def final(flags, x, received, y, near, tiles, coupling, side):
+    depth, width = x.shape
+    rows = y.shape[1]
+    inputs = [x, *received, y, near]
+    return pl.pallas_call(
+        functools.partial(final_kernel, side),
+        out_shape=(
+            jax.ShapeDtypeStruct((3, width, width), jnp.float32),
+            jax.ShapeDtypeStruct((4, width, width), jnp.float32),
+        ),
+        in_specs=[SMEM_SPEC] + [VMEM_SPEC] * len(inputs) + [ANY_SPEC] * 2,
+        out_specs=(ANY_SPEC, ANY_SPEC),
+        input_output_aliases={1 + len(inputs): 0, 2 + len(inputs): 1},
+        scratch_shapes=[
+            pltpu.VMEM((1, rows, width), jnp.float32),
+            pltpu.VMEM((2, width, width), jnp.float32),
+            pltpu.VMEM((depth, width), jnp.float32),
+            pltpu.VMEM((width, depth), jnp.bfloat16),
+            pltpu.VMEM((width, depth), jnp.bfloat16),
+            pltpu.SemaphoreType.DMA((4,)),
+            pltpu.SemaphoreType.DMA,
+            pltpu.SemaphoreType.DMA((2,)),
+        ],
+        compiler_params=pltpu.CompilerParams(vmem_limit_bytes=24 << 20),
+        cost_estimate=pl.CostEstimate(
+            flops=4_000_000_000, bytes_accessed=4 * width * width * 4, transcendentals=0
+        ),
+        name="final",
+    )(flags, *inputs, tiles, coupling)
 
 
 def local(weighted_jacobian_strips, leading_pose_index, levenberg_shift, removal_flags):
@@ -730,17 +829,11 @@
     grams = (passed_along(gram_one, 1), passed_along(gram_two, 2))
     partial = early(x, parts[:-1], starts[:-1], side)
     ready = before_last(flags, x, grams, [part[1] for part in known], parts[:-1], side)
-    schur, coupling = late(
-        flags,
-        x,
-        levenberg_shift,
-        (direct, onward, second, extra),
-        low,
-        parts[-1],
-        ready,
-        partial,
-        starts[-1],
-        side,
+    schur, coupling, near = late(
+        flags, x, levenberg_shift, second, low, parts[-1], ready, partial, starts[-1], side
+    )
+    schur, coupling = final(
+        flags, x, (direct, onward, extra), parts[-1][1], near, schur, coupling, side
     )
     return schur[None], coupling[None]
 

time: 252 us -> 246 us (0.976)
  the two profiles are of different devices: /device:TPU:0 before, /device:TPU:1 now
where the time goes in v6:
time: 246 us
  Pallas kernels  91.7 us (37%)
  waiting for transfers between devices  81.1 us (33%)
  starting transfers between devices  60.4 us (25%)
  local copies, waits for them, and re-layouts  11.6 us (5%)
    pallas_call x3, Pallas kernels, factored_part(): pl.pallas_call(functools.partial(part_kernel, side, bounds, number), out_...  50.6 us
    ppermute x16, starting transfers between devices, passed_along(): return lax.ppermute(value, AXES, pairs)  50.1 us
    all_to_all x1, waiting for transfers between devices, local(): lax.all_to_all(chunks, AXES, split_axis=0, concat_axis=0, tiled=True)  43.8 us
    ppermute x16, waiting for transfers between devices, passed_along(): return lax.ppermute(value, AXES, pairs)  37.3 us
    pallas_call x1, Pallas kernels, late(): pl.pallas_call(functools.partial(late_kernel, side, cut), out_shape=(jax....  12 us
    unnamed x48, local copies, waits for them, and re-layouts  11 us
    pallas_call x1, Pallas kernels, early(): pl.pallas_call(functools.partial(early_kernel, side, starts), out_shape=j...  9.91 us
    pallas_call x1, Pallas kernels, final(): pl.pallas_call(functools.partial(final_kernel, side), out_shape=(jax.Shap...  9.89 us
  transfers between devices with their start and end apart: 19, of which 6 were waited for; matrix products, arithmetic and copies ran while one was open for 0% of the time, Pallas kernels for 24%

profile of v6, /device:TPU:1, one launch (start us, length us, event | category | flops | bytes accessed | tf_op | source)
XLA Modules:
  0.0 245.9 jit_solution(4997149567577668988)
XLA Ops:
  0.6 4.1 %bucket.1 = f32[32,54,256]{2,1,0:T(8,128)} custom-call(s32[1,128]{1,0:T(1,128)} %bitcast.7, f32[3,128,768]{2,1,0:T(8,128)} %bitcast.6), custom_call_target="tpu_custom_call" | custom-call | tf_op jit(solution)/shard_map/bucket/pallas_call | solution.py:85
  4.8 7.1 %all-to-all-start = ((f32[32,54,256]{2,1,0:T(8,128)}), f32[32,54,256]{2,1,0:T(8,128)S(1)}, u32[]{:S(2)}, u32[]{:S(2)}) async-start(f32[32,54,256]{2,1,0:T(8,128)} %bucket.1), calls=%async_computation | async-start | bytes 3670016 | tf_op jit(solution)/shard_map/all_to_all | solution.py:804
  11.9 43.8 %all-to-all-done.in_ref = f32[32,54,256]{2,1,0:T(8,128)S(1)} async-done(((f32[32,54,256]{2,1,0:T(8,128)}), f32[32,54,256]{2,1,0:T(8,128)S(1)}, u32[]{:S(2)}, u32[]{:S(2)}) %all-to-all-start) | async-done | bytes 1769504 | tf_op jit(solution)/shard_map/all_to_all | solution.py:804
  56.1 0.8 copy-done.4
  56.9 18.1 %factor_part.3 = (f32[768,768]{1,0:T(8,128)S(1)}, f32[384,256]{1,0:T(8,128)}, f32[384,256]{1,0:T(8,128)S(1)}, f32[192,256]{1,0:T(8,128)S(1)}, f32[192,256]{1,0:T(8,128)S(1)}) custom-call(f32[576,768]{1,0:T(8,128)S(1)} %get-tuple-element.32.refs_0_.x_ref, f32[1,768]{1,0:T(1,128)S(1)} %copy-done.20), custom_call_target="tpu_custom_call" | custom-call | flops 20000000000 | bytes 5308416 | tf_op jit(solution)/shard_map/factor_part/pallas_call | solution.py:384
  75.1 1.9 collective-permute-start.13
  77.0 16.2 %factor_part.4 = (f32[768,768]{1,0:T(8,128)S(1)}, f32[384,256]{1,0:T(8,128)}, f32[384,256]{1,0:T(8,128)S(1)}, f32[192,256]{1,0:T(8,128)}, f32[192,256]{1,0:T(8,128)S(1)}) custom-call(f32[576,768]{1,0:T(8,128)S(1)} %get-tuple-element.32.refs_0_.x_ref, f32[768,768]{1,0:T(8,128)S(1)} %get-tuple-element.35.refs_1_, f32[384,256]{1,0:T(8,128)} %get-tuple-element.36.refs_2_, ...), custom_call_target="tpu_custom_call" | custom-call | flops 20000000000 | bytes 5308416 | tf_op jit(solution)/shard_map/factor_part/pallas_call | solution.py:384
  93.2 1.4 copy-done.21
  94.7 0.7 copy-done.18
  95.4 1.3 collective-permute-start.16
  97.9 2.2 collective-permute-done.17.refs_10_.refs_7_
  101.3 3.4 %collective-permute-done.16.refs_9_.refs_6_ = f32[192,256]{1,0:T(8,128)S(1)} collective-permute-done((f32[192,256]{1,0:T(8,128)}, f32[192,256]{1,0:T(8,128)S(1)}, u32[]{:S(2)}, u32[]{:S(2)}) %collective-permute-start.16) | collective-permute-done | bytes 196640 | tf_op jit(solution)/shard_map/ppermute | solution.py:29
  105.4 3.1 %collective-permute-start.15 = (f32[384,256]{1,0:T(8,128)S(1)}, f32[384,256]{1,0:T(8,128)S(1)}, u32[]{:S(2)}, u32[]{:S(2)}) collective-permute-start(f32[384,256]{1,0:T(8,128)S(1)} %get-tuple-element.49.refs_1_), channel_id=1, source_target_pairs={{0,31},{1,0},{2,1},{3,2},{4,3},{5,4},{6,5},{7,6},{8,7},{9,8},{10,9... | collective-permute-start | bytes 1179656 | tf_op jit(solution)/shard_map/ppermute | solution.py:29
  108.6 1.5 collective-permute-start.11
  110.8 1.5 copy-done.2
  112.3 0.9 copy-done.17
  113.2 0.9 copy-done.19
  114.2 1.7 copy-done.22
  115.8 16.3 %factor_part.5 = (f32[768,768]{1,0:T(8,128)S(1)}, f32[384,256]{1,0:T(8,128)S(1)}, f32[384,256]{1,0:T(8,128)S(1)}, f32[192,256]{1,0:T(8,128)S(1)}, f32[192,256]{1...) custom-call(f32[576,768]{1,0:T(8,128)S(1)} %copy-done.2, f32[768,768]{1,0:T(8,128)S(1)} %copy-done.22, ...), custom_call_target="tpu_custom_call" | custom-call | flops 20000000000 | bytes 5308416 | tf_op jit(solution)/shard_map/factor_part/pallas_call | solution.py:384
  132.1 1.9 collective-permute-start
  134.2 1.3 collective-permute-start.9
  135.5 7.9 %collective-permute-start.5 = (f32[384,256]{1,0:T(8,128)S(1)}, f32[384,256]{1,0:T(8,128)S(1)}, u32[]{:S(2)}, u32[]{:S(2)}) collective-permute-start(f32[384,256]{1,0:T(8,128)S(1)} %get-tuple-element.43), channel_id=1, source_target_pairs={{0,1},{1,2},{2,3},{3,4},{4,5},{5,6},{6,7},{7,8},{8,9},{9,10},{10,1... | collective-permute-start | bytes 1179656 | tf_op jit(solution)/shard_map/ppermute | solution.py:29
  143.4 9.9 %early.1.refs_12_ = f32[4,768,768]{2,1,0:T(8,128)} custom-call(f32[576,768]{1,0:T(8,128)S(1)} %copy-done.2, f32[384,256]{1,0:T(8,128)S(1)} %collective-permute-done.10.refs_3_.refs_0_, f32[384,256]{1,0:T(8,128)S(1)} %collective-permute-done.11.refs_4_.refs_1_, f32[192,256]{1,0:T(8,128)S(1)} %copy-done.15, ...), custom_call_target="tpu_custom_call" | custom-call | flops 8000000000 | bytes 9437184 | tf_op jit(solution)/shard_map/early/pallas_call | solution.py:458
  153.3 18.4 %collective-permute-done.9.gram_two_ref = f32[192,192]{1,0:T(8,128)S(1)} collective-permute-done((f32[192,192]{1,0:T(8,128)S(1)}, f32[192,192]{1,0:T(8,128)S(1)}, u32[]{:S(2)}, u32[]{:S(2)}) %collective-permute-start.9) | collective-permute-done | bytes 147488 | tf_op jit(solution)/shard_map/ppermute | solution.py:29
  172.5 19.6 %collective-permute-start.7 = (f32[192,256]{1,0:T(8,128)S(1)}, f32[192,256]{1,0:T(8,128)S(1)}, u32[]{:S(2)}, u32[]{:S(2)}) collective-permute-start(f32[192,256]{1,0:T(8,128)S(1)} %get-tuple-element.45), channel_id=1, source_target_pairs={{0,30},{1,31},{2,0},{3,1},{4,2},{5,3},{6,4},{7,5},{8,6},{9,7},{10,... | collective-permute-start | bytes 589832 | tf_op jit(solution)/shard_map/ppermute | solution.py:29
  192.0 1.3 collective-permute-start.2
  193.3 0.9 copy-done.9
  194.3 4.8 %before_last.1 = (f32[576,768]{1,0:T(8,128)S(1)}, f32[576,768]{1,0:T(8,128)S(1)}, f32[384,768]{1,0:T(8,128)S(1)}, bf16[768,576]{1,0:T(8,128)(2,1)S(1)}, bf16[768,576]{1,0:T(8,128)(2,1)S(1)}) custom-call(s32[5]{0:T(128)S(1)} %gather_fusion, f32[576,768]{1,0:T(8,128)S(1)} %copy-done.2, f32[192,384]{1,0:T(8,128)S(1)} %collective-permute-done.8.gram_one_ref, ...), custom_call_target="tpu_custom_call" | custom-call | flops 4000000000 | bytes 9437184 | tf_op jit(solution)/shard_map/before_last/pallas_call | solution.py:539
  199.0 12.3 %collective-permute-start.4 = (f32[384,256]{1,0:T(8,128)S(1)}, f32[384,256]{1,0:T(8,128)S(1)}, u32[]{:S(2)}, u32[]{:S(2)}) collective-permute-start(f32[384,256]{1,0:T(8,128)S(1)} %get-tuple-element.41.refs_2_), channel_id=1, source_target_pairs={{0,31},{1,0},{2,1},{3,2},{4,3},{5,4},{6,5},{7,6},{8,7},{9,8},{10,9... | collective-permute-start | bytes 1179656 | tf_op jit(solution)/shard_map/ppermute | solution.py:29
  211.4 12.0 %late.1 = (f32[3,768,768]{2,1,0:T(8,128)}, f32[4,768,768]{2,1,0:T(8,128)}, f32[576,768]{1,0:T(8,128)S(1)}) custom-call(s32[5]{0:T(128)S(1)} %gather_fusion, f32[576,768]{1,0:T(8,128)S(1)} %copy-done.3, f32[1,768]{1,0:T(1,128)S(1)} %copy-done.20, f32[384,768]{1,0:T(8,128)S(1)} %collective-permute-done.1.refs_2_, ...), custom_call_target="tpu_custom_call", output_to_operand_aliasing={{1}: (13, {})} | custom-call | flops 12000000000 | bytes 16515072 | tf_op jit(solution)/shard_map/late/pallas_call | solution.py:664
  223.4 12.4 %collective-permute-done.4.y_ref = f32[384,256]{1,0:T(8,128)S(1)} collective-permute-done((f32[384,256]{1,0:T(8,128)S(1)}, f32[384,256]{1,0:T(8,128)S(1)}, u32[]{:S(2)}, u32[]{:S(2)}) %collective-permute-start.4) | collective-permute-done | bytes 393248 | tf_op jit(solution)/shard_map/ppermute | solution.py:29
  235.8 9.9 %final.1 = (f32[3,768,768]{2,1,0:T(8,128)}, f32[4,768,768]{2,1,0:T(8,128)}) custom-call(s32[5]{0:T(128)S(1)} %gather_fusion, f32[576,768]{1,0:T(8,128)S(1)} %copy-done.3, f32[384,768]{1,0:T(8,128)S(1)} %collective-permute-done.direct_ref, f32[384,768]{1,0:T(8,128)S(1)} %collective-permute-done.2.onward_ref, ...), custom_call_target="tpu_custom_call", output_to_operand_aliasing={{0}: (7, {}), {1}: (8, {})} | custom-call | flops 4000000000 | bytes 9437184 | tf_op jit(solution)/shard_map/final/pallas_call | solution.py:760
  (66 shorter events, 5.1 us)
Async XLA Ops:
  0.6 96.2 %copy-start = (s32[32]{0:T(128)S(1)}, s32[32]{0:T(128)}, u32[]{:S(2)}) copy-start(s32[32]{0:T(128)} %param.8) | copy-start | bytes 388
  4.8 50.9 %all-to-all-start = ((f32[32,54,256]{2,1,0:T(8,128)}), f32[32,54,256]{2,1,0:T(8,128)S(1)}, u32[]{:S(2)}, u32[]{:S(2)}) async-start(f32[32,54,256]{2,1,0:T(8,128)} %bucket.1), calls=%async_computation | async-start | bytes 3670016 | tf_op jit(solution)/shard_map/all_to_all | solution.py:804
  11.9 45.1 %copy-start.20 = (f32[1,768]{1,0:T(1,128)S(1)}, f32[1,768]{1,0:T(1,128)}, u32[]{:S(2)}) copy-start(f32[1,768]{1,0:T(1,128)} %refs_1_.3) | copy-start | bytes 9220
  56.9 20.1 %copy-start.1 = (f32[576,768]{1,0:T(8,128)}, f32[576,768]{1,0:T(8,128)S(1)}, u32[]{:S(2)}) copy-start(f32[576,768]{1,0:T(8,128)S(1)} %get-tuple-element.32.refs_0_.x_ref) | copy-start | bytes 5308420
  75.1 18.1 %copy-start.16 = (f32[192,256]{1,0:T(8,128)}, f32[192,256]{1,0:T(8,128)S(1)}, u32[]{:S(2)}) copy-start(f32[192,256]{1,0:T(8,128)S(1)} %get-tuple-element.37.refs_3_) | copy-start | bytes 589828
  75.1 33.5 %collective-permute-start.13 = (f32[192,256]{1,0:T(8,128)S(1)}, f32[192,256]{1,0:T(8,128)S(1)}, u32[]{:S(2)}, u32[]{:S(2)}) collective-permute-start(f32[192,256]{1,0:T(8,128)S(1)} %get-tuple-element.37.refs_3_), channel_id=1, source_target_pairs={{0,30},{1,31},{2,0},{3,1},{4,2},{5,3},{6,4},{7,5},{8,6},{9,7},{10,... | collective-permute-start | bytes 589832 | tf_op jit(solution)/shard_map/ppermute | solution.py:29
  77.0 19.7 %copy-start.23 = (s32[5]{0:T(128)S(1)}, s32[5]{0:T(128)}, u32[]{:S(2)}) copy-start(s32[5]{0:T(128)} %constant.29.clone) | copy-start | bytes 64
  94.6 37.5 %copy-start.6 = (f32[384,256]{1,0:T(8,128)}, f32[384,256]{1,0:T(8,128)S(1)}, u32[]{:S(2)}) copy-start(f32[384,256]{1,0:T(8,128)S(1)} %get-tuple-element.49.refs_1_) | copy-start | bytes 1179652
  94.6 5.5 %collective-permute-start.17 = (f32[192,256]{1,0:T(8,128)S(1)}, f32[192,256]{1,0:T(8,128)S(1)}, u32[]{:S(2)}, u32[]{:S(2)}) collective-permute-start(f32[192,256]{1,0:T(8,128)S(1)} %get-tuple-element.40.refs_5_), channel_id=1, source_target_pairs={{0,30},{1,31},{2,0},{3,1},{4,2},{5,3},{6,4},{7,5},{8,6},{9,7},{10,... | collective-permute-start | bytes 589832 | tf_op jit(solution)/shard_map/ppermute | solution.py:29
  95.4 9.3 %collective-permute-start.16 = (f32[192,256]{1,0:T(8,128)}, f32[192,256]{1,0:T(8,128)S(1)}, u32[]{:S(2)}, u32[]{:S(2)}) collective-permute-start(f32[192,256]{1,0:T(8,128)} %get-tuple-element.51), channel_id=1, source_target_pairs={{0,2},{1,3},{2,4},{3,5},{4,6},{5,7},{6,8},{7,9},{8,10},{9,11},{10,... | collective-permute-start | bytes 589832 | tf_op jit(solution)/shard_map/ppermute | solution.py:29
  96.7 13.4 %collective-permute-start.12 = (f32[192,256]{1,0:T(8,128)S(1)}, f32[192,256]{1,0:T(8,128)S(1)}, u32[]{:S(2)}, u32[]{:S(2)}) collective-permute-start(f32[192,256]{1,0:T(8,128)S(1)} %get-tuple-element.50), channel_id=1, source_target_pairs={{0,2},{1,3},{2,4},{3,5},{4,6},{5,7},{6,8},{7,9},{8,10},{9,11},{10,... | collective-permute-start | bytes 589832 | tf_op jit(solution)/shard_map/ppermute | solution.py:29
  97.4 36.7 %collective-permute-start.10 = (f32[384,256]{1,0:T(8,128)}, f32[384,256]{1,0:T(8,128)S(1)}, u32[]{:S(2)}, u32[]{:S(2)}) collective-permute-start(f32[384,256]{1,0:T(8,128)} %get-tuple-element.36.refs_2_), channel_id=1, source_target_pairs={{0,1},{1,2},{2,3},{3,4},{4,5},{5,6},{6,7},{7,8},{8,9},{9,10},{10,1... | collective-permute-start | bytes 1179656 | tf_op jit(solution)/shard_map/ppermute | solution.py:29
  100.8 31.3 %collective-permute-start.14 = (f32[384,256]{1,0:T(8,128)}, f32[384,256]{1,0:T(8,128)S(1)}, u32[]{:S(2)}, u32[]{:S(2)}) collective-permute-start(f32[384,256]{1,0:T(8,128)} %get-tuple-element.39.refs_4_), channel_id=1, source_target_pairs={{0,1},{1,2},{2,3},{3,4},{4,5},{5,6},{6,7},{7,8},{8,9},{9,10},{10,1... | collective-permute-start | bytes 1179656 | tf_op jit(solution)/shard_map/ppermute | solution.py:29
  105.4 28.7 %collective-permute-start.15 = (f32[384,256]{1,0:T(8,128)S(1)}, f32[384,256]{1,0:T(8,128)S(1)}, u32[]{:S(2)}, u32[]{:S(2)}) collective-permute-start(f32[384,256]{1,0:T(8,128)S(1)} %get-tuple-element.49.refs_1_), channel_id=1, source_target_pairs={{0,31},{1,0},{2,1},{3,2},{4,3},{5,4},{6,5},{7,6},{8,7},{9,8},{10,9... | collective-permute-start | bytes 1179656 | tf_op jit(solution)/shard_map/ppermute | solution.py:29
  108.6 34.8 %copy-start.8 = (f32[192,256]{1,0:T(8,128)}, f32[192,256]{1,0:T(8,128)S(1)}, u32[]{:S(2)}) copy-start(f32[192,256]{1,0:T(8,128)S(1)} %collective-permute-done.13.refs_6_.refs_3_) | copy-start | bytes 589828
  108.6 26.9 %collective-permute-start.11 = (f32[384,256]{1,0:T(8,128)S(1)}, f32[384,256]{1,0:T(8,128)S(1)}, u32[]{:S(2)}, u32[]{:S(2)}) collective-permute-start(f32[384,256]{1,0:T(8,128)S(1)} %get-tuple-element.48.refs_0_), channel_id=1, source_target_pairs={{0,31},{1,0},{2,1},{3,2},{4,3},{5,4},{6,5},{7,6},{8,7},{9,8},{10,9... | collective-permute-start | bytes 1179656 | tf_op jit(solution)/shard_map/ppermute | solution.py:29
  110.8 81.2 %collective-permute-start.1 = (f32[384,768]{1,0:T(8,128)S(1)}, f32[384,768]{1,0:T(8,128)S(1)}, u32[]{:S(2)}, u32[]{:S(2)}) collective-permute-start(f32[384,768]{1,0:T(8,128)S(1)} %get-tuple-element.33), channel_id=1, source_target_pairs={{0,2},{1,3},{2,4},{3,5},{4,6},{5,7},{6,8},{7,9},{8,10},{9,11},{10,... | collective-permute-start | bytes 3538952 | tf_op jit(solution)/shard_map/ppermute | solution.py:29
  115.8 27.5 %copy-start.11 = (f32[192,256]{1,0:T(8,128)S(1)}, f32[192,256]{1,0:T(8,128)}, u32[]{:S(2)}) copy-start(f32[192,256]{1,0:T(8,128)} %copy-done.10) | copy-start | bytes 589828
  115.8 27.5 %copy-start.13 = (f32[192,256]{1,0:T(8,128)S(1)}, f32[192,256]{1,0:T(8,128)}, u32[]{:S(2)}) copy-start(f32[192,256]{1,0:T(8,128)} %copy-done.12) | copy-start | bytes 589828
  115.8 27.5 %copy-start.15 = (f32[192,256]{1,0:T(8,128)S(1)}, f32[192,256]{1,0:T(8,128)}, u32[]{:S(2)}) copy-start(f32[192,256]{1,0:T(8,128)} %copy-done.14) | copy-start | bytes 589828
  132.1 103.7 %collective-permute-start = (f32[384,768]{1,0:T(8,128)S(1)}, f32[384,768]{1,0:T(8,128)S(1)}, u32[]{:S(2)}, u32[]{:S(2)}) collective-permute-start(f32[384,768]{1,0:T(8,128)S(1)} %get-tuple-element.33), channel_id=1, source_target_pairs={{0,1},{2,3},{4,5},{6,7},{8,9},{10,11},{12,13},{14,15},{16,17},{18,... | collective-permute-start | bytes 3538952 | tf_op jit(solution)/shard_map/ppermute | solution.py:810
  134.1 38.4 %collective-permute-start.8 = (f32[192,384]{1,0:T(8,128)S(1)}, f32[192,384]{1,0:T(8,128)S(1)}, u32[]{:S(2)}, u32[]{:S(2)}) collective-permute-start(f32[192,384]{1,0:T(8,128)S(1)} %get-tuple-element.46), channel_id=1, source_target_pairs={{0,1},{1,2},{2,3},{3,4},{4,5},{5,6},{6,7},{7,8},{8,9},{9,10},{10,1... | collective-permute-start | bytes 884744 | tf_op jit(solution)/shard_map/ppermute | solution.py:29
  134.2 37.6 %collective-permute-start.9 = (f32[192,192]{1,0:T(8,128)S(1)}, f32[192,192]{1,0:T(8,128)S(1)}, u32[]{:S(2)}, u32[]{:S(2)}) collective-permute-start(f32[192,192]{1,0:T(8,128)S(1)} %get-tuple-element.47), channel_id=1, source_target_pairs={{0,2},{1,3},{2,4},{3,5},{4,6},{5,7},{6,8},{7,9},{8,10},{9,11},{10,... | collective-permute-start | bytes 442376 | tf_op jit(solution)/shard_map/ppermute | solution.py:29
  135.5 57.8 %copy-start.7 = (f32[384,256]{1,0:T(8,128)S(1)}, f32[384,256]{1,0:T(8,128)}, u32[]{:S(2)}) copy-start(f32[384,256]{1,0:T(8,128)} %copy-done.6) | copy-start | bytes 1179652
  135.5 75.8 %collective-permute-start.5 = (f32[384,256]{1,0:T(8,128)S(1)}, f32[384,256]{1,0:T(8,128)S(1)}, u32[]{:S(2)}, u32[]{:S(2)}) collective-permute-start(f32[384,256]{1,0:T(8,128)S(1)} %get-tuple-element.43), channel_id=1, source_target_pairs={{0,1},{1,2},{2,3},{3,4},{4,5},{5,6},{6,7},{7,8},{8,9},{9,10},{10,1... | collective-permute-start | bytes 1179656 | tf_op jit(solution)/shard_map/ppermute | solution.py:29
  171.7 27.3 %collective-permute-start.6 = (f32[192,256]{1,0:T(8,128)S(1)}, f32[192,256]{1,0:T(8,128)S(1)}, u32[]{:S(2)}, u32[]{:S(2)}) collective-permute-start(f32[192,256]{1,0:T(8,128)S(1)} %get-tuple-element.44), channel_id=1, source_target_pairs={{0,2},{1,3},{2,4},{3,5},{4,6},{5,7},{6,8},{7,9},{8,10},{9,11},{10,... | collective-permute-start | bytes 589832 | tf_op jit(solution)/shard_map/ppermute | solution.py:29
  172.5 38.9 %collective-permute-start.7 = (f32[192,256]{1,0:T(8,128)S(1)}, f32[192,256]{1,0:T(8,128)S(1)}, u32[]{:S(2)}, u32[]{:S(2)}) collective-permute-start(f32[192,256]{1,0:T(8,128)S(1)} %get-tuple-element.45), channel_id=1, source_target_pairs={{0,30},{1,31},{2,0},{3,1},{4,2},{5,3},{6,4},{7,5},{8,6},{9,7},{10,... | collective-permute-start | bytes 589832 | tf_op jit(solution)/shard_map/ppermute | solution.py:29
  192.0 43.8 %collective-permute-start.2 = (f32[384,768]{1,0:T(8,128)S(1)}, f32[384,768]{1,0:T(8,128)S(1)}, u32[]{:S(2)}, u32[]{:S(2)}) collective-permute-start(f32[384,768]{1,0:T(8,128)S(1)} %collective-permute-done.1.refs_2_), channel_id=1, source_target_pairs={{1,0},{3,2},{5,4},{7,6},{9,8},{11,10},{13,12},{15,14},{17,16},{19,... | collective-permute-start | bytes 3538952 | tf_op jit(solution)/shard_map/ppermute | solution.py:824
  194.2 17.1 %copy-start.5 = (f32[192,768]{1,0:T(8,128)S(1)}, f32[192,768]{1,0:T(8,128)}, u32[]{:S(2)}) copy-start(f32[192,768]{1,0:T(8,128)} %copy-done.4) | copy-start | bytes 1769476
  194.2 17.1 %copy-start.3 = (f32[576,768]{1,0:T(8,128)S(1)}, f32[576,768]{1,0:T(8,128)}, u32[]{:S(2)}) copy-start(f32[576,768]{1,0:T(8,128)} %copy-done.1) | copy-start | bytes 5308420
  199.0 36.8 %collective-permute-start.4 = (f32[384,256]{1,0:T(8,128)S(1)}, f32[384,256]{1,0:T(8,128)S(1)}, u32[]{:S(2)}, u32[]{:S(2)}) collective-permute-start(f32[384,256]{1,0:T(8,128)S(1)} %get-tuple-element.41.refs_2_), channel_id=1, source_target_pairs={{0,31},{1,0},{2,1},{3,2},{4,3},{5,4},{6,5},{7,6},{8,7},{9,8},{10,9... | collective-permute-start | bytes 1179656 | tf_op jit(solution)/shard_map/ppermute | solution.py:29
  211.3 24.5 %collective-permute-start.3 = (f32[192,768]{1,0:T(8,128)S(1)}, f32[192,768]{1,0:T(8,128)S(1)}, u32[]{:S(2)}, u32[]{:S(2)}) collective-permute-start(f32[192,768]{1,0:T(8,128)S(1)} %copy-done.5), channel_id=1, source_target_pairs={{0,1},{1,2},{2,3},{3,4},{4,5},{5,6},{6,7},{7,8},{8,9},{9,10},{10,1... | collective-permute-start | bytes 1769480 | tf_op jit(solution)/shard_map/ppermute | solution.py:29
  (11 other events, 10.9 us)

commit v7 on v6

--- a/solution.py
+++ b/solution.py
@@ -689,19 +689,64 @@
     )(flags, *inputs, partial)
 
 
-def final_kernel(side, flags_ref, x_ref, direct_ref, onward_ref, extra_ref, y_ref, given_ref, *refs):
+def beside_kernel(flags_ref, direct_ref, onward_ref, extra_ref, near_ref, tiles_ref, schur_ref, tile_ref, high_ref, less_ref, sem):
+    width = near_ref.shape[1]
+
+    @pl.when(flags_ref[3] <= 0)
+    def _():
+        below = direct_ref[...] + onward_ref[...]
+        left_refs = (high_ref, less_ref)
+        keep_halves(left_refs, jnp.concatenate([below, extra_ref[...]], axis=0).T)
+
+        def put(lanes, value):
+            tile_ref[:, lanes] = value
+
+        tall_product(
+            left_refs, width, near_ref.shape[0], lambda lanes: near_ref[:, lanes], put, width
+        )
+        copy = pltpu.make_async_copy(tile_ref, schur_ref.at[1], sem)
+        copy.start()
+        copy.wait()
+
+
+def beside(flags, received, near, tiles):
+    depth, width = near.shape
+    inputs = [*received, near]
+    return pl.pallas_call(
+        beside_kernel,
+        out_shape=jax.ShapeDtypeStruct((3, width, width), jnp.float32),
+        in_specs=[SMEM_SPEC] + [VMEM_SPEC] * len(inputs) + [ANY_SPEC],
+        out_specs=ANY_SPEC,
+        input_output_aliases={1 + len(inputs): 0},
+        scratch_shapes=[
+            pltpu.VMEM((width, width), jnp.float32),
+            pltpu.VMEM((width, depth), jnp.bfloat16),
+            pltpu.VMEM((width, depth), jnp.bfloat16),
+            pltpu.SemaphoreType.DMA,
+        ],
+        compiler_params=pltpu.CompilerParams(vmem_limit_bytes=16 << 20),
+        cost_estimate=pl.CostEstimate(
+            flops=3_000_000_000, bytes_accessed=2 * width * width * 4, transcendentals=0
+        ),
+        name="beside",
+    )(flags, *inputs, tiles)
+
+
+def final_kernel(side, flags_ref, x_ref, direct_ref, onward_ref, y_ref, *refs):
     tiles_ref, _, schur_ref, coupling_ref = refs[:4]
-    buffer_ref, tile_ref, near_ref, high_ref, less_ref, sems, ins, outs = refs[4:]
+    buffer_ref, tile_ref, small_ref, high_ref, less_ref, sems, ins, outs = refs[4:]
     left_refs = (high_ref, less_ref)
     rows, width = buffer_ref.shape[1:]
-    above, under = flags_ref[1] > 0, flags_ref[3] > 0
-    taken = pltpu.make_async_copy(tiles_ref.at[2], tile_ref.at[1], ins)
+    above = flags_ref[1] > 0
+    taken = pltpu.make_async_copy(tiles_ref.at[2], tile_ref.at[1], ins.at[1])
+    taken_beside = pltpu.make_async_copy(tiles_ref.at[1], tile_ref.at[0], ins.at[0])
     back = pltpu.make_async_copy(tile_ref.at[1], schur_ref.at[2], outs.at[1])
     beside = pltpu.make_async_copy(tile_ref.at[0], schur_ref.at[1], outs.at[0])
 
     @pl.when(above)
     def _():
         taken.start()
+        taken_beside.start()
 
     copies = put_coupling(
         side,
@@ -714,16 +759,15 @@
         sems,
         (1,),
     )
-    near_ref[...] = given_ref[...]
 
     @pl.when(above)
     def _():
         keep_halves(left_refs, y_ref[side:, :])
 
-        def put_near(lanes, value):
-            near_ref[:side, lanes] = near_ref[:side, lanes] - value
-
-        tall_product(left_refs, side, rows, lambda lanes: buffer_ref[0, :, lanes], put_near, width)
+        def put_small(lanes, value):
+            small_ref[:, lanes] = value
+
+        tall_product(left_refs, side, rows, lambda lanes: buffer_ref[0, :, lanes], put_small, width)
         keep_halves(left_refs, buffer_ref[0].T)
         taken.wait()
 
@@ -732,16 +776,13 @@
 
         tall_product(left_refs, width, rows, lambda lanes: buffer_ref[0, :, lanes], put_diag, width)
         back.start()
-
-    @pl.when(jnp.logical_not(under))
-    def _():
-        below = direct_ref[...] + onward_ref[...]
-        keep_halves(left_refs, jnp.concatenate([below, extra_ref[...]], axis=0).T)
+        keep_halves(left_refs, (direct_ref[:side, :] + onward_ref[:side, :]).T)
+        taken_beside.wait()
 
         def put_beside(lanes, value):
-            tile_ref[0, :, lanes] = value
-
-        tall_product(left_refs, width, 3 * side, lambda lanes: near_ref[:, lanes], put_beside, width)
+            tile_ref[0, :, lanes] = tile_ref[0, :, lanes] - value
+
+        tall_product(left_refs, width, side, lambda lanes: small_ref[:, lanes], put_beside, width)
         beside.start()
         beside.wait()
 
@@ -753,10 +794,10 @@
         copy.wait()
 
 
-def final(flags, x, received, y, near, tiles, coupling, side):
+def final(flags, x, received, y, tiles, coupling, side):
     depth, width = x.shape
     rows = y.shape[1]
-    inputs = [x, *received, y, near]
+    inputs = [x, *received, y]
     return pl.pallas_call(
         functools.partial(final_kernel, side),
         out_shape=(
@@ -769,11 +810,11 @@
         scratch_shapes=[
             pltpu.VMEM((1, rows, width), jnp.float32),
             pltpu.VMEM((2, width, width), jnp.float32),
-            pltpu.VMEM((depth, width), jnp.float32),
+            pltpu.VMEM((side, width), jnp.float32),
             pltpu.VMEM((width, depth), jnp.bfloat16),
             pltpu.VMEM((width, depth), jnp.bfloat16),
             pltpu.SemaphoreType.DMA((4,)),
-            pltpu.SemaphoreType.DMA,
+            pltpu.SemaphoreType.DMA((2,)),
             pltpu.SemaphoreType.DMA((2,)),
         ],
         compiler_params=pltpu.CompilerParams(vmem_limit_bytes=24 << 20),
@@ -832,9 +873,8 @@
     schur, coupling, near = late(
         flags, x, levenberg_shift, second, low, parts[-1], ready, partial, starts[-1], side
     )
-    schur, coupling = final(
-        flags, x, (direct, onward, extra), parts[-1][1], near, schur, coupling, side
-    )
+    schur = beside(flags, (direct, onward, extra), near, schur)
+    schur, coupling = final(flags, x, (direct, onward), parts[-1][1], schur, coupling, side)
     return schur[None], coupling[None]
 
 

time: 246 us -> 243 us (0.988)
  the two profiles are of different devices: /device:TPU:1 before, /device:TPU:0 now
where the time goes in v7:
time: 243 us; the launch traced here: 238 us
  Pallas kernels  89.3 us (37%)
  waiting for transfers between devices  82.6 us (34%)
  starting transfers between devices  53.6 us (22%)
  local copies, waits for them, and re-layouts  11.6 us (5%)
    pallas_call x3, Pallas kernels, factored_part(): pl.pallas_call(functools.partial(part_kernel, side, bounds, number), out_...  50.6 us
    all_to_all x1, waiting for transfers between devices, local(): lax.all_to_all(chunks, AXES, split_axis=0, concat_axis=0, tiled=True)  44.3 us
    ppermute x16, starting transfers between devices, passed_along(): return lax.ppermute(value, AXES, pairs)  41 us
    ppermute x16, waiting for transfers between devices, passed_along(): return lax.ppermute(value, AXES, pairs)  25.2 us
    pallas_call x1, Pallas kernels, late(): pl.pallas_call(functools.partial(late_kernel, side, cut), out_shape=(jax....  15.8 us
    ppermute x1, waiting for transfers between devices, local(): lax.ppermute(second, AXES, [(k + 1, k) for k in range(0, count, 2)])  13.1 us
    unnamed x48, local copies, waits for them, and re-layouts  11 us
    pallas_call x1, Pallas kernels, early(): pl.pallas_call(functools.partial(early_kernel, side, starts), out_shape=j...  9.93 us
  transfers between devices with their start and end apart: 19, of which 6 were waited for; matrix products, arithmetic and copies ran while one was open for 0% of the time, Pallas kernels for 27%

profile of v7, /device:TPU:0, one launch (start us, length us, event | category | flops | bytes accessed | tf_op | source)
XLA Modules:
  0.0 238.2 jit_solution(13429722454410864915)
XLA Ops:
  0.6 4.1 %bucket.1 = f32[32,54,256]{2,1,0:T(8,128)} custom-call(s32[1,128]{1,0:T(1,128)} %bitcast.7, f32[3,128,768]{2,1,0:T(8,128)} %bitcast.6), custom_call_target="tpu_custom_call" | custom-call | tf_op jit(solution)/shard_map/bucket/pallas_call | solution.py:85
  4.8 7.3 %all-to-all-start = ((f32[32,54,256]{2,1,0:T(8,128)}), f32[32,54,256]{2,1,0:T(8,128)S(1)}, u32[]{:S(2)}, u32[]{:S(2)}) async-start(f32[32,54,256]{2,1,0:T(8,128)} %bucket.1), calls=%async_computation | async-start | bytes 3670016 | tf_op jit(solution)/shard_map/all_to_all | solution.py:845
  12.1 44.3 %all-to-all-done.in_ref = f32[32,54,256]{2,1,0:T(8,128)S(1)} async-done(((f32[32,54,256]{2,1,0:T(8,128)}), f32[32,54,256]{2,1,0:T(8,128)S(1)}, u32[]{:S(2)}, u32[]{:S(2)}) %all-to-all-start) | async-done | bytes 1769504 | tf_op jit(solution)/shard_map/all_to_all | solution.py:845
  56.9 0.8 copy-done.4
  57.7 18.1 %factor_part.3 = (f32[768,768]{1,0:T(8,128)S(1)}, f32[384,256]{1,0:T(8,128)}, f32[384,256]{1,0:T(8,128)S(1)}, f32[192,256]{1,0:T(8,128)S(1)}, f32[192,256]{1,0:T(8,128)S(1)}) custom-call(f32[576,768]{1,0:T(8,128)S(1)} %get-tuple-element.32.refs_0_.x_ref, f32[1,768]{1,0:T(1,128)S(1)} %copy-done.20), custom_call_target="tpu_custom_call" | custom-call | flops 20000000000 | bytes 5308416 | tf_op jit(solution)/shard_map/factor_part/pallas_call | solution.py:384
  75.8 2.1 collective-permute-start.13
  77.9 16.2 %factor_part.4 = (f32[768,768]{1,0:T(8,128)S(1)}, f32[384,256]{1,0:T(8,128)}, f32[384,256]{1,0:T(8,128)S(1)}, f32[192,256]{1,0:T(8,128)}, f32[192,256]{1,0:T(8,128)S(1)}) custom-call(f32[576,768]{1,0:T(8,128)S(1)} %get-tuple-element.32.refs_0_.x_ref, f32[768,768]{1,0:T(8,128)S(1)} %get-tuple-element.34.refs_1_, f32[384,256]{1,0:T(8,128)} %get-tuple-element.35.refs_2_, ...), custom_call_target="tpu_custom_call" | custom-call | flops 20000000000 | bytes 5308416 | tf_op jit(solution)/shard_map/factor_part/pallas_call | solution.py:384
  94.1 1.4 copy-done.21
  95.6 0.8 copy-done.18
  96.3 1.9 collective-permute-start.16
  99.3 11.6 %collective-permute-done.17.refs_10_.refs_7_ = f32[192,256]{1,0:T(8,128)S(1)} collective-permute-done((f32[192,256]{1,0:T(8,128)S(1)}, f32[192,256]{1,0:T(8,128)S(1)}, u32[]{:S(2)}, u32[]{:S(2)}) %collective-permute-start.17) | collective-permute-done | bytes 196640 | tf_op jit(solution)/shard_map/ppermute | solution.py:29
  112.5 5.2 %collective-permute-start.15 = (f32[384,256]{1,0:T(8,128)S(1)}, f32[384,256]{1,0:T(8,128)S(1)}, u32[]{:S(2)}, u32[]{:S(2)}) collective-permute-start(f32[384,256]{1,0:T(8,128)S(1)} %get-tuple-element.49.refs_1_), channel_id=1, source_target_pairs={{0,31},{1,0},{2,1},{3,2},{4,3},{5,4},{6,5},{7,6},{8,7},{9,8},{10,9... | collective-permute-start | bytes 1179656 | tf_op jit(solution)/shard_map/ppermute | solution.py:29
  118.4 24.5 %collective-permute-start.1 = (f32[384,768]{1,0:T(8,128)S(1)}, f32[384,768]{1,0:T(8,128)S(1)}, u32[]{:S(2)}, u32[]{:S(2)}) collective-permute-start(f32[384,768]{1,0:T(8,128)S(1)} %get-tuple-element.33), channel_id=1, source_target_pairs={{0,2},{1,3},{2,4},{3,5},{4,6},{5,7},{6,8},{7,9},{8,10},{9,11},{10,... | collective-permute-start | bytes 3538952 | tf_op jit(solution)/shard_map/ppermute | solution.py:29
  143.0 1.5 copy-done.2
  144.4 0.9 copy-done.17
  145.4 0.9 copy-done.19
  146.3 1.7 copy-done.22
  148.0 16.3 %factor_part.5 = (f32[768,768]{1,0:T(8,128)S(1)}, f32[384,256]{1,0:T(8,128)S(1)}, f32[384,256]{1,0:T(8,128)S(1)}, f32[192,256]{1,0:T(8,128)S(1)}, f32[192,256]{1...) custom-call(f32[576,768]{1,0:T(8,128)S(1)} %copy-done.2, f32[768,768]{1,0:T(8,128)S(1)} %copy-done.22, ...), custom_call_target="tpu_custom_call" | custom-call | flops 20000000000 | bytes 5308416 | tf_op jit(solution)/shard_map/factor_part/pallas_call | solution.py:384
  164.3 4.0 %collective-permute-start = (f32[384,768]{1,0:T(8,128)S(1)}, f32[384,768]{1,0:T(8,128)S(1)}, u32[]{:S(2)}, u32[]{:S(2)}) collective-permute-start(f32[384,768]{1,0:T(8,128)S(1)} %get-tuple-element.33), channel_id=1, source_target_pairs={{0,1},{2,3},{4,5},{6,7},{8,9},{10,11},{12,13},{14,15},{16,17},{18,... | collective-permute-start | bytes 3538952 | tf_op jit(solution)/shard_map/ppermute | solution.py:851
  168.4 1.4 collective-permute-start.9
  169.8 1.5 collective-permute-start.5
  171.3 9.9 %early.1.refs_12_ = f32[4,768,768]{2,1,0:T(8,128)} custom-call(f32[576,768]{1,0:T(8,128)S(1)} %copy-done.2, f32[384,256]{1,0:T(8,128)S(1)} %collective-permute-done.10.refs_3_.refs_0_, f32[384,256]{1,0:T(8,128)S(1)} %collective-permute-done.11.refs_4_.refs_1_, f32[192,256]{1,0:T(8,128)S(1)} %copy-done.15, ...), custom_call_target="tpu_custom_call" | custom-call | flops 8000000000 | bytes 9437184 | tf_op jit(solution)/shard_map/early/pallas_call | solution.py:458
  181.3 3.8 %collective-permute-done.8.gram_one_ref = f32[192,384]{1,0:T(8,128)S(1)} collective-permute-done((f32[192,384]{1,0:T(8,128)S(1)}, f32[192,384]{1,0:T(8,128)S(1)}, u32[]{:S(2)}, u32[]{:S(2)}) %collective-permute-start.8) | collective-permute-done | bytes 294944 | tf_op jit(solution)/shard_map/ppermute | solution.py:29
  185.8 1.3 collective-permute-start.2
  187.1 0.9 copy-done.9
  188.0 5.0 %before_last.1 = (f32[576,768]{1,0:T(8,128)S(1)}, f32[576,768]{1,0:T(8,128)S(1)}, f32[384,768]{1,0:T(8,128)S(1)}, bf16[768,576]{1,0:T(8,128)(2,1)S(1)}, bf16[768,576]{1,0:T(8,128)(2,1)S(1)}) custom-call(s32[5]{0:T(128)S(1)} %gather_fusion, f32[576,768]{1,0:T(8,128)S(1)} %copy-done.2, f32[192,384]{1,0:T(8,128)S(1)} %collective-permute-done.8.gram_one_ref, ...), custom_call_target="tpu_custom_call" | custom-call | flops 4000000000 | bytes 9437184 | tf_op jit(solution)/shard_map/before_last/pallas_call | solution.py:539
  193.1 2.0 collective-permute-done.7.refs_6_
  195.1 2.8 %collective-permute-start.4 = (f32[192,768]{1,0:T(8,128)S(1)}, f32[192,768]{1,0:T(8,128)S(1)}, u32[]{:S(2)}, u32[]{:S(2)}) collective-permute-start(f32[192,768]{1,0:T(8,128)S(1)} %copy-done.5), channel_id=1, source_target_pairs={{0,1},{1,2},{2,3},{3,4},{4,5},{5,6},{6,7},{7,8},{8,9},{9,10},{10,1... | collective-permute-start | bytes 1769480 | tf_op jit(solution)/shard_map/ppermute | solution.py:29
  198.0 15.8 %late.1 = (f32[3,768,768]{2,1,0:T(8,128)}, f32[4,768,768]{2,1,0:T(8,128)}, f32[576,768]{1,0:T(8,128)S(1)}) custom-call(s32[5]{0:T(128)S(1)} %gather_fusion, f32[576,768]{1,0:T(8,128)S(1)} %copy-done.3, f32[1,768]{1,0:T(1,128)S(1)} %copy-done.20, f32[384,768]{1,0:T(8,128)S(1)} %collective-permute-done.1.refs_2_, ...), custom_call_target="tpu_custom_call", output_to_operand_aliasing={{1}: (13, {})} | custom-call | flops 12000000000 | bytes 16515072 | tf_op jit(solution)/shard_map/late/pallas_call | solution.py:664
  213.8 13.1 %collective-permute-done.2.onward_ref = f32[384,768]{1,0:T(8,128)S(1)} collective-permute-done((f32[384,768]{1,0:T(8,128)S(1)}, f32[384,768]{1,0:T(8,128)S(1)}, u32[]{:S(2)}, u32[]{:S(2)}) %collective-permute-start.2) | collective-permute-done | bytes 1179680 | tf_op jit(solution)/shard_map/ppermute | solution.py:865
  227.5 7.8 %collective-permute-done.3.y_ref = f32[384,256]{1,0:T(8,128)S(1)} collective-permute-done((f32[384,256]{1,0:T(8,128)S(1)}, f32[384,256]{1,0:T(8,128)S(1)}, u32[]{:S(2)}, u32[]{:S(2)}) %collective-permute-start.3) | collective-permute-done | bytes 393248 | tf_op jit(solution)/shard_map/ppermute | solution.py:29
  235.3 2.8 %final.1 = (f32[3,768,768]{2,1,0:T(8,128)}, f32[4,768,768]{2,1,0:T(8,128)}) custom-call(s32[5]{0:T(128)S(1)} %gather_fusion, f32[576,768]{1,0:T(8,128)S(1)} %copy-done.3, f32[384,768]{1,0:T(8,128)S(1)} %collective-permute-done.direct_ref, f32[384,768]{1,0:T(8,128)S(1)} %collective-permute-done.2.onward_ref, ...), custom_call_target="tpu_custom_call", output_to_operand_aliasing={{0}: (5, {}), {1}: (6, {})} | custom-call | flops 4000000000 | bytes 9437184 | tf_op jit(solution)/shard_map/final/pallas_call | solution.py:801
  (67 shorter events, 5.4 us)
Async XLA Ops:
  0.6 97.6 %copy-start = (s32[32]{0:T(128)S(1)}, s32[32]{0:T(128)}, u32[]{:S(2)}) copy-start(s32[32]{0:T(128)} %param.8) | copy-start | bytes 388
  4.8 51.7 %all-to-all-start = ((f32[32,54,256]{2,1,0:T(8,128)}), f32[32,54,256]{2,1,0:T(8,128)S(1)}, u32[]{:S(2)}, u32[]{:S(2)}) async-start(f32[32,54,256]{2,1,0:T(8,128)} %bucket.1), calls=%async_computation | async-start | bytes 3670016 | tf_op jit(solution)/shard_map/all_to_all | solution.py:845
  12.1 45.6 %copy-start.20 = (f32[1,768]{1,0:T(1,128)S(1)}, f32[1,768]{1,0:T(1,128)}, u32[]{:S(2)}) copy-start(f32[1,768]{1,0:T(1,128)} %refs_1_.3) | copy-start | bytes 9220
  57.7 20.2 %copy-start.1 = (f32[576,768]{1,0:T(8,128)}, f32[576,768]{1,0:T(8,128)S(1)}, u32[]{:S(2)}) copy-start(f32[576,768]{1,0:T(8,128)S(1)} %get-tuple-element.32.refs_0_.x_ref) | copy-start | bytes 5308420
  75.8 18.3 %copy-start.16 = (f32[192,256]{1,0:T(8,128)}, f32[192,256]{1,0:T(8,128)S(1)}, u32[]{:S(2)}) copy-start(f32[192,256]{1,0:T(8,128)S(1)} %get-tuple-element.36.refs_3_) | copy-start | bytes 589828
  75.8 41.9 %collective-permute-start.13 = (f32[192,256]{1,0:T(8,128)S(1)}, f32[192,256]{1,0:T(8,128)S(1)}, u32[]{:S(2)}, u32[]{:S(2)}) collective-permute-start(f32[192,256]{1,0:T(8,128)S(1)} %get-tuple-element.36.refs_3_), channel_id=1, source_target_pairs={{0,30},{1,31},{2,0},{3,1},{4,2},{5,3},{6,4},{7,5},{8,6},{9,7},{10,... | collective-permute-start | bytes 589832 | tf_op jit(solution)/shard_map/ppermute | solution.py:29
  77.9 20.3 %copy-start.23 = (s32[5]{0:T(128)S(1)}, s32[5]{0:T(128)}, u32[]{:S(2)}) copy-start(s32[5]{0:T(128)} %constant.29.clone) | copy-start | bytes 64
  95.5 68.8 %copy-start.6 = (f32[384,256]{1,0:T(8,128)}, f32[384,256]{1,0:T(8,128)S(1)}, u32[]{:S(2)}) copy-start(f32[384,256]{1,0:T(8,128)S(1)} %get-tuple-element.49.refs_1_) | copy-start | bytes 1179652
  95.5 15.5 %collective-permute-start.17 = (f32[192,256]{1,0:T(8,128)S(1)}, f32[192,256]{1,0:T(8,128)S(1)}, u32[]{:S(2)}, u32[]{:S(2)}) collective-permute-start(f32[192,256]{1,0:T(8,128)S(1)} %get-tuple-element.39.refs_5_), channel_id=1, source_target_pairs={{0,30},{1,31},{2,0},{3,1},{4,2},{5,3},{6,4},{7,5},{8,6},{9,7},{10,... | collective-permute-start | bytes 589832 | tf_op jit(solution)/shard_map/ppermute | solution.py:29
  96.3 15.5 %collective-permute-start.16 = (f32[192,256]{1,0:T(8,128)}, f32[192,256]{1,0:T(8,128)S(1)}, u32[]{:S(2)}, u32[]{:S(2)}) collective-permute-start(f32[192,256]{1,0:T(8,128)} %get-tuple-element.51), channel_id=1, source_target_pairs={{0,2},{1,3},{2,4},{3,5},{4,6},{5,7},{6,8},{7,9},{8,10},{9,11},{10,... | collective-permute-start | bytes 589832 | tf_op jit(solution)/shard_map/ppermute | solution.py:29
  98.2 19.5 %collective-permute-start.12 = (f32[192,256]{1,0:T(8,128)S(1)}, f32[192,256]{1,0:T(8,128)S(1)}, u32[]{:S(2)}, u32[]{:S(2)}) collective-permute-start(f32[192,256]{1,0:T(8,128)S(1)} %get-tuple-element.50), channel_id=1, source_target_pairs={{0,2},{1,3},{2,4},{3,5},{4,6},{5,7},{6,8},{7,9},{8,10},{9,11},{10,... | collective-permute-start | bytes 589832 | tf_op jit(solution)/shard_map/ppermute | solution.py:29
  98.9 69.5 %collective-permute-start.10 = (f32[384,256]{1,0:T(8,128)}, f32[384,256]{1,0:T(8,128)S(1)}, u32[]{:S(2)}, u32[]{:S(2)}) collective-permute-start(f32[384,256]{1,0:T(8,128)} %get-tuple-element.35.refs_2_), channel_id=1, source_target_pairs={{0,1},{1,2},{2,3},{3,4},{4,5},{5,6},{6,7},{7,8},{8,9},{9,10},{10,1... | collective-permute-start | bytes 1179656 | tf_op jit(solution)/shard_map/ppermute | solution.py:29
  111.6 52.6 %collective-permute-start.14 = (f32[384,256]{1,0:T(8,128)}, f32[384,256]{1,0:T(8,128)S(1)}, u32[]{:S(2)}, u32[]{:S(2)}) collective-permute-start(f32[384,256]{1,0:T(8,128)} %get-tuple-element.38.refs_4_), channel_id=1, source_target_pairs={{0,1},{1,2},{2,3},{3,4},{4,5},{5,6},{6,7},{7,8},{8,9},{9,10},{10,1... | collective-permute-start | bytes 1179656 | tf_op jit(solution)/shard_map/ppermute | solution.py:29
  112.5 55.8 %collective-permute-start.15 = (f32[384,256]{1,0:T(8,128)S(1)}, f32[384,256]{1,0:T(8,128)S(1)}, u32[]{:S(2)}, u32[]{:S(2)}) collective-permute-start(f32[384,256]{1,0:T(8,128)S(1)} %get-tuple-element.49.refs_1_), channel_id=1, source_target_pairs={{0,31},{1,0},{2,1},{3,2},{4,3},{5,4},{6,5},{7,6},{8,7},{9,8},{10,9... | collective-permute-start | bytes 1179656 | tf_op jit(solution)/shard_map/ppermute | solution.py:29
  117.7 53.6 %copy-start.8 = (f32[192,256]{1,0:T(8,128)}, f32[192,256]{1,0:T(8,128)S(1)}, u32[]{:S(2)}) copy-start(f32[192,256]{1,0:T(8,128)S(1)} %collective-permute-done.13.refs_6_.refs_3_) | copy-start | bytes 589828
  117.7 52.2 %collective-permute-start.11 = (f32[384,256]{1,0:T(8,128)S(1)}, f32[384,256]{1,0:T(8,128)S(1)}, u32[]{:S(2)}, u32[]{:S(2)}) collective-permute-start(f32[384,256]{1,0:T(8,128)S(1)} %get-tuple-element.48.refs_0_), channel_id=1, source_target_pairs={{0,31},{1,0},{2,1},{3,2},{4,3},{5,4},{6,5},{7,6},{8,7},{9,8},{10,9... | collective-permute-start | bytes 1179656 | tf_op jit(solution)/shard_map/ppermute | solution.py:29
  118.4 67.3 %collective-permute-start.1 = (f32[384,768]{1,0:T(8,128)S(1)}, f32[384,768]{1,0:T(8,128)S(1)}, u32[]{:S(2)}, u32[]{:S(2)}) collective-permute-start(f32[384,768]{1,0:T(8,128)S(1)} %get-tuple-element.33), channel_id=1, source_target_pairs={{0,2},{1,3},{2,4},{3,5},{4,6},{5,7},{6,8},{7,9},{8,10},{9,11},{10,... | collective-permute-start | bytes 3538952 | tf_op jit(solution)/shard_map/ppermute | solution.py:29
  148.0 23.3 %copy-start.11 = (f32[192,256]{1,0:T(8,128)S(1)}, f32[192,256]{1,0:T(8,128)}, u32[]{:S(2)}) copy-start(f32[192,256]{1,0:T(8,128)} %copy-done.10) | copy-start | bytes 589828
  148.0 23.3 %copy-start.13 = (f32[192,256]{1,0:T(8,128)S(1)}, f32[192,256]{1,0:T(8,128)}, u32[]{:S(2)}) copy-start(f32[192,256]{1,0:T(8,128)} %copy-done.12) | copy-start | bytes 589828
  148.0 23.3 %copy-start.15 = (f32[192,256]{1,0:T(8,128)S(1)}, f32[192,256]{1,0:T(8,128)}, u32[]{:S(2)}) copy-start(f32[192,256]{1,0:T(8,128)} %copy-done.14) | copy-start | bytes 589828
  164.3 49.5 %collective-permute-start = (f32[384,768]{1,0:T(8,128)S(1)}, f32[384,768]{1,0:T(8,128)S(1)}, u32[]{:S(2)}, u32[]{:S(2)}) collective-permute-start(f32[384,768]{1,0:T(8,128)S(1)} %get-tuple-element.33), channel_id=1, source_target_pairs={{0,1},{2,3},{4,5},{6,7},{8,9},{10,11},{12,13},{14,15},{16,17},{18,... | collective-permute-start | bytes 3538952 | tf_op jit(solution)/shard_map/ppermute | solution.py:851
  168.3 16.8 %collective-permute-start.8 = (f32[192,384]{1,0:T(8,128)S(1)}, f32[192,384]{1,0:T(8,128)S(1)}, u32[]{:S(2)}, u32[]{:S(2)}) collective-permute-start(f32[192,384]{1,0:T(8,128)S(1)} %get-tuple-element.46), channel_id=1, source_target_pairs={{0,1},{1,2},{2,3},{3,4},{4,5},{5,6},{6,7},{7,8},{8,9},{9,10},{10,1... | collective-permute-start | bytes 884744 | tf_op jit(solution)/shard_map/ppermute | solution.py:29
  168.4 12.9 %collective-permute-start.9 = (f32[192,192]{1,0:T(8,128)S(1)}, f32[192,192]{1,0:T(8,128)S(1)}, u32[]{:S(2)}, u32[]{:S(2)}) collective-permute-start(f32[192,192]{1,0:T(8,128)S(1)} %get-tuple-element.47), channel_id=1, source_target_pairs={{0,2},{1,3},{2,4},{3,5},{4,6},{5,7},{6,8},{7,9},{8,10},{9,11},{10,... | collective-permute-start | bytes 442376 | tf_op jit(solution)/shard_map/ppermute | solution.py:29
  169.8 17.2 %copy-start.7 = (f32[384,256]{1,0:T(8,128)S(1)}, f32[384,256]{1,0:T(8,128)}, u32[]{:S(2)}) copy-start(f32[384,256]{1,0:T(8,128)} %copy-done.6) | copy-start | bytes 1179652
  169.8 28.1 %collective-permute-start.5 = (f32[384,256]{1,0:T(8,128)S(1)}, f32[384,256]{1,0:T(8,128)S(1)}, u32[]{:S(2)}, u32[]{:S(2)}) collective-permute-start(f32[384,256]{1,0:T(8,128)S(1)} %get-tuple-element.43), channel_id=1, source_target_pairs={{0,1},{1,2},{2,3},{3,4},{4,5},{5,6},{6,7},{7,8},{8,9},{9,10},{10,1... | collective-permute-start | bytes 1179656 | tf_op jit(solution)/shard_map/ppermute | solution.py:29
  181.3 11.8 %collective-permute-start.6 = (f32[192,256]{1,0:T(8,128)S(1)}, f32[192,256]{1,0:T(8,128)S(1)}, u32[]{:S(2)}, u32[]{:S(2)}) collective-permute-start(f32[192,256]{1,0:T(8,128)S(1)} %get-tuple-element.44), channel_id=1, source_target_pairs={{0,2},{1,3},{2,4},{3,5},{4,6},{5,7},{6,8},{7,9},{8,10},{9,11},{10,... | collective-permute-start | bytes 589832 | tf_op jit(solution)/shard_map/ppermute | solution.py:29
  185.1 10.0 %collective-permute-start.7 = (f32[192,256]{1,0:T(8,128)S(1)}, f32[192,256]{1,0:T(8,128)S(1)}, u32[]{:S(2)}, u32[]{:S(2)}) collective-permute-start(f32[192,256]{1,0:T(8,128)S(1)} %get-tuple-element.45), channel_id=1, source_target_pairs={{0,30},{1,31},{2,0},{3,1},{4,2},{5,3},{6,4},{7,5},{8,6},{9,7},{10,... | collective-permute-start | bytes 589832 | tf_op jit(solution)/shard_map/ppermute | solution.py:29
  185.8 41.2 %collective-permute-start.2 = (f32[384,768]{1,0:T(8,128)S(1)}, f32[384,768]{1,0:T(8,128)S(1)}, u32[]{:S(2)}, u32[]{:S(2)}) collective-permute-start(f32[384,768]{1,0:T(8,128)S(1)} %collective-permute-done.1.refs_2_), channel_id=1, source_target_pairs={{1,0},{3,2},{5,4},{7,6},{9,8},{11,10},{13,12},{15,14},{17,16},{19,... | collective-permute-start | bytes 3538952 | tf_op jit(solution)/shard_map/ppermute | solution.py:865
  188.0 7.1 %copy-start.5 = (f32[192,768]{1,0:T(8,128)S(1)}, f32[192,768]{1,0:T(8,128)}, u32[]{:S(2)}) copy-start(f32[192,768]{1,0:T(8,128)} %copy-done.4) | copy-start | bytes 1769476
  188.0 10.0 %copy-start.3 = (f32[576,768]{1,0:T(8,128)S(1)}, f32[576,768]{1,0:T(8,128)}, u32[]{:S(2)}) copy-start(f32[576,768]{1,0:T(8,128)} %copy-done.1) | copy-start | bytes 5308420
  193.0 42.2 %collective-permute-start.3 = (f32[384,256]{1,0:T(8,128)S(1)}, f32[384,256]{1,0:T(8,128)S(1)}, u32[]{:S(2)}, u32[]{:S(2)}) collective-permute-start(f32[384,256]{1,0:T(8,128)S(1)} %get-tuple-element.40.refs_2_), channel_id=1, source_target_pairs={{0,31},{1,0},{2,1},{3,2},{4,3},{5,4},{6,5},{7,6},{8,7},{9,8},{10,9... | collective-permute-start | bytes 1179656 | tf_op jit(solution)/shard_map/ppermute | solution.py:29
  195.1 18.7 %collective-permute-start.4 = (f32[192,768]{1,0:T(8,128)S(1)}, f32[192,768]{1,0:T(8,128)S(1)}, u32[]{:S(2)}, u32[]{:S(2)}) collective-permute-start(f32[192,768]{1,0:T(8,128)S(1)} %copy-done.5), channel_id=1, source_target_pairs={{0,1},{1,2},{2,3},{3,4},{4,5},{5,6},{6,7},{7,8},{8,9},{9,10},{10,1... | collective-permute-start | bytes 1769480 | tf_op jit(solution)/shard_map/ppermute | solution.py:29
  (11 other events, 11.0 us)
